TPU v7x, 32 devices: a whole 2x2x4 slice. The times are simulated.
32 devices in a mesh: mode: 4 (over z), ra: 2 (over y), rb: 4 (over x, core).
Axes of the slice: x: 2, y: 2, z: 4, core: 2. Of those that a mesh axis runs over, the one named last changes fastest.
Arguments:
- density_slab: float32 [1024, 32, 512], P('mode', 'ra', 'rb'), may hold values from -111 to 111
- start_basis: float32 [1024, 256], replicated, may hold values from -4 to 4
Outputs:
- projected_slab: float32 [256, 32, 512], P('mode', 'ra', 'rb')
All inputs are finite; a program needn't handle non-finite values.
Results may differ from a plain program's by a relative error of at most 0.0002.
Values sent between devices are 32-bit elements; how exact they have to be, the bound alone decides.
No kernel may reach another device: no remote copies, remote signals or barrier semaphores. Data moves between devices by JAX's collectives and lax.ppermute only.
A program may use at most 64 MiB of HBM per device.

v0:
```python
import functools

import jax
import jax.numpy as jnp
from jax import lax
from jax.experimental import pallas as pl
from jax.experimental.pallas import tpu as pltpu
from jax.sharding import PartitionSpec as P


SUB, LANES = 8, 128
HALF = LANES // 2
VMEM_BYTES = 20 * 2**20
LIFT = 2.0**20


def mm(a, b, a_dim, b_dim):
    return lax.dot_general(
        a,
        b,
        (((a_dim,), (b_dim,)), ((), ())),
        precision=lax.Precision.HIGHEST,
        preferred_element_type=jnp.float32,
    )


def eliminate(groups, ones):
    sub = lax.broadcasted_iota(jnp.int32, (SUB, LANES), 0)
    done = []
    for p in range(len(groups)):
        first = p * SUB
        rows = [jnp.broadcast_to(groups[p][j : j + 1, :], (SUB, LANES)) for j in range(SUB)]
        across = [
            jnp.broadcast_to(groups[p][:, first + j : first + j + 1], (SUB, LANES)) * ones for j in range(SUB)
        ]
        block = [
            [jnp.broadcast_to(across[j][i : i + 1, :], (SUB, LANES)) if j >= i else None for j in range(SUB)]
            for i in range(SUB)
        ]
        lower = [[None] * SUB for _ in range(SUB)]
        inverse = []
        for i in range(SUB):
            inverse.append(1.0 / block[i][i])
            for j in range(i + 1, SUB):
                lower[j][i] = block[i][j] * inverse[i]
            for j in range(i + 1, SUB):
                for m in range(j, SUB):
                    block[j][m] = block[j][m] - lower[j][i] * block[i][m]
            for j in range(i + 1, SUB):
                rows[j] = rows[j] - lower[j][i] * rows[i]
        scaled = [rows[i] * inverse[i] for i in range(SUB)]
        for g in range(p + 1, len(groups)):
            tile = groups[g]
            columns = [
                jnp.broadcast_to(tile[:, first + j : first + j + 1], (SUB, LANES)) for j in range(SUB)
            ]
            for i in range(SUB):
                for j in range(i + 1, SUB):
                    columns[j] = columns[j] - columns[i] * lower[j][i]
            for i in range(SUB):
                tile = tile - columns[i] * scaled[i]
            groups[g] = tile
        out = rows[0] * lax.rsqrt(block[0][0])
        for i in range(1, SUB):
            out = jnp.where(sub == i, rows[i] * lax.rsqrt(block[i][i]), out)
        done.append(out)
    return done


def begin(inner, work):
    order = inner.shape[0]
    row = lax.broadcasted_iota(jnp.int32, (order, order), 0)
    col = lax.broadcasted_iota(jnp.int32, (order, order), 1)
    work[:, :order] = inner
    work[:, order:] = (row == col).astype(jnp.float32)


def step(work, top, ones):
    order = work.shape[0]
    low = top + HALF
    lane = lax.broadcasted_iota(jnp.int32, (SUB, LANES), 1)
    sub = lax.broadcasted_iota(jnp.int32, (SUB, LANES), 0)
    groups = []
    for g in range(HALF // SUB):
        tile = work[top + g * SUB : top + (g + 1) * SUB, top:low]
        unit = (lane == sub + (g * SUB + HALF)).astype(jnp.float32)
        groups.append(jnp.concatenate([tile, unit[:, HALF:]], axis=1))
    small = jnp.concatenate([tile[:, HALF:] for tile in eliminate(groups, ones)], axis=0)
    wide = mm(small, work[top:low, :], 1, 0)
    if low < order:
        work[low:, :] = work[low:, :] - mm(wide[:, low:order], wide, 0, 0)
    work[top:low, :] = wide


def lanes(d, count, rows):
    if rows % LANES:
        return pl.ds(d * rows, rows)
    here = lax.axis_index("mode")
    return pl.ds(pl.multiple_of(lax.rem(here - d + count, count) * rows, rows), rows)


def stage_side(stage):
    axis, bit = stage
    return lax.rem(lax.axis_index(axis) // bit, 2)


def row_places(stages, height):
    members = 1 << (len(stages) - 1)
    share = height // (2 * members)
    mine = sum((stage_side(stage) << index) for index, stage in enumerate(stages[1:]))
    side = stage_side(stages[0])
    return [
        [pl.ds(pl.multiple_of((top * members + (mine ^ d)) * share, share), share) for d in range(members)]
        for top in (side, 1 - side)
    ]


def gather_rows(parts, stages, matrix):
    for part, places in zip(parts, row_places(stages, matrix.shape[0])):
        share = part.shape[0] // len(places)
        for d, place in enumerate(places):
            matrix[place, :] = part[d * share : (d + 1) * share, :]


def spread_out(inner, blocks, outs, stages, matrix):
    count, rows = len(blocks), blocks[0].shape[0]
    for d, block in enumerate(blocks):
        matrix[:, lanes(d, count, rows)] = mm(inner, block[...], 1, 1)
    for out, places in zip(outs, row_places(stages, matrix.shape[0])):
        share = out.shape[0] // len(places)
        for d, place in enumerate(places):
            out[d * share : (d + 1) * share, :] = matrix[place, :]


def first_kernel(count, stages, basis_ref, *refs):
    blocks, outs, matrix = refs[:count], refs[count:-1], refs[-1]
    rows = blocks[0].shape[0]
    here = lax.axis_index("mode")
    inner = None
    for d, block in enumerate(blocks):
        place = pl.ds(pl.multiple_of(lax.rem(here - d + count, count) * rows, rows), rows)
        term = mm(basis_ref[place, :], block[...], 0, 0)
        inner = term if inner is None else inner + term
    spread_out(inner, blocks, outs, stages, matrix)


def second_kernel(count, inputs, stages, *refs):
    parts, blocks = refs[:inputs], refs[inputs : inputs + count]
    outs, matrix = refs[inputs + count : -1], refs[-1]
    rows = blocks[0].shape[0]
    gather_rows(parts, stages, matrix)
    inner = None
    for d, block in enumerate(blocks):
        term = mm(matrix[:, lanes(d, count, rows)], block[...], 1, 0)
        inner = term if inner is None else inner + term
    spread_out(inner * LIFT, blocks, outs, stages, matrix)


def inner_kernel(stages, *refs):
    *parts, work, matrix = refs
    gather_rows(parts, stages, matrix)
    whole = matrix[...]
    begin(mm(whole, whole, 1, 1), work)


def step_kernel(top, work_ref, work, ones):
    ones[...] = jnp.ones_like(ones)
    work[...] = work_ref[...]
    step(work, top, ones[...])


def last_kernel(count, inputs, stages, work_ref, *refs):
    parts, blocks = refs[:inputs], refs[inputs : inputs + count]
    outs, (work, matrix, held, ones) = refs[inputs + count : -4], refs[-4:]
    rank, rows = matrix.shape[0], blocks[0].shape[0]
    gather_rows(parts, stages, matrix)
    factor = work_ref[:, rank:] * (1.0 / LIFT)
    inner = None
    projected = None
    for d, block in enumerate(blocks):
        basis = mm(factor, matrix[:, lanes(d, count, rows)], 1, 0)
        term = mm(basis, basis, 1, 1)
        inner = term if inner is None else inner + term
        term = mm(basis, block[...], 1, 0)
        projected = term if projected is None else projected + term
    held[...] = projected
    begin(inner, work)
    ones[...] = jnp.ones_like(ones)
    for top in range(0, rank, HALF):
        step(work, top, ones[...])
    held[...] = mm(work[:, rank:], held[...], 1, 0)
    here = lax.axis_index("mode")
    part = rank // count
    for d, out in enumerate(outs):
        place = pl.ds(pl.multiple_of(lax.rem(here + d, count) * part, part), part)
        out[...] = held[place, :]


def pick_kernel(distances, count, fibres, slab_ref, *outs):
    rows, width = outs[0].shape
    share = width // LANES
    for d, out in zip(distances, outs):
        target = lax.rem(lax.axis_index("mode") + d, count)
        for j in range(share):
            start = target * share + j
            out[:, j * LANES : (j + 1) * LANES] = slab_ref[pl.ds(start, rows, stride=fibres), :]


def join_kernel(fibres, *refs):
    *pieces, out_ref = refs
    count = len(pieces)
    rows, width = pieces[0].shape
    share = width // LANES
    for d, piece in enumerate(pieces):
        source = lax.rem(lax.axis_index("mode") - d + count, count)
        for j in range(share):
            start = source * share + j
            out_ref[pl.ds(start, rows, stride=fibres), :] = piece[:, j * LANES : (j + 1) * LANES]


def call(kernel, out_shapes, scratch, *operands, **options):
    whole = pl.BlockSpec(memory_space=pltpu.VMEM)
    return pl.pallas_call(
        kernel,
        out_shape=[jax.ShapeDtypeStruct(shape, jnp.float32) for shape in out_shapes],
        in_specs=[whole] * len(operands),
        out_specs=[whole] * len(out_shapes),
        scratch_shapes=[pltpu.VMEM(shape, jnp.float32) for shape in scratch],
        compiler_params=pltpu.CompilerParams(vmem_limit_bytes=VMEM_BYTES),
        **options,
    )(*operands)


def exchange(block, axis, bit):
    size = lax.axis_size(axis)
    return lax.ppermute(block, axis, [(k, k ^ bit) for k in range(size)])


def bits_of(axis):
    return [1 << b for b in range(lax.axis_size(axis).bit_length() - 1)]


def plane_exchange(block, stages, d):
    inner = lax.axis_size("rb")
    flip = 0
    for index, (axis, bit) in enumerate(stages[1:]):
        flip |= (d >> index & 1) * (bit if axis == "rb" else bit * inner)
    size = inner * lax.axis_size("ra")
    return lax.ppermute(block, ("ra", "rb"), [(k, k ^ flip) for k in range(size)])


def all_reduce(kept, sent, stages):
    members = 1 << (len(stages) - 1)
    share = kept.shape[0] // members
    far_first = range(members - 1, 0, -1)
    got = exchange(sent, *stages[0])

    def summed(d):
        place = slice(d * share, (d + 1) * share)
        return kept[place] + got[place]

    arrived = []
    for d in far_first:
        part = summed(d)
        arrived.append(plane_exchange(part, stages, d))
    held = summed(0)
    for part in arrived:
        held = held + part
    for bit in bits_of("mode"):
        held = held + exchange(held, "mode", bit)
    whole = {0: held}
    for d in far_first:
        whole[d] = plane_exchange(held, stages, d)
    held = jnp.concatenate([whole[d] for d in range(members)])
    return [held, exchange(held, *stages[0])]


def turned(blocks, count, here):
    return jnp.stack(
        [
            lax.dynamic_index_in_dim(blocks, (here - d) % count, 0, keepdims=False)
            for d in range(count)
        ]
    )


def shifted(piece, d, count):
    return lax.ppermute(piece, "mode", [(k, (k + d) % count) for k in range(count)]) if d else piece


def body(density_slab, start_basis):
    count = lax.axis_size("mode")
    here = lax.axis_index("mode")
    rows, nj, nk = density_slab.shape
    width, rank = start_basis.shape
    stages = [(axis, bit) for axis in ("rb", "ra") for bit in bits_of(axis)]

    share = nj // count
    slab = density_slab.reshape(rows * nj, nk)
    far_first = sorted(range(1, count), key=lambda d: abs(d - count // 2))
    blocks = [None] * count
    for distances in (far_first[:1], far_first[1:] + [0]):
        picked = call(
            functools.partial(pick_kernel, distances, count, nj),
            [(rows, share * nk)] * len(distances),
            [],
            slab,
        )
        for d, piece in zip(distances, picked):
            blocks[d] = shifted(piece, d, count)

    def turn(matrix):
        if rows % LANES == 0:
            return matrix
        split = matrix.reshape(-1, count, rows).transpose(1, 0, 2)
        return turned(split, count, here).transpose(1, 0, 2).reshape(-1, width)

    def total(partials):
        kept, sent = partials
        return all_reduce(turn(kept), turn(sent), stages)

    half = [(rank // 2, width)] * 2
    inner_shape = (rank, share * nk)
    tall = (rank, width)
    work = (rank, 2 * rank)
    applied = total(
        call(
            functools.partial(first_kernel, count, stages),
            half,
            [tall],
            start_basis,
            *blocks,
        ),
    )
    turned_in = [turn(part) for part in applied]
    again = total(
        call(
            functools.partial(second_kernel, count, len(applied), stages),
            half,
            [tall],
            *turned_in,
            *blocks,
        ),
    )
    (factor,) = call(functools.partial(inner_kernel, stages), [work], [tall], *applied)
    for top in range(0, rank, HALF):
        (factor,) = call(functools.partial(step_kernel, top), [work], [(SUB, LANES)], factor)
    outward = call(
        functools.partial(last_kernel, count, len(again), stages),
        [(rank // count, share * nk)] * count,
        [work, tall, inner_shape, (SUB, LANES)],
        factor,
        *[turn(part) for part in again],
        *blocks,
    )
    back = [shifted(piece, d, count) for d, piece in enumerate(outward)]
    (out,) = call(functools.partial(join_kernel, nj), [(rank // count * nj, nk)], [], *back)
    return out.reshape(rank // count, nj, nk)


def solution(mesh):
    in_specs = (P("mode", "ra", "rb"), P())
    out_specs = P("mode", "ra", "rb")

    return jax.shard_map(body, mesh=mesh, in_specs=in_specs, out_specs=out_specs, check_vma=False)
```

profile of v0, /device:TPU:0, one launch (start us, length us, event | category | flops | bytes accessed | tf_op | source)
XLA Modules:
  0.0 167.4 jit_solution(7929289097785266446)
XLA Ops:
  1.8 4.1 %collective-permute-start.1 = (f32[256,512]{1,0:T(8,128)S(1)}, f32[256,512]{1,0:T(8,128)S(1)}, u32[]{:S(2)}, u32[]{:S(2)}) collective-permute-start(f32[256,512]{1,0:T(8,128)S(1)} %shard_map.29), channel_id=1, source_target_pairs={{0,16},{8,24},{16,0},{24,8},{1,17},{9,25},{17,1},{25,9},{2,18},{10... | collective-permute-start | bytes 1572872 | tf_op jit(solution)/shard_map/ppermute | solution.py:288
  8.3 2.2 %collective-permute-start.2 = (f32[256,512]{1,0:T(8,128)S(1)}, f32[256,512]{1,0:T(8,128)S(1)}, u32[]{:S(2)}, u32[]{:S(2)}) collective-permute-start(f32[256,512]{1,0:T(8,128)S(1)} %get-tuple-element.18), channel_id=1, source_target_pairs={{0,24},{8,0},{16,8},{24,16},{1,25},{9,1},{17,9},{25,17},{2,26},{10... | collective-permute-start | bytes 1572872 | tf_op jit(solution)/shard_map/ppermute | solution.py:288
  10.5 30.7 %collective-permute-done.1.refs_2_.refs_4_ = f32[256,512]{1,0:T(8,128)S(1)} collective-permute-done((f32[256,512]{1,0:T(8,128)S(1)}, f32[256,512]{1,0:T(8,128)S(1)}, u32[]{:S(2)}, u32[]{:S(2)}) %collective-permute-start.1) | collective-permute-done | bytes 524320 | tf_op jit(solution)/shard_map/ppermute | solution.py:288
  42.7 3.8 %shard_map.30 = (f32[128,1024]{1,0:T(8,128)S(1)}, f32[128,1024]{1,0:T(8,128)S(1)}) custom-call(f32[1024,256]{1,0:T(8,128)S(1)} %copy-done.1, f32[256,512]{1,0:T(8,128)S(1)} %get-tuple-element.16.refs_0_.refs_2_, f32[256,512]{1,0:T(8,128)S(1)} %collective-permute-done.refs_1_.refs_3_, f32[256,512]{1,0:T(8,128)S(1)} %collective-permute-done.1.refs_2_.refs_4_, ...), custom_call_target="tpu_custom_call" | custom-call | tf_op jit(solution)/shard_map/pallas_call | solution.py:223
  48.5 2.6 %collective-permute-start.4 = (f32[32,1024]{1,0:T(8,128)S(1)}, f32[32,1024]{1,0:T(8,128)S(1)}, u32[]{:S(2)}, u32[]{:S(2)}) collective-permute-start(f32[32,1024]{1,0:T(8,128)S(1)} %get-tuple-element.30), channel_id=1, source_target_pairs={{0,6},{1,7},{2,4},{3,5},{4,2},{5,3},{6,0},{7,1},{8,14},{9,15},{10,... | collective-permute-start | bytes 393224 | tf_op jit(solution)/shard_map/ppermute | solution.py:249
  52.1 3.8 %collective-permute-done.4 = f32[32,1024]{1,0:T(8,128)S(1)} collective-permute-done((f32[32,1024]{1,0:T(8,128)S(1)}, f32[32,1024]{1,0:T(8,128)S(1)}, u32[]{:S(2)}, u32[]{:S(2)}) %collective-permute-start.4) | collective-permute-done | bytes 131104 | tf_op jit(solution)/shard_map/ppermute | solution.py:249
  58.0 9.6 %collective-permute-start.7 = (f32[32,1024]{1,0:T(8,128)S(1)}, f32[32,1024]{1,0:T(8,128)S(1)}, u32[]{:S(2)}, u32[]{:S(2)}) collective-permute-start(f32[32,1024]{1,0:T(8,128)S(1)} %fusion.5), channel_id=1, source_target_pairs={{0,8},{8,0},{16,24},{24,16},{1,9},{9,1},{17,25},{25,17},{2,10},{10... | collective-permute-start | bytes 393224 | tf_op jit(solution)/shard_map/ppermute | solution.py:236
  67.6 3.2 %collective-permute-done.7 = f32[32,1024]{1,0:T(8,128)S(1)} collective-permute-done((f32[32,1024]{1,0:T(8,128)S(1)}, f32[32,1024]{1,0:T(8,128)S(1)}, u32[]{:S(2)}, u32[]{:S(2)}) %collective-permute-start.7) | collective-permute-done | bytes 131104 | tf_op jit(solution)/shard_map/ppermute | solution.py:236
  70.9 3.7 %collective-permute-start.8 = (f32[32,1024]{1,0:T(8,128)S(1)}, f32[32,1024]{1,0:T(8,128)S(1)}, u32[]{:S(2)}, u32[]{:S(2)}) collective-permute-start(f32[32,1024]{1,0:T(8,128)S(1)} %add.61), channel_id=1, source_target_pairs={{0,16},{8,24},{16,0},{24,8},{1,17},{9,25},{17,1},{25,9},{2,18},{10... | collective-permute-start | bytes 393224 | tf_op jit(solution)/shard_map/ppermute | solution.py:236
  74.6 5.2 %collective-permute-done.8 = f32[32,1024]{1,0:T(8,128)S(1)} collective-permute-done((f32[32,1024]{1,0:T(8,128)S(1)}, f32[32,1024]{1,0:T(8,128)S(1)}, u32[]{:S(2)}, u32[]{:S(2)}) %collective-permute-start.8) | collective-permute-done | bytes 131104 | tf_op jit(solution)/shard_map/ppermute | solution.py:236
  79.8 3.3 %collective-permute-start.11 = (f32[32,1024]{1,0:T(8,128)S(1)}, f32[32,1024]{1,0:T(8,128)S(1)}, u32[]{:S(2)}, u32[]{:S(2)}) collective-permute-start(f32[32,1024]{1,0:T(8,128)S(1)} %add.62), channel_id=1, source_target_pairs={{0,6},{1,7},{2,4},{3,5},{4,2},{5,3},{6,0},{7,1},{8,14},{9,15},{10,... | collective-permute-start | bytes 393224 | tf_op jit(solution)/shard_map/ppermute | solution.py:249
  83.8 3.2 %collective-permute-done.11 = f32[32,1024]{1,0:T(8,128)S(1)} collective-permute-done((f32[32,1024]{1,0:T(8,128)S(1)}, f32[32,1024]{1,0:T(8,128)S(1)}, u32[]{:S(2)}, u32[]{:S(2)}) %collective-permute-start.11) | collective-permute-done | bytes 131104 | tf_op jit(solution)/shard_map/ppermute | solution.py:249
  87.0 2.4 %collective-permute-done.10 = f32[32,1024]{1,0:T(8,128)S(1)} collective-permute-done((f32[32,1024]{1,0:T(8,128)S(1)}, f32[32,1024]{1,0:T(8,128)S(1)}, u32[]{:S(2)}, u32[]{:S(2)}) %collective-permute-start.10) | collective-permute-done | bytes 131104 | tf_op jit(solution)/shard_map/ppermute | solution.py:249
  91.8 3.8 %shard_map.36 = (f32[128,1024]{1,0:T(8,128)S(1)}, f32[128,1024]{1,0:T(8,128)S(1)}) custom-call(f32[128,1024]{1,0:T(8,128)S(1)} %pad_maximum_fusion.refs_0_, f32[128,1024]{1,0:T(8,128)S(1)} %collective-permute-done.12.refs_1_, f32[256,512]{1,0:T(8,128)S(1)} %get-tuple-element.16.refs_0_.refs_2_, f32[256,512]{1,0:T(8,128)S(1)} %collective-permute-done.refs_1_.refs_3_, ...), custom_call_target="tpu_custom_call" | custom-call | tf_op jit(solution)/shard_map/pallas_call | solution.py:223
  101.2 3.8 %collective-permute-done.14 = f32[32,1024]{1,0:T(8,128)S(1)} collective-permute-done((f32[32,1024]{1,0:T(8,128)S(1)}, f32[32,1024]{1,0:T(8,128)S(1)}, u32[]{:S(2)}, u32[]{:S(2)}) %collective-permute-start.14) | collective-permute-done | bytes 131104 | tf_op jit(solution)/shard_map/ppermute | solution.py:249
  107.0 5.1 %collective-permute-done.17 = f32[32,1024]{1,0:T(8,128)S(1)} collective-permute-done((f32[32,1024]{1,0:T(8,128)S(1)}, f32[32,1024]{1,0:T(8,128)S(1)}, u32[]{:S(2)}, u32[]{:S(2)}) %collective-permute-start.17) | collective-permute-done | bytes 131104 | tf_op jit(solution)/shard_map/ppermute | solution.py:236
  112.9 7.2 %collective-permute-done.18 = f32[32,1024]{1,0:T(8,128)S(1)} collective-permute-done((f32[32,1024]{1,0:T(8,128)S(1)}, f32[32,1024]{1,0:T(8,128)S(1)}, u32[]{:S(2)}, u32[]{:S(2)}) %collective-permute-start.18) | collective-permute-done | bytes 131104 | tf_op jit(solution)/shard_map/ppermute | solution.py:236
  123.9 2.9 %collective-permute-done.21 = f32[32,1024]{1,0:T(8,128)S(1)} collective-permute-done((f32[32,1024]{1,0:T(8,128)S(1)}, f32[32,1024]{1,0:T(8,128)S(1)}, u32[]{:S(2)}, u32[]{:S(2)}) %collective-permute-start.21) | collective-permute-done | bytes 131104 | tf_op jit(solution)/shard_map/ppermute | solution.py:249
  131.2 2.4 %shard_map.32.work_ref = f32[256,512]{1,0:T(8,128)S(1)} custom-call(f32[256,512]{1,0:T(8,128)S(1)} %shard_map.31.work_ref), custom_call_target="tpu_custom_call" | custom-call | tf_op jit(solution)/shard_map/pallas_call | solution.py:223
  133.7 2.5 %shard_map.33.work_ref = f32[256,512]{1,0:T(8,128)S(1)} custom-call(f32[256,512]{1,0:T(8,128)S(1)} %shard_map.32.work_ref), custom_call_target="tpu_custom_call" | custom-call | tf_op jit(solution)/shard_map/pallas_call | solution.py:223
  140.4 13.0 %shard_map.37 = (f32[64,512]{1,0:T(8,128)S(1)}, f32[64,512]{1,0:T(8,128)S(1)}, f32[64,512]{1,0:T(8,128)S(1)}, f32[64,512]{1,0:T(8,128)S(1)}) custom-call(f32[256,512]{1,0:T(8,128)S(1)} %shard_map.35.work_ref, f32[128,1024]{1,0:T(8,128)S(1)} %pad_maximum_fusion.1.refs_0_, f32[128,1024]{1,0:T(8,128)S(1)} %collective-permute-done.22.refs_1_, ...), custom_call_target="tpu_custom_call" | custom-call | tf_op jit(solution)/shard_map/pallas_call | solution.py:223
  153.5 2.5 %collective-permute-start.24 = (f32[64,512]{1,0:T(8,128)S(1)}, f32[64,512]{1,0:T(8,128)S(1)}, u32[]{:S(2)}, u32[]{:S(2)}) collective-permute-start(f32[64,512]{1,0:T(8,128)S(1)} %get-tuple-element.25), channel_id=1, source_target_pairs={{0,16},{8,24},{16,0},{24,8},{1,17},{9,25},{17,1},{25,9},{2,18},{10... | collective-permute-start | bytes 393224 | tf_op jit(solution)/shard_map/ppermute | solution.py:288
  157.3 4.5 %collective-permute-done.23.refs_1_ = f32[64,512]{1,0:T(8,128)S(1)} collective-permute-done((f32[64,512]{1,0:T(8,128)S(1)}, f32[64,512]{1,0:T(8,128)S(1)}, u32[]{:S(2)}, u32[]{:S(2)}) %collective-permute-start.23) | collective-permute-done | bytes 131104 | tf_op jit(solution)/shard_map/ppermute | solution.py:288
  161.8 4.7 %collective-permute-done.24.refs_2_ = f32[64,512]{1,0:T(8,128)S(1)} collective-permute-done((f32[64,512]{1,0:T(8,128)S(1)}, f32[64,512]{1,0:T(8,128)S(1)}, u32[]{:S(2)}, u32[]{:S(2)}) %collective-permute-start.24) | collective-permute-done | bytes 131104 | tf_op jit(solution)/shard_map/ppermute | solution.py:288
  (53 shorter events, 36.9 us)
Async XLA Ops:
  1.8 39.4 %collective-permute-start.1 = (f32[256,512]{1,0:T(8,128)S(1)}, f32[256,512]{1,0:T(8,128)S(1)}, u32[]{:S(2)}, u32[]{:S(2)}) collective-permute-start(f32[256,512]{1,0:T(8,128)S(1)} %shard_map.29), channel_id=1, source_target_pairs={{0,16},{8,24},{16,0},{24,8},{1,17},{9,25},{17,1},{25,9},{2,18},{10... | collective-permute-start | bytes 1572872 | tf_op jit(solution)/shard_map/ppermute | solution.py:288
  6.7 34.6 %collective-permute-start = (f32[256,512]{1,0:T(8,128)S(1)}, f32[256,512]{1,0:T(8,128)S(1)}, u32[]{:S(2)}, u32[]{:S(2)}) collective-permute-start(f32[256,512]{1,0:T(8,128)S(1)} %get-tuple-element.17), channel_id=1, source_target_pairs={{0,8},{8,16},{16,24},{24,0},{1,9},{9,17},{17,25},{25,1},{2,10},{10... | collective-permute-start | bytes 1572872 | tf_op jit(solution)/shard_map/ppermute | solution.py:288
  8.3 34.4 %collective-permute-start.2 = (f32[256,512]{1,0:T(8,128)S(1)}, f32[256,512]{1,0:T(8,128)S(1)}, u32[]{:S(2)}, u32[]{:S(2)}) collective-permute-start(f32[256,512]{1,0:T(8,128)S(1)} %get-tuple-element.18), channel_id=1, source_target_pairs={{0,24},{8,0},{16,8},{24,16},{1,25},{9,1},{17,9},{25,17},{2,26},{10... | collective-permute-start | bytes 1572872 | tf_op jit(solution)/shard_map/ppermute | solution.py:288
  46.5 2.0 %collective-permute-start.3 = (f32[128,1024]{1,0:T(8,128)S(1)}, f32[128,1024]{1,0:T(8,128)S(1)}, u32[]{:S(2)}, u32[]{:S(2)}) collective-permute-start(f32[128,1024]{1,0:T(8,128)S(1)} %get-tuple-element.20), channel_id=1, source_target_pairs={{0,1},{1,0},{2,3},{3,2},{4,5},{5,4},{6,7},{7,6},{8,9},{9,8},{10,11... | collective-permute-start | bytes 1572872 | tf_op jit(solution)/shard_map/ppermute | solution.py:236
  48.5 7.3 %collective-permute-start.4 = (f32[32,1024]{1,0:T(8,128)S(1)}, f32[32,1024]{1,0:T(8,128)S(1)}, u32[]{:S(2)}, u32[]{:S(2)}) collective-permute-start(f32[32,1024]{1,0:T(8,128)S(1)} %get-tuple-element.30), channel_id=1, source_target_pairs={{0,6},{1,7},{2,4},{3,5},{4,2},{5,3},{6,0},{7,1},{8,14},{9,15},{10,... | collective-permute-start | bytes 393224 | tf_op jit(solution)/shard_map/ppermute | solution.py:249
  51.1 6.9 %collective-permute-start.6 = (f32[32,1024]{1,0:T(8,128)S(1)}, f32[32,1024]{1,0:T(8,128)S(1)}, u32[]{:S(2)}, u32[]{:S(2)}) collective-permute-start(f32[32,1024]{1,0:T(8,128)S(1)} %get-tuple-element.31), channel_id=1, source_target_pairs={{0,2},{1,3},{2,0},{3,1},{4,6},{5,7},{6,4},{7,5},{8,10},{9,11},{10,... | collective-permute-start | bytes 393224 | tf_op jit(solution)/shard_map/ppermute | solution.py:249
  51.6 6.3 %collective-permute-start.5 = (f32[32,1024]{1,0:T(8,128)S(1)}, f32[32,1024]{1,0:T(8,128)S(1)}, u32[]{:S(2)}, u32[]{:S(2)}) collective-permute-start(f32[32,1024]{1,0:T(8,128)S(1)} %get-tuple-element.32), channel_id=1, source_target_pairs={{0,4},{1,5},{2,6},{3,7},{4,0},{5,1},{6,2},{7,3},{8,12},{9,13},{10,... | collective-permute-start | bytes 393224 | tf_op jit(solution)/shard_map/ppermute | solution.py:249
  58.0 12.9 %collective-permute-start.7 = (f32[32,1024]{1,0:T(8,128)S(1)}, f32[32,1024]{1,0:T(8,128)S(1)}, u32[]{:S(2)}, u32[]{:S(2)}) collective-permute-start(f32[32,1024]{1,0:T(8,128)S(1)} %fusion.5), channel_id=1, source_target_pairs={{0,8},{8,0},{16,24},{24,16},{1,9},{9,1},{17,25},{25,17},{2,10},{10... | collective-permute-start | bytes 393224 | tf_op jit(solution)/shard_map/ppermute | solution.py:236
  70.9 8.9 %collective-permute-start.8 = (f32[32,1024]{1,0:T(8,128)S(1)}, f32[32,1024]{1,0:T(8,128)S(1)}, u32[]{:S(2)}, u32[]{:S(2)}) collective-permute-start(f32[32,1024]{1,0:T(8,128)S(1)} %add.61), channel_id=1, source_target_pairs={{0,16},{8,24},{16,0},{24,8},{1,17},{9,25},{17,1},{25,9},{2,18},{10... | collective-permute-start | bytes 393224 | tf_op jit(solution)/shard_map/ppermute | solution.py:236
  79.8 7.2 %collective-permute-start.11 = (f32[32,1024]{1,0:T(8,128)S(1)}, f32[32,1024]{1,0:T(8,128)S(1)}, u32[]{:S(2)}, u32[]{:S(2)}) collective-permute-start(f32[32,1024]{1,0:T(8,128)S(1)} %add.62), channel_id=1, source_target_pairs={{0,6},{1,7},{2,4},{3,5},{4,2},{5,3},{6,0},{7,1},{8,14},{9,15},{10,... | collective-permute-start | bytes 393224 | tf_op jit(solution)/shard_map/ppermute | solution.py:249
  83.1 6.3 %collective-permute-start.10 = (f32[32,1024]{1,0:T(8,128)S(1)}, f32[32,1024]{1,0:T(8,128)S(1)}, u32[]{:S(2)}, u32[]{:S(2)}) collective-permute-start(f32[32,1024]{1,0:T(8,128)S(1)} %add.62), channel_id=1, source_target_pairs={{0,4},{1,5},{2,6},{3,7},{4,0},{5,1},{6,2},{7,3},{8,12},{9,13},{10,... | collective-permute-start | bytes 393224 | tf_op jit(solution)/shard_map/ppermute | solution.py:249
  83.1 6.6 %collective-permute-start.9 = (f32[32,1024]{1,0:T(8,128)S(1)}, f32[32,1024]{1,0:T(8,128)S(1)}, u32[]{:S(2)}, u32[]{:S(2)}) collective-permute-start(f32[32,1024]{1,0:T(8,128)S(1)} %add.62), channel_id=1, source_target_pairs={{0,2},{1,3},{2,0},{3,1},{4,6},{5,7},{6,4},{7,5},{8,10},{9,11},{10,... | collective-permute-start | bytes 393224 | tf_op jit(solution)/shard_map/ppermute | solution.py:249
  97.6 7.3 %collective-permute-start.14 = (f32[32,1024]{1,0:T(8,128)S(1)}, f32[32,1024]{1,0:T(8,128)S(1)}, u32[]{:S(2)}, u32[]{:S(2)}) collective-permute-start(f32[32,1024]{1,0:T(8,128)S(1)} %get-tuple-element.27), channel_id=1, source_target_pairs={{0,6},{1,7},{2,4},{3,5},{4,2},{5,3},{6,0},{7,1},{8,14},{9,15},{10,... | collective-permute-start | bytes 393224 | tf_op jit(solution)/shard_map/ppermute | solution.py:249
  99.2 7.7 %collective-permute-start.16 = (f32[32,1024]{1,0:T(8,128)S(1)}, f32[32,1024]{1,0:T(8,128)S(1)}, u32[]{:S(2)}, u32[]{:S(2)}) collective-permute-start(f32[32,1024]{1,0:T(8,128)S(1)} %get-tuple-element.28), channel_id=1, source_target_pairs={{0,2},{1,3},{2,0},{3,1},{4,6},{5,7},{6,4},{7,5},{8,10},{9,11},{10,... | collective-permute-start | bytes 393224 | tf_op jit(solution)/shard_map/ppermute | solution.py:249
  100.6 6.3 %collective-permute-start.15 = (f32[32,1024]{1,0:T(8,128)S(1)}, f32[32,1024]{1,0:T(8,128)S(1)}, u32[]{:S(2)}, u32[]{:S(2)}) collective-permute-start(f32[32,1024]{1,0:T(8,128)S(1)} %get-tuple-element.29), channel_id=1, source_target_pairs={{0,4},{1,5},{2,6},{3,7},{4,0},{5,1},{6,2},{7,3},{8,12},{9,13},{10,... | collective-permute-start | bytes 393224 | tf_op jit(solution)/shard_map/ppermute | solution.py:249
  107.0 5.1 %collective-permute-start.17 = (f32[32,1024]{1,0:T(8,128)S(1)}, f32[32,1024]{1,0:T(8,128)S(1)}, u32[]{:S(2)}, u32[]{:S(2)}) collective-permute-start(f32[32,1024]{1,0:T(8,128)S(1)} %fusion.2), channel_id=1, source_target_pairs={{0,8},{8,0},{16,24},{24,16},{1,9},{9,1},{17,25},{25,17},{2,10},{10... | collective-permute-start | bytes 393224 | tf_op jit(solution)/shard_map/ppermute | solution.py:236
  112.1 8.0 %collective-permute-start.18 = (f32[32,1024]{1,0:T(8,128)S(1)}, f32[32,1024]{1,0:T(8,128)S(1)}, u32[]{:S(2)}, u32[]{:S(2)}) collective-permute-start(f32[32,1024]{1,0:T(8,128)S(1)} %add.70), channel_id=1, source_target_pairs={{0,16},{8,24},{16,0},{24,8},{1,17},{9,25},{17,1},{25,9},{2,18},{10... | collective-permute-start | bytes 393224 | tf_op jit(solution)/shard_map/ppermute | solution.py:236
  120.2 6.6 %collective-permute-start.21 = (f32[32,1024]{1,0:T(8,128)S(1)}, f32[32,1024]{1,0:T(8,128)S(1)}, u32[]{:S(2)}, u32[]{:S(2)}) collective-permute-start(f32[32,1024]{1,0:T(8,128)S(1)} %add.71), channel_id=1, source_target_pairs={{0,6},{1,7},{2,4},{3,5},{4,2},{5,3},{6,0},{7,1},{8,14},{9,15},{10,... | collective-permute-start | bytes 393224 | tf_op jit(solution)/shard_map/ppermute | solution.py:249
  121.8 7.2 %collective-permute-start.20 = (f32[32,1024]{1,0:T(8,128)S(1)}, f32[32,1024]{1,0:T(8,128)S(1)}, u32[]{:S(2)}, u32[]{:S(2)}) collective-permute-start(f32[32,1024]{1,0:T(8,128)S(1)} %add.71), channel_id=1, source_target_pairs={{0,4},{1,5},{2,6},{3,7},{4,0},{5,1},{6,2},{7,3},{8,12},{9,13},{10,... | collective-permute-start | bytes 393224 | tf_op jit(solution)/shard_map/ppermute | solution.py:249
  123.9 6.1 %collective-permute-start.19 = (f32[32,1024]{1,0:T(8,128)S(1)}, f32[32,1024]{1,0:T(8,128)S(1)}, u32[]{:S(2)}, u32[]{:S(2)}) collective-permute-start(f32[32,1024]{1,0:T(8,128)S(1)} %add.71), channel_id=1, source_target_pairs={{0,2},{1,3},{2,0},{3,1},{4,6},{5,7},{6,4},{7,5},{8,10},{9,11},{10,... | collective-permute-start | bytes 393224 | tf_op jit(solution)/shard_map/ppermute | solution.py:249
  130.0 10.4 %collective-permute-start.22 = (f32[128,1024]{1,0:T(8,128)S(1)}, f32[128,1024]{1,0:T(8,128)S(1)}, u32[]{:S(2)}, u32[]{:S(2)}) collective-permute-start(f32[128,1024]{1,0:T(8,128)S(1)} %pad_maximum_fusion.1.refs_0_), channel_id=1, source_target_pairs={{0,1},{1,0},{2,3},{3,2},{4,5},{5,4},{6,7},{7,6},{8,9},{9,8},{10,11... | collective-permute-start | bytes 1572872 | tf_op jit(solution)/shard_map/ppermute | solution.py:236
  153.4 8.4 %collective-permute-start.23 = (f32[64,512]{1,0:T(8,128)S(1)}, f32[64,512]{1,0:T(8,128)S(1)}, u32[]{:S(2)}, u32[]{:S(2)}) collective-permute-start(f32[64,512]{1,0:T(8,128)S(1)} %get-tuple-element.24), channel_id=1, source_target_pairs={{0,8},{8,16},{16,24},{24,0},{1,9},{9,17},{17,25},{25,1},{2,10},{10... | collective-permute-start | bytes 393224 | tf_op jit(solution)/shard_map/ppermute | solution.py:288
  153.5 13.0 %collective-permute-start.24 = (f32[64,512]{1,0:T(8,128)S(1)}, f32[64,512]{1,0:T(8,128)S(1)}, u32[]{:S(2)}, u32[]{:S(2)}) collective-permute-start(f32[64,512]{1,0:T(8,128)S(1)} %get-tuple-element.25), channel_id=1, source_target_pairs={{0,16},{8,24},{16,0},{24,8},{1,17},{9,25},{17,1},{25,9},{2,18},{10... | collective-permute-start | bytes 393224 | tf_op jit(solution)/shard_map/ppermute | solution.py:288
  155.9 10.5 %collective-permute-start.25 = (f32[64,512]{1,0:T(8,128)S(1)}, f32[64,512]{1,0:T(8,128)S(1)}, u32[]{:S(2)}, u32[]{:S(2)}) collective-permute-start(f32[64,512]{1,0:T(8,128)S(1)} %get-tuple-element.26), channel_id=1, source_target_pairs={{0,24},{8,0},{16,8},{24,16},{1,25},{9,1},{17,9},{25,17},{2,26},{10... | collective-permute-start | bytes 393224 | tf_op jit(solution)/shard_map/ppermute | solution.py:288
  (4 other events, 46.6 us)
where the time goes:
time: 168 us; the launch traced here: 167 us
  waiting for transfers between devices  91.3 us (54%)
  starting transfers between devices  41.3 us (25%)
  Pallas kernels  32.7 us (19%)
    ppermute x6, waiting for transfers between devices, shifted(): lax.ppermute(piece, 'mode', [(k, (k + d) % count) for k in range(count)])  41.3 us
    pallas_call x11, Pallas kernels, call(): pl.pallas_call(kernel, out_shape=[jax.ShapeDtypeStruct(shape, jnp.float32...  32.7 us
    ppermute x8, waiting for transfers between devices, exchange(): return lax.ppermute(block, axis, [(k, k ^ bit) for k in range(size)])  26.3 us
    ppermute x12, waiting for transfers between devices, plane_exchange(): lax.ppermute(block, ('ra', 'rb'), [(k, k ^ flip) for k in range(size)])  23.7 us
    ppermute x12, starting transfers between devices, plane_exchange(): lax.ppermute(block, ('ra', 'rb'), [(k, k ^ flip) for k in range(size)])  14.8 us
    ppermute x8, starting transfers between devices, exchange(): return lax.ppermute(block, axis, [(k, k ^ bit) for k in range(size)])  14.6 us
    ppermute x6, starting transfers between devices, shifted(): lax.ppermute(piece, 'mode', [(k, (k + d) % count) for k in range(count)])  11.9 us
  transfers between devices with their start and end apart: 26, of which 21 were waited for; matrix products, arithmetic and copies ran while one was open for 0% of the time, Pallas kernels for 7%

commit v1 on v0

--- a/solution.py
+++ b/solution.py
@@ -92,11 +92,10 @@
     work[top:low, :] = wide
 
 
-def lanes(d, count, rows):
+def lanes(d, rows):
     if rows % LANES:
         return pl.ds(d * rows, rows)
-    here = lax.axis_index("mode")
-    return pl.ds(pl.multiple_of(lax.rem(here - d + count, count) * rows, rows), rows)
+    return pl.ds(pl.multiple_of((lax.axis_index("mode") ^ d) * rows, rows), rows)
 
 
 def stage_side(stage):
@@ -123,24 +122,32 @@
 
 
 def spread_out(inner, blocks, outs, stages, matrix):
-    count, rows = len(blocks), blocks[0].shape[0]
+    rows = blocks[0].shape[0]
     for d, block in enumerate(blocks):
-        matrix[:, lanes(d, count, rows)] = mm(inner, block[...], 1, 1)
+        matrix[:, lanes(d, rows)] = mm(inner, block[...], 1, 1)
     for out, places in zip(outs, row_places(stages, matrix.shape[0])):
         share = out.shape[0] // len(places)
         for d, place in enumerate(places):
             out[d * share : (d + 1) * share, :] = matrix[place, :]
 
 
-def first_kernel(count, stages, basis_ref, *refs):
+def basis_term(basis_ref, block, d):
+    rows = block.shape[0]
+    place = pl.ds(pl.multiple_of((lax.axis_index("mode") ^ d) * rows, rows), rows)
+    return mm(basis_ref[place, :], block[...], 0, 0)
+
+
+def early_kernel(basis_ref, *refs):
+    *blocks, out_ref = refs
+    inner = basis_term(basis_ref, blocks[0], 0)
+    for d, block in enumerate(blocks[1:], 1):
+        inner = inner + basis_term(basis_ref, block, d)
+    out_ref[...] = inner
+
+
+def first_kernel(count, stages, basis_ref, early_ref, *refs):
     blocks, outs, matrix = refs[:count], refs[count:-1], refs[-1]
-    rows = blocks[0].shape[0]
-    here = lax.axis_index("mode")
-    inner = None
-    for d, block in enumerate(blocks):
-        place = pl.ds(pl.multiple_of(lax.rem(here - d + count, count) * rows, rows), rows)
-        term = mm(basis_ref[place, :], block[...], 0, 0)
-        inner = term if inner is None else inner + term
+    inner = early_ref[...] + basis_term(basis_ref, blocks[-1], count - 1)
     spread_out(inner, blocks, outs, stages, matrix)
 
 
@@ -151,7 +158,7 @@
     gather_rows(parts, stages, matrix)
     inner = None
     for d, block in enumerate(blocks):
-        term = mm(matrix[:, lanes(d, count, rows)], block[...], 1, 0)
+        term = mm(matrix[:, lanes(d, rows)], block[...], 1, 0)
         inner = term if inner is None else inner + term
     spread_out(inner * LIFT, blocks, outs, stages, matrix)
 
@@ -178,7 +185,7 @@
     inner = None
     projected = None
     for d, block in enumerate(blocks):
-        basis = mm(factor, matrix[:, lanes(d, count, rows)], 1, 0)
+        basis = mm(factor, matrix[:, lanes(d, rows)], 1, 0)
         term = mm(basis, basis, 1, 1)
         inner = term if inner is None else inner + term
         term = mm(basis, block[...], 1, 0)
@@ -192,15 +199,15 @@
     here = lax.axis_index("mode")
     part = rank // count
     for d, out in enumerate(outs):
-        place = pl.ds(pl.multiple_of(lax.rem(here + d, count) * part, part), part)
+        place = pl.ds(pl.multiple_of((here ^ d) * part, part), part)
         out[...] = held[place, :]
 
 
-def pick_kernel(distances, count, fibres, slab_ref, *outs):
+def pick_kernel(distances, fibres, slab_ref, *outs):
     rows, width = outs[0].shape
     share = width // LANES
     for d, out in zip(distances, outs):
-        target = lax.rem(lax.axis_index("mode") + d, count)
+        target = lax.axis_index("mode") ^ d
         for j in range(share):
             start = target * share + j
             out[:, j * LANES : (j + 1) * LANES] = slab_ref[pl.ds(start, rows, stride=fibres), :]
@@ -208,11 +215,10 @@
 
 def join_kernel(fibres, *refs):
     *pieces, out_ref = refs
-    count = len(pieces)
     rows, width = pieces[0].shape
     share = width // LANES
     for d, piece in enumerate(pieces):
-        source = lax.rem(lax.axis_index("mode") - d + count, count)
+        source = lax.axis_index("mode") ^ d
         for j in range(share):
             start = source * share + j
             out_ref[pl.ds(start, rows, stride=fibres), :] = piece[:, j * LANES : (j + 1) * LANES]
@@ -278,14 +284,10 @@
 def turned(blocks, count, here):
     return jnp.stack(
         [
-            lax.dynamic_index_in_dim(blocks, (here - d) % count, 0, keepdims=False)
+            lax.dynamic_index_in_dim(blocks, here ^ d, 0, keepdims=False)
             for d in range(count)
         ]
     )
-
-
-def shifted(piece, d, count):
-    return lax.ppermute(piece, "mode", [(k, (k + d) % count) for k in range(count)]) if d else piece
 
 
 def body(density_slab, start_basis):
@@ -297,17 +299,17 @@
 
     share = nj // count
     slab = density_slab.reshape(rows * nj, nk)
-    far_first = sorted(range(1, count), key=lambda d: abs(d - count // 2))
+    far_first = sorted(range(1, count), key=lambda d: (d < count // 2, d))
     blocks = [None] * count
     for distances in (far_first[:1], far_first[1:] + [0]):
         picked = call(
-            functools.partial(pick_kernel, distances, count, nj),
+            functools.partial(pick_kernel, distances, nj),
             [(rows, share * nk)] * len(distances),
             [],
             slab,
         )
         for d, piece in zip(distances, picked):
-            blocks[d] = shifted(piece, d, count)
+            blocks[d] = exchange(piece, "mode", d) if d else piece
 
     def turn(matrix):
         if rows % LANES == 0:
@@ -323,12 +325,14 @@
     inner_shape = (rank, share * nk)
     tall = (rank, width)
     work = (rank, 2 * rank)
+    (early,) = call(early_kernel, [inner_shape], [], start_basis, *blocks[:-1])
     applied = total(
         call(
             functools.partial(first_kernel, count, stages),
             half,
             [tall],
             start_basis,
+            early,
             *blocks,
         ),
     )
@@ -353,7 +357,9 @@
         *[turn(part) for part in again],
         *blocks,
     )
-    back = [shifted(piece, d, count) for d, piece in enumerate(outward)]
+    back = list(outward)
+    for d in far_first:
+        back[d] = exchange(outward[d], "mode", d)
     (out,) = call(functools.partial(join_kernel, nj), [(rank // count * nj, nk)], [], *back)
     return out.reshape(rank // count, nj, nk)
 

time: 168 us -> 167 us (level)
    ppermute x6 -> x0, waiting for transfers between devices: 41.3 us -> none  [shifted(): lax.ppermute(piece, 'mode', [(k, (k + d) % count) for k in range(count)])]
    ppermute x8 -> x14, waiting for transfers between devices: 26.3 us -> 66.7 us  [exchange(): return lax.ppermute(block, axis, [(k, k ^ bit) for k in range(size)])]
    ppermute x6 -> x0, starting transfers between devices: 11.9 us -> none  [shifted(): lax.ppermute(piece, 'mode', [(k, (k + d) % count) for k in range(count)])]
    ppermute x8 -> x14, starting transfers between devices: 14.6 us -> 26 us  [exchange(): return lax.ppermute(block, axis, [(k, k ^ bit) for k in range(size)])]
    pallas_call x11 -> x12, Pallas kernels: 32.7 us -> 33.2 us  [call(): pl.pallas_call(kernel, out_shape=[jax.ShapeDtypeStruct(shape, jnp.float32...]
  transfers between devices with their start and end apart: 26 -> 26, of which waited for: 21 -> 22; matrix products, arithmetic and copies ran while one was open for 0% -> 0% of each run, Pallas kernels for 7% -> 7%
where the time goes in v1:
time: 167 us; the launch traced here: 166 us
  waiting for transfers between devices  90.4 us (54%)
  starting transfers between devices  40.8 us (24%)
  Pallas kernels  33.2 us (20%)
    ppermute x14, waiting for transfers between devices, exchange(): return lax.ppermute(block, axis, [(k, k ^ bit) for k in range(size)])  66.7 us
    pallas_call x12, Pallas kernels, call(): pl.pallas_call(kernel, out_shape=[jax.ShapeDtypeStruct(shape, jnp.float32...  33.2 us
    ppermute x14, starting transfers between devices, exchange(): return lax.ppermute(block, axis, [(k, k ^ bit) for k in range(size)])  26 us
    ppermute x12, waiting for transfers between devices, plane_exchange(): lax.ppermute(block, ('ra', 'rb'), [(k, k ^ flip) for k in range(size)])  23.6 us
    ppermute x12, starting transfers between devices, plane_exchange(): lax.ppermute(block, ('ra', 'rb'), [(k, k ^ flip) for k in range(size)])  14.8 us
  transfers between devices with their start and end apart: 26, of which 22 were waited for; matrix products, arithmetic and copies ran while one was open for 0% of the time, Pallas kernels for 7%

profile of v1, /device:TPU:0, one launch (start us, length us, event | category | flops | bytes accessed | tf_op | source)
XLA Modules:
  0.0 166.4 jit_solution(6159832978846695633)
XLA Ops:
  1.8 4.1 %collective-permute-start.1 = (f32[256,512]{1,0:T(8,128)S(1)}, f32[256,512]{1,0:T(8,128)S(1)}, u32[]{:S(2)}, u32[]{:S(2)}) collective-permute-start(f32[256,512]{1,0:T(8,128)S(1)} %shard_map.29), channel_id=1, source_target_pairs={{0,16},{8,24},{16,0},{24,8},{1,17},{9,25},{17,1},{25,9},{2,18},{10... | collective-permute-start | bytes 1572872 | tf_op jit(solution)/shard_map/ppermute | solution.py:242
  8.3 22.6 %collective-permute-done.1.refs_2_.refs_4_ = f32[256,512]{1,0:T(8,128)S(1)} collective-permute-done((f32[256,512]{1,0:T(8,128)S(1)}, f32[256,512]{1,0:T(8,128)S(1)}, u32[]{:S(2)}, u32[]{:S(2)}) %collective-permute-start.1) | collective-permute-done | bytes 524320 | tf_op jit(solution)/shard_map/ppermute | solution.py:242
  32.7 8.9 %collective-permute-done.2.refs_3_.refs_5_ = f32[256,512]{1,0:T(8,128)S(1)} collective-permute-done((f32[256,512]{1,0:T(8,128)S(1)}, f32[256,512]{1,0:T(8,128)S(1)}, u32[]{:S(2)}, u32[]{:S(2)}) %collective-permute-start.2) | collective-permute-done | bytes 524320 | tf_op jit(solution)/shard_map/ppermute | solution.py:242
  41.6 2.5 %shard_map.31 = (f32[128,1024]{1,0:T(8,128)S(1)}, f32[128,1024]{1,0:T(8,128)S(1)}) custom-call(f32[1024,256]{1,0:T(8,128)S(1)} %copy-done.1, f32[256,512]{1,0:T(8,128)S(1)} %shard_map.30.early_ref, f32[256,512]{1,0:T(8,128)S(1)} %get-tuple-element.16.refs_0_.refs_2_, f32[256,512]{1,0:T(8,128)S(1)} %collective-permute-done.refs_1_.refs_3_, ...), custom_call_target="tpu_custom_call" | custom-call | tf_op jit(solution)/shard_map/pallas_call | solution.py:229
  46.1 2.5 %collective-permute-start.4 = (f32[32,1024]{1,0:T(8,128)S(1)}, f32[32,1024]{1,0:T(8,128)S(1)}, u32[]{:S(2)}, u32[]{:S(2)}) collective-permute-start(f32[32,1024]{1,0:T(8,128)S(1)} %get-tuple-element.30), channel_id=1, source_target_pairs={{0,6},{1,7},{2,4},{3,5},{4,2},{5,3},{6,0},{7,1},{8,14},{9,15},{10,... | collective-permute-start | bytes 393224 | tf_op jit(solution)/shard_map/ppermute | solution.py:255
  49.7 3.8 %collective-permute-done.4 = f32[32,1024]{1,0:T(8,128)S(1)} collective-permute-done((f32[32,1024]{1,0:T(8,128)S(1)}, f32[32,1024]{1,0:T(8,128)S(1)}, u32[]{:S(2)}, u32[]{:S(2)}) %collective-permute-start.4) | collective-permute-done | bytes 131104 | tf_op jit(solution)/shard_map/ppermute | solution.py:255
  55.5 10.8 %collective-permute-start.7 = (f32[32,1024]{1,0:T(8,128)S(1)}, f32[32,1024]{1,0:T(8,128)S(1)}, u32[]{:S(2)}, u32[]{:S(2)}) collective-permute-start(f32[32,1024]{1,0:T(8,128)S(1)} %fusion.5), channel_id=1, source_target_pairs={{0,8},{8,0},{16,24},{24,16},{1,9},{9,1},{17,25},{25,17},{2,10},{10... | collective-permute-start | bytes 393224 | tf_op jit(solution)/shard_map/ppermute | solution.py:242
  66.3 3.2 %collective-permute-done.7 = f32[32,1024]{1,0:T(8,128)S(1)} collective-permute-done((f32[32,1024]{1,0:T(8,128)S(1)}, f32[32,1024]{1,0:T(8,128)S(1)}, u32[]{:S(2)}, u32[]{:S(2)}) %collective-permute-start.7) | collective-permute-done | bytes 131104 | tf_op jit(solution)/shard_map/ppermute | solution.py:242
  69.6 3.7 %collective-permute-start.8 = (f32[32,1024]{1,0:T(8,128)S(1)}, f32[32,1024]{1,0:T(8,128)S(1)}, u32[]{:S(2)}, u32[]{:S(2)}) collective-permute-start(f32[32,1024]{1,0:T(8,128)S(1)} %add.61), channel_id=1, source_target_pairs={{0,16},{8,24},{16,0},{24,8},{1,17},{9,25},{17,1},{25,9},{2,18},{10... | collective-permute-start | bytes 393224 | tf_op jit(solution)/shard_map/ppermute | solution.py:242
  73.3 5.2 %collective-permute-done.8 = f32[32,1024]{1,0:T(8,128)S(1)} collective-permute-done((f32[32,1024]{1,0:T(8,128)S(1)}, f32[32,1024]{1,0:T(8,128)S(1)}, u32[]{:S(2)}, u32[]{:S(2)}) %collective-permute-start.8) | collective-permute-done | bytes 131104 | tf_op jit(solution)/shard_map/ppermute | solution.py:242
  78.5 3.3 %collective-permute-start.11 = (f32[32,1024]{1,0:T(8,128)S(1)}, f32[32,1024]{1,0:T(8,128)S(1)}, u32[]{:S(2)}, u32[]{:S(2)}) collective-permute-start(f32[32,1024]{1,0:T(8,128)S(1)} %add.62), channel_id=1, source_target_pairs={{0,6},{1,7},{2,4},{3,5},{4,2},{5,3},{6,0},{7,1},{8,14},{9,15},{10,... | collective-permute-start | bytes 393224 | tf_op jit(solution)/shard_map/ppermute | solution.py:255
  82.5 3.2 %collective-permute-done.11 = f32[32,1024]{1,0:T(8,128)S(1)} collective-permute-done((f32[32,1024]{1,0:T(8,128)S(1)}, f32[32,1024]{1,0:T(8,128)S(1)}, u32[]{:S(2)}, u32[]{:S(2)}) %collective-permute-start.11) | collective-permute-done | bytes 131104 | tf_op jit(solution)/shard_map/ppermute | solution.py:255
  85.7 2.4 %collective-permute-done.10 = f32[32,1024]{1,0:T(8,128)S(1)} collective-permute-done((f32[32,1024]{1,0:T(8,128)S(1)}, f32[32,1024]{1,0:T(8,128)S(1)}, u32[]{:S(2)}, u32[]{:S(2)}) %collective-permute-start.10) | collective-permute-done | bytes 131104 | tf_op jit(solution)/shard_map/ppermute | solution.py:255
  90.5 3.9 %shard_map.37 = (f32[128,1024]{1,0:T(8,128)S(1)}, f32[128,1024]{1,0:T(8,128)S(1)}) custom-call(f32[128,1024]{1,0:T(8,128)S(1)} %pad_maximum_fusion.refs_0_, f32[128,1024]{1,0:T(8,128)S(1)} %collective-permute-done.12.refs_1_, f32[256,512]{1,0:T(8,128)S(1)} %get-tuple-element.16.refs_0_.refs_2_, f32[256,512]{1,0:T(8,128)S(1)} %collective-permute-done.refs_1_.refs_3_, ...), custom_call_target="tpu_custom_call" | custom-call | tf_op jit(solution)/shard_map/pallas_call | solution.py:229
  99.9 3.8 %collective-permute-done.14 = f32[32,1024]{1,0:T(8,128)S(1)} collective-permute-done((f32[32,1024]{1,0:T(8,128)S(1)}, f32[32,1024]{1,0:T(8,128)S(1)}, u32[]{:S(2)}, u32[]{:S(2)}) %collective-permute-start.14) | collective-permute-done | bytes 131104 | tf_op jit(solution)/shard_map/ppermute | solution.py:255
  105.8 5.1 %collective-permute-done.17 = f32[32,1024]{1,0:T(8,128)S(1)} collective-permute-done((f32[32,1024]{1,0:T(8,128)S(1)}, f32[32,1024]{1,0:T(8,128)S(1)}, u32[]{:S(2)}, u32[]{:S(2)}) %collective-permute-start.17) | collective-permute-done | bytes 131104 | tf_op jit(solution)/shard_map/ppermute | solution.py:242
  111.6 7.2 %collective-permute-done.18 = f32[32,1024]{1,0:T(8,128)S(1)} collective-permute-done((f32[32,1024]{1,0:T(8,128)S(1)}, f32[32,1024]{1,0:T(8,128)S(1)}, u32[]{:S(2)}, u32[]{:S(2)}) %collective-permute-start.18) | collective-permute-done | bytes 131104 | tf_op jit(solution)/shard_map/ppermute | solution.py:242
  122.6 2.9 %collective-permute-done.21 = f32[32,1024]{1,0:T(8,128)S(1)} collective-permute-done((f32[32,1024]{1,0:T(8,128)S(1)}, f32[32,1024]{1,0:T(8,128)S(1)}, u32[]{:S(2)}, u32[]{:S(2)}) %collective-permute-start.21) | collective-permute-done | bytes 131104 | tf_op jit(solution)/shard_map/ppermute | solution.py:255
  130.0 2.6 %shard_map.33.work_ref = f32[256,512]{1,0:T(8,128)S(1)} custom-call(f32[256,512]{1,0:T(8,128)S(1)} %shard_map.32.work_ref), custom_call_target="tpu_custom_call" | custom-call | tf_op jit(solution)/shard_map/pallas_call | solution.py:229
  132.6 2.4 %shard_map.34.work_ref = f32[256,512]{1,0:T(8,128)S(1)} custom-call(f32[256,512]{1,0:T(8,128)S(1)} %shard_map.33.work_ref), custom_call_target="tpu_custom_call" | custom-call | tf_op jit(solution)/shard_map/pallas_call | solution.py:229
  139.1 13.2 %shard_map.38 = (f32[64,512]{1,0:T(8,128)S(1)}, f32[64,512]{1,0:T(8,128)S(1)}, f32[64,512]{1,0:T(8,128)S(1)}, f32[64,512]{1,0:T(8,128)S(1)}) custom-call(f32[256,512]{1,0:T(8,128)S(1)} %shard_map.36.work_ref, f32[128,1024]{1,0:T(8,128)S(1)} %pad_maximum_fusion.1.refs_0_, f32[128,1024]{1,0:T(8,128)S(1)} %collective-permute-done.22.refs_1_, ...), custom_call_target="tpu_custom_call" | custom-call | tf_op jit(solution)/shard_map/pallas_call | solution.py:229
  152.4 2.5 %collective-permute-start.24 = (f32[64,512]{1,0:T(8,128)S(1)}, f32[64,512]{1,0:T(8,128)S(1)}, u32[]{:S(2)}, u32[]{:S(2)}) collective-permute-start(f32[64,512]{1,0:T(8,128)S(1)} %get-tuple-element.25), channel_id=1, source_target_pairs={{0,16},{8,24},{16,0},{24,8},{1,17},{9,25},{17,1},{25,9},{2,18},{10... | collective-permute-start | bytes 393224 | tf_op jit(solution)/shard_map/ppermute | solution.py:242
  156.8 3.6 %collective-permute-done.23.refs_1_ = f32[64,512]{1,0:T(8,128)S(1)} collective-permute-done((f32[64,512]{1,0:T(8,128)S(1)}, f32[64,512]{1,0:T(8,128)S(1)}, u32[]{:S(2)}, u32[]{:S(2)}) %collective-permute-start.23) | collective-permute-done | bytes 131104 | tf_op jit(solution)/shard_map/ppermute | solution.py:242
  160.4 5.1 %collective-permute-done.24.refs_2_ = f32[64,512]{1,0:T(8,128)S(1)} collective-permute-done((f32[64,512]{1,0:T(8,128)S(1)}, f32[64,512]{1,0:T(8,128)S(1)}, u32[]{:S(2)}, u32[]{:S(2)}) %collective-permute-start.24) | collective-permute-done | bytes 131104 | tf_op jit(solution)/shard_map/ppermute | solution.py:242
  (54 shorter events, 37.8 us)
Async XLA Ops:
  1.8 29.1 %collective-permute-start.1 = (f32[256,512]{1,0:T(8,128)S(1)}, f32[256,512]{1,0:T(8,128)S(1)}, u32[]{:S(2)}, u32[]{:S(2)}) collective-permute-start(f32[256,512]{1,0:T(8,128)S(1)} %shard_map.29), channel_id=1, source_target_pairs={{0,16},{8,24},{16,0},{24,8},{1,17},{9,25},{17,1},{25,9},{2,18},{10... | collective-permute-start | bytes 1572872 | tf_op jit(solution)/shard_map/ppermute | solution.py:242
  6.6 24.5 %collective-permute-start = (f32[256,512]{1,0:T(8,128)S(1)}, f32[256,512]{1,0:T(8,128)S(1)}, u32[]{:S(2)}, u32[]{:S(2)}) collective-permute-start(f32[256,512]{1,0:T(8,128)S(1)} %get-tuple-element.17), channel_id=1, source_target_pairs={{0,8},{8,0},{16,24},{24,16},{1,9},{9,1},{17,25},{25,17},{2,10},{10... | collective-permute-start | bytes 1572872 | tf_op jit(solution)/shard_map/ppermute | solution.py:242
  8.3 33.3 %collective-permute-start.2 = (f32[256,512]{1,0:T(8,128)S(1)}, f32[256,512]{1,0:T(8,128)S(1)}, u32[]{:S(2)}, u32[]{:S(2)}) collective-permute-start(f32[256,512]{1,0:T(8,128)S(1)} %get-tuple-element.18), channel_id=1, source_target_pairs={{0,24},{8,16},{16,8},{24,0},{1,25},{9,17},{17,9},{25,1},{2,26},{10... | collective-permute-start | bytes 1572872 | tf_op jit(solution)/shard_map/ppermute | solution.py:242
  44.1 2.0 %collective-permute-start.3 = (f32[128,1024]{1,0:T(8,128)S(1)}, f32[128,1024]{1,0:T(8,128)S(1)}, u32[]{:S(2)}, u32[]{:S(2)}) collective-permute-start(f32[128,1024]{1,0:T(8,128)S(1)} %get-tuple-element.20), channel_id=1, source_target_pairs={{0,1},{1,0},{2,3},{3,2},{4,5},{5,4},{6,7},{7,6},{8,9},{9,8},{10,11... | collective-permute-start | bytes 1572872 | tf_op jit(solution)/shard_map/ppermute | solution.py:242
  46.1 7.3 %collective-permute-start.4 = (f32[32,1024]{1,0:T(8,128)S(1)}, f32[32,1024]{1,0:T(8,128)S(1)}, u32[]{:S(2)}, u32[]{:S(2)}) collective-permute-start(f32[32,1024]{1,0:T(8,128)S(1)} %get-tuple-element.30), channel_id=1, source_target_pairs={{0,6},{1,7},{2,4},{3,5},{4,2},{5,3},{6,0},{7,1},{8,14},{9,15},{10,... | collective-permute-start | bytes 393224 | tf_op jit(solution)/shard_map/ppermute | solution.py:255
  48.6 6.9 %collective-permute-start.6 = (f32[32,1024]{1,0:T(8,128)S(1)}, f32[32,1024]{1,0:T(8,128)S(1)}, u32[]{:S(2)}, u32[]{:S(2)}) collective-permute-start(f32[32,1024]{1,0:T(8,128)S(1)} %get-tuple-element.31), channel_id=1, source_target_pairs={{0,2},{1,3},{2,0},{3,1},{4,6},{5,7},{6,4},{7,5},{8,10},{9,11},{10,... | collective-permute-start | bytes 393224 | tf_op jit(solution)/shard_map/ppermute | solution.py:255
  49.1 6.3 %collective-permute-start.5 = (f32[32,1024]{1,0:T(8,128)S(1)}, f32[32,1024]{1,0:T(8,128)S(1)}, u32[]{:S(2)}, u32[]{:S(2)}) collective-permute-start(f32[32,1024]{1,0:T(8,128)S(1)} %get-tuple-element.32), channel_id=1, source_target_pairs={{0,4},{1,5},{2,6},{3,7},{4,0},{5,1},{6,2},{7,3},{8,12},{9,13},{10,... | collective-permute-start | bytes 393224 | tf_op jit(solution)/shard_map/ppermute | solution.py:255
  55.5 14.1 %collective-permute-start.7 = (f32[32,1024]{1,0:T(8,128)S(1)}, f32[32,1024]{1,0:T(8,128)S(1)}, u32[]{:S(2)}, u32[]{:S(2)}) collective-permute-start(f32[32,1024]{1,0:T(8,128)S(1)} %fusion.5), channel_id=1, source_target_pairs={{0,8},{8,0},{16,24},{24,16},{1,9},{9,1},{17,25},{25,17},{2,10},{10... | collective-permute-start | bytes 393224 | tf_op jit(solution)/shard_map/ppermute | solution.py:242
  69.6 8.9 %collective-permute-start.8 = (f32[32,1024]{1,0:T(8,128)S(1)}, f32[32,1024]{1,0:T(8,128)S(1)}, u32[]{:S(2)}, u32[]{:S(2)}) collective-permute-start(f32[32,1024]{1,0:T(8,128)S(1)} %add.61), channel_id=1, source_target_pairs={{0,16},{8,24},{16,0},{24,8},{1,17},{9,25},{17,1},{25,9},{2,18},{10... | collective-permute-start | bytes 393224 | tf_op jit(solution)/shard_map/ppermute | solution.py:242
  78.5 7.2 %collective-permute-start.11 = (f32[32,1024]{1,0:T(8,128)S(1)}, f32[32,1024]{1,0:T(8,128)S(1)}, u32[]{:S(2)}, u32[]{:S(2)}) collective-permute-start(f32[32,1024]{1,0:T(8,128)S(1)} %add.62), channel_id=1, source_target_pairs={{0,6},{1,7},{2,4},{3,5},{4,2},{5,3},{6,0},{7,1},{8,14},{9,15},{10,... | collective-permute-start | bytes 393224 | tf_op jit(solution)/shard_map/ppermute | solution.py:255
  81.8 6.3 %collective-permute-start.10 = (f32[32,1024]{1,0:T(8,128)S(1)}, f32[32,1024]{1,0:T(8,128)S(1)}, u32[]{:S(2)}, u32[]{:S(2)}) collective-permute-start(f32[32,1024]{1,0:T(8,128)S(1)} %add.62), channel_id=1, source_target_pairs={{0,4},{1,5},{2,6},{3,7},{4,0},{5,1},{6,2},{7,3},{8,12},{9,13},{10,... | collective-permute-start | bytes 393224 | tf_op jit(solution)/shard_map/ppermute | solution.py:255
  81.9 6.6 %collective-permute-start.9 = (f32[32,1024]{1,0:T(8,128)S(1)}, f32[32,1024]{1,0:T(8,128)S(1)}, u32[]{:S(2)}, u32[]{:S(2)}) collective-permute-start(f32[32,1024]{1,0:T(8,128)S(1)} %add.62), channel_id=1, source_target_pairs={{0,2},{1,3},{2,0},{3,1},{4,6},{5,7},{6,4},{7,5},{8,10},{9,11},{10,... | collective-permute-start | bytes 393224 | tf_op jit(solution)/shard_map/ppermute | solution.py:255
  96.4 7.3 %collective-permute-start.14 = (f32[32,1024]{1,0:T(8,128)S(1)}, f32[32,1024]{1,0:T(8,128)S(1)}, u32[]{:S(2)}, u32[]{:S(2)}) collective-permute-start(f32[32,1024]{1,0:T(8,128)S(1)} %get-tuple-element.27), channel_id=1, source_target_pairs={{0,6},{1,7},{2,4},{3,5},{4,2},{5,3},{6,0},{7,1},{8,14},{9,15},{10,... | collective-permute-start | bytes 393224 | tf_op jit(solution)/shard_map/ppermute | solution.py:255
  98.0 7.7 %collective-permute-start.16 = (f32[32,1024]{1,0:T(8,128)S(1)}, f32[32,1024]{1,0:T(8,128)S(1)}, u32[]{:S(2)}, u32[]{:S(2)}) collective-permute-start(f32[32,1024]{1,0:T(8,128)S(1)} %get-tuple-element.28), channel_id=1, source_target_pairs={{0,2},{1,3},{2,0},{3,1},{4,6},{5,7},{6,4},{7,5},{8,10},{9,11},{10,... | collective-permute-start | bytes 393224 | tf_op jit(solution)/shard_map/ppermute | solution.py:255
  99.3 6.3 %collective-permute-start.15 = (f32[32,1024]{1,0:T(8,128)S(1)}, f32[32,1024]{1,0:T(8,128)S(1)}, u32[]{:S(2)}, u32[]{:S(2)}) collective-permute-start(f32[32,1024]{1,0:T(8,128)S(1)} %get-tuple-element.29), channel_id=1, source_target_pairs={{0,4},{1,5},{2,6},{3,7},{4,0},{5,1},{6,2},{7,3},{8,12},{9,13},{10,... | collective-permute-start | bytes 393224 | tf_op jit(solution)/shard_map/ppermute | solution.py:255
  105.7 5.1 %collective-permute-start.17 = (f32[32,1024]{1,0:T(8,128)S(1)}, f32[32,1024]{1,0:T(8,128)S(1)}, u32[]{:S(2)}, u32[]{:S(2)}) collective-permute-start(f32[32,1024]{1,0:T(8,128)S(1)} %fusion.2), channel_id=1, source_target_pairs={{0,8},{8,0},{16,24},{24,16},{1,9},{9,1},{17,25},{25,17},{2,10},{10... | collective-permute-start | bytes 393224 | tf_op jit(solution)/shard_map/ppermute | solution.py:242
  110.9 8.0 %collective-permute-start.18 = (f32[32,1024]{1,0:T(8,128)S(1)}, f32[32,1024]{1,0:T(8,128)S(1)}, u32[]{:S(2)}, u32[]{:S(2)}) collective-permute-start(f32[32,1024]{1,0:T(8,128)S(1)} %add.70), channel_id=1, source_target_pairs={{0,16},{8,24},{16,0},{24,8},{1,17},{9,25},{17,1},{25,9},{2,18},{10... | collective-permute-start | bytes 393224 | tf_op jit(solution)/shard_map/ppermute | solution.py:242
  118.9 6.6 %collective-permute-start.21 = (f32[32,1024]{1,0:T(8,128)S(1)}, f32[32,1024]{1,0:T(8,128)S(1)}, u32[]{:S(2)}, u32[]{:S(2)}) collective-permute-start(f32[32,1024]{1,0:T(8,128)S(1)} %add.71), channel_id=1, source_target_pairs={{0,6},{1,7},{2,4},{3,5},{4,2},{5,3},{6,0},{7,1},{8,14},{9,15},{10,... | collective-permute-start | bytes 393224 | tf_op jit(solution)/shard_map/ppermute | solution.py:255
  120.5 7.2 %collective-permute-start.20 = (f32[32,1024]{1,0:T(8,128)S(1)}, f32[32,1024]{1,0:T(8,128)S(1)}, u32[]{:S(2)}, u32[]{:S(2)}) collective-permute-start(f32[32,1024]{1,0:T(8,128)S(1)} %add.71), channel_id=1, source_target_pairs={{0,4},{1,5},{2,6},{3,7},{4,0},{5,1},{6,2},{7,3},{8,12},{9,13},{10,... | collective-permute-start | bytes 393224 | tf_op jit(solution)/shard_map/ppermute | solution.py:255
  122.6 6.1 %collective-permute-start.19 = (f32[32,1024]{1,0:T(8,128)S(1)}, f32[32,1024]{1,0:T(8,128)S(1)}, u32[]{:S(2)}, u32[]{:S(2)}) collective-permute-start(f32[32,1024]{1,0:T(8,128)S(1)} %add.71), channel_id=1, source_target_pairs={{0,2},{1,3},{2,0},{3,1},{4,6},{5,7},{6,4},{7,5},{8,10},{9,11},{10,... | collective-permute-start | bytes 393224 | tf_op jit(solution)/shard_map/ppermute | solution.py:255
  128.8 10.4 %collective-permute-start.22 = (f32[128,1024]{1,0:T(8,128)S(1)}, f32[128,1024]{1,0:T(8,128)S(1)}, u32[]{:S(2)}, u32[]{:S(2)}) collective-permute-start(f32[128,1024]{1,0:T(8,128)S(1)} %pad_maximum_fusion.1.refs_0_), channel_id=1, source_target_pairs={{0,1},{1,0},{2,3},{3,2},{4,5},{5,4},{6,7},{7,6},{8,9},{9,8},{10,11... | collective-permute-start | bytes 1572872 | tf_op jit(solution)/shard_map/ppermute | solution.py:242
  152.3 8.0 %collective-permute-start.23 = (f32[64,512]{1,0:T(8,128)S(1)}, f32[64,512]{1,0:T(8,128)S(1)}, u32[]{:S(2)}, u32[]{:S(2)}) collective-permute-start(f32[64,512]{1,0:T(8,128)S(1)} %get-tuple-element.24), channel_id=1, source_target_pairs={{0,8},{8,0},{16,24},{24,16},{1,9},{9,1},{17,25},{25,17},{2,10},{10... | collective-permute-start | bytes 393224 | tf_op jit(solution)/shard_map/ppermute | solution.py:242
  152.4 13.0 %collective-permute-start.24 = (f32[64,512]{1,0:T(8,128)S(1)}, f32[64,512]{1,0:T(8,128)S(1)}, u32[]{:S(2)}, u32[]{:S(2)}) collective-permute-start(f32[64,512]{1,0:T(8,128)S(1)} %get-tuple-element.25), channel_id=1, source_target_pairs={{0,16},{8,24},{16,0},{24,8},{1,17},{9,25},{17,1},{25,9},{2,18},{10... | collective-permute-start | bytes 393224 | tf_op jit(solution)/shard_map/ppermute | solution.py:242
  154.9 10.5 %collective-permute-start.25 = (f32[64,512]{1,0:T(8,128)S(1)}, f32[64,512]{1,0:T(8,128)S(1)}, u32[]{:S(2)}, u32[]{:S(2)}) collective-permute-start(f32[64,512]{1,0:T(8,128)S(1)} %get-tuple-element.26), channel_id=1, source_target_pairs={{0,24},{8,16},{16,8},{24,0},{1,25},{9,17},{17,9},{25,1},{2,26},{10... | collective-permute-start | bytes 393224 | tf_op jit(solution)/shard_map/ppermute | solution.py:242
  (4 other events, 35.1 us)

commit v2 on v1

--- a/solution.py
+++ b/solution.py
@@ -9,6 +9,7 @@
 
 
 SUB, LANES = 8, 128
+PARTS = 8
 HALF = LANES // 2
 VMEM_BYTES = 20 * 2**20
 LIFT = 2.0**20
@@ -151,11 +152,11 @@
     spread_out(inner, blocks, outs, stages, matrix)
 
 
-def second_kernel(count, inputs, stages, *refs):
+def second_kernel(count, inputs, arrived, stages, *refs):
     parts, blocks = refs[:inputs], refs[inputs : inputs + count]
     outs, matrix = refs[inputs + count : -1], refs[-1]
     rows = blocks[0].shape[0]
-    gather_rows(parts, stages, matrix)
+    gather_rows(parts, arrived, matrix)
     inner = None
     for d, block in enumerate(blocks):
         term = mm(matrix[:, lanes(d, rows)], block[...], 1, 0)
@@ -203,14 +204,36 @@
         out[...] = held[place, :]
 
 
-def pick_kernel(distances, fibres, slab_ref, *outs):
-    rows, width = outs[0].shape
-    share = width // LANES
-    for d, out in zip(distances, outs):
-        target = lax.axis_index("mode") ^ d
-        for j in range(share):
-            start = target * share + j
-            out[:, j * LANES : (j + 1) * LANES] = slab_ref[pl.ds(start, rows, stride=fibres), :]
+def pick_kernel(distances, fibres, slab_ref, *refs):
+    *outs, slab, sems = refs
+    parts = sems.shape[0]
+    height, rows = slab.shape[0] // parts, outs[0].shape[0] // parts
+    share = outs[0].shape[1] // LANES
+    copies = []
+    for part in range(parts):
+        place = pl.ds(part * height, height)
+        copies.append(pltpu.make_async_copy(slab_ref.at[place, :], slab.at[place, :], sems.at[part]))
+        copies[-1].start()
+    for part, copy in enumerate(copies):
+        copy.wait()
+        for d, out in zip(distances, outs):
+            target = lax.axis_index("mode") ^ d
+            for j in range(share):
+                start = part * height + target * share + j
+                out[part * rows : (part + 1) * rows, j * LANES : (j + 1) * LANES] = slab[
+                    pl.ds(start, rows, stride=fibres), :
+                ]
+
+
+def pick(distances, fibres, out_shape, slab):
+    return pl.pallas_call(
+        functools.partial(pick_kernel, distances, fibres),
+        out_shape=[jax.ShapeDtypeStruct(out_shape, jnp.float32)] * len(distances),
+        in_specs=[pl.BlockSpec(memory_space=pltpu.HBM)],
+        out_specs=[pl.BlockSpec(memory_space=pltpu.VMEM)] * len(distances),
+        scratch_shapes=[pltpu.VMEM(slab.shape, jnp.float32), pltpu.SemaphoreType.DMA((PARTS,))],
+        compiler_params=pltpu.CompilerParams(vmem_limit_bytes=VMEM_BYTES),
+    )(slab)
 
 
 def join_kernel(fibres, *refs):
@@ -247,12 +270,13 @@
 
 
 def plane_exchange(block, stages, d):
-    inner = lax.axis_size("rb")
+    axes = ("mode", "ra", "rb")
+    sizes = [lax.axis_size(axis) for axis in axes]
+    strides = {"mode": sizes[1] * sizes[2], "ra": sizes[2], "rb": 1}
     flip = 0
     for index, (axis, bit) in enumerate(stages[1:]):
-        flip |= (d >> index & 1) * (bit if axis == "rb" else bit * inner)
-    size = inner * lax.axis_size("ra")
-    return lax.ppermute(block, ("ra", "rb"), [(k, k ^ flip) for k in range(size)])
+        flip |= (d >> index & 1) * bit * strides[axis]
+    return lax.ppermute(block, axes, [(k, k ^ flip) for k in range(sizes[0] * sizes[1] * sizes[2])])
 
 
 def all_reduce(kept, sent, stages):
@@ -273,6 +297,8 @@
     for part in arrived:
         held = held + part
     for bit in bits_of("mode"):
+        if ("mode", bit) in stages:
+            continue
         held = held + exchange(held, "mode", bit)
     whole = {0: held}
     for d in far_first:
@@ -296,20 +322,19 @@
     rows, nj, nk = density_slab.shape
     width, rank = start_basis.shape
     stages = [(axis, bit) for axis in ("rb", "ra") for bit in bits_of(axis)]
+    wider = stages + [("mode", 1)]
+    if rank >> len(wider) < SUB:
+        wider = stages
 
     share = nj // count
-    slab = density_slab.reshape(rows * nj, nk)
+    slab = pltpu.with_memory_space_constraint(density_slab.reshape(rows * nj, nk), pltpu.HBM)
     far_first = sorted(range(1, count), key=lambda d: (d < count // 2, d))
     blocks = [None] * count
+    picked = []
     for distances in (far_first[:1], far_first[1:] + [0]):
-        picked = call(
-            functools.partial(pick_kernel, distances, nj),
-            [(rows, share * nk)] * len(distances),
-            [],
-            slab,
-        )
-        for d, piece in zip(distances, picked):
-            blocks[d] = exchange(piece, "mode", d) if d else piece
+        picked += pick(distances, nj, (rows, share * nk), slab)
+    for d, piece in zip(far_first + [0], picked):
+        blocks[d] = exchange(piece, "mode", d) if d else piece
 
     def turn(matrix):
         if rows % LANES == 0:
@@ -317,7 +342,7 @@
         split = matrix.reshape(-1, count, rows).transpose(1, 0, 2)
         return turned(split, count, here).transpose(1, 0, 2).reshape(-1, width)
 
-    def total(partials):
+    def total(partials, stages):
         kept, sent = partials
         return all_reduce(turn(kept), turn(sent), stages)
 
@@ -328,25 +353,27 @@
     (early,) = call(early_kernel, [inner_shape], [], start_basis, *blocks[:-1])
     applied = total(
         call(
-            functools.partial(first_kernel, count, stages),
+            functools.partial(first_kernel, count, wider),
             half,
             [tall],
             start_basis,
             early,
             *blocks,
         ),
+        wider,
     )
     turned_in = [turn(part) for part in applied]
     again = total(
         call(
-            functools.partial(second_kernel, count, len(applied), stages),
+            functools.partial(second_kernel, count, len(applied), wider, stages),
             half,
             [tall],
             *turned_in,
             *blocks,
         ),
-    )
-    (factor,) = call(functools.partial(inner_kernel, stages), [work], [tall], *applied)
+        stages,
+    )
+    (factor,) = call(functools.partial(inner_kernel, wider), [work], [tall], *applied)
     for top in range(0, rank, HALF):
         (factor,) = call(functools.partial(step_kernel, top), [work], [(SUB, LANES)], factor)
     outward = call(

time: 167 us -> 170 us (1.018)
  starting transfers between devices: 40.8 us -> 47.4 us
  waiting for transfers between devices: 90.4 us -> 86.7 us
  Pallas kernels: 33.2 us -> 35.7 us
    ppermute x12 -> x20, starting transfers between devices: 14.8 us -> 32.2 us  [plane_exchange(): lax.ppermute(block, axes, [(k, k ^ flip) for k in range(sizes[0] * sizes[...]
    ppermute x14 -> x13, starting transfers between devices: 26 us -> 15.2 us  [exchange(): return lax.ppermute(block, axis, [(k, k ^ bit) for k in range(size)])]
    ppermute x14 -> x13, waiting for transfers between devices: 66.7 us -> 62.8 us  [exchange(): return lax.ppermute(block, axis, [(k, k ^ bit) for k in range(size)])]
    pallas_call x0 -> x2, Pallas kernels: none -> 3.31 us  [pick(): pl.pallas_call(functools.partial(pick_kernel, distances, fibres), out_sha...]
    pallas_call x12 -> x10, Pallas kernels: 33.2 us -> 32.4 us  [call(): pl.pallas_call(kernel, out_shape=[jax.ShapeDtypeStruct(shape, jnp.float32...]
    ppermute x12 -> x20, waiting for transfers between devices: 23.6 us -> 23.9 us  [plane_exchange(): lax.ppermute(block, axes, [(k, k ^ flip) for k in range(sizes[0] * sizes[...]
  transfers between devices with their start and end apart: 26 -> 33, of which waited for: 22 -> 21; matrix products, arithmetic and copies ran while one was open for 0% -> 0% of each run, Pallas kernels for 7% -> 8%
where the time goes in v2:
time: 170 us
  waiting for transfers between devices  86.7 us (51%)
  starting transfers between devices  47.4 us (28%)
  Pallas kernels  35.7 us (21%)
    ppermute x13, waiting for transfers between devices, exchange(): return lax.ppermute(block, axis, [(k, k ^ bit) for k in range(size)])  62.8 us
    pallas_call x10, Pallas kernels, call(): pl.pallas_call(kernel, out_shape=[jax.ShapeDtypeStruct(shape, jnp.float32...  32.4 us
    ppermute x20, starting transfers between devices, plane_exchange(): lax.ppermute(block, axes, [(k, k ^ flip) for k in range(sizes[0] * sizes[...  32.2 us
    ppermute x20, waiting for transfers between devices, plane_exchange(): lax.ppermute(block, axes, [(k, k ^ flip) for k in range(sizes[0] * sizes[...  23.9 us
    ppermute x13, starting transfers between devices, exchange(): return lax.ppermute(block, axis, [(k, k ^ bit) for k in range(size)])  15.2 us
  transfers between devices with their start and end apart: 33, of which 21 were waited for; matrix products, arithmetic and copies ran while one was open for 0% of the time, Pallas kernels for 8%

profile of v2, /device:TPU:0, one launch (start us, length us, event | category | flops | bytes accessed | tf_op | source)
XLA Modules:
  0.0 170.3 jit_solution(5633990862076653099)
XLA Ops:
  1.7 4.1 %collective-permute-start.1 = (f32[256,512]{1,0:T(8,128)S(1)}, f32[256,512]{1,0:T(8,128)S(1)}, u32[]{:S(2)}, u32[]{:S(2)}) collective-permute-start(f32[256,512]{1,0:T(8,128)S(1)} %shard_map.29), channel_id=1, source_target_pairs={{0,16},{8,24},{16,0},{24,8},{1,17},{9,25},{17,1},{25,9},{2,18},{10... | collective-permute-start | bytes 1572872 | tf_op jit(solution)/shard_map/ppermute | solution.py:265
  9.1 21.6 %collective-permute-done.1.refs_2_.refs_4_ = f32[256,512]{1,0:T(8,128)S(1)} collective-permute-done((f32[256,512]{1,0:T(8,128)S(1)}, f32[256,512]{1,0:T(8,128)S(1)}, u32[]{:S(2)}, u32[]{:S(2)}) %collective-permute-start.1) | collective-permute-done | bytes 524320 | tf_op jit(solution)/shard_map/ppermute | solution.py:265
  30.7 11.5 %collective-permute-done.refs_1_.refs_3_ = f32[256,512]{1,0:T(8,128)S(1)} collective-permute-done((f32[256,512]{1,0:T(8,128)S(1)}, f32[256,512]{1,0:T(8,128)S(1)}, u32[]{:S(2)}, u32[]{:S(2)}) %collective-permute-start) | collective-permute-done | bytes 524320 | tf_op jit(solution)/shard_map/ppermute | solution.py:265
  43.7 2.5 %shard_map.31 = (f32[128,1024]{1,0:T(8,128)S(1)}, f32[128,1024]{1,0:T(8,128)S(1)}) custom-call(f32[1024,256]{1,0:T(8,128)S(1)} %copy-done, f32[256,512]{1,0:T(8,128)S(1)} %shard_map.30.early_ref, f32[256,512]{1,0:T(8,128)S(1)} %get-tuple-element.16.refs_0_.refs_2_, f32[256,512]{1,0:T(8,128)S(1)} %collective-permute-done.refs_1_.refs_3_, ...), custom_call_target="tpu_custom_call" | custom-call | tf_op jit(solution)/shard_map/pallas_call | solution.py:252
  48.3 10.4 %collective-permute-start.4 = (f32[16,1024]{1,0:T(8,128)S(1)}, f32[16,1024]{1,0:T(8,128)S(1)}, u32[]{:S(2)}, u32[]{:S(2)}) collective-permute-start(f32[16,1024]{1,0:T(8,128)S(1)} %get-tuple-element.32), channel_id=1, source_target_pairs={{0,14},{1,15},{2,12},{3,13},{4,10},{5,11},{6,8},{7,9},{8,6},{9,7},... | collective-permute-start | bytes 196616 | tf_op jit(solution)/shard_map/ppermute | solution.py:279
  59.8 2.4 %collective-permute-start.8 = (f32[16,1024]{1,0:T(8,128)S(1)}, f32[16,1024]{1,0:T(8,128)S(1)}, u32[]{:S(2)}, u32[]{:S(2)}) collective-permute-start(f32[16,1024]{1,0:T(8,128)S(1)} %get-tuple-element.35), channel_id=1, source_target_pairs={{0,6},{1,7},{2,4},{3,5},{4,2},{5,3},{6,0},{7,1},{8,14},{9,15},{10,... | collective-permute-start | bytes 196616 | tf_op jit(solution)/shard_map/ppermute | solution.py:279
  62.2 2.0 %collective-permute-start.6 = (f32[16,1024]{1,0:T(8,128)S(1)}, f32[16,1024]{1,0:T(8,128)S(1)}, u32[]{:S(2)}, u32[]{:S(2)}) collective-permute-start(f32[16,1024]{1,0:T(8,128)S(1)} %get-tuple-element.37), channel_id=1, source_target_pairs={{0,10},{1,11},{2,8},{3,9},{4,14},{5,15},{6,12},{7,13},{8,2},{9,3},... | collective-permute-start | bytes 196616 | tf_op jit(solution)/shard_map/ppermute | solution.py:279
  69.4 2.4 %collective-permute-start.11 = (f32[16,1024]{1,0:T(8,128)S(1)}, f32[16,1024]{1,0:T(8,128)S(1)}, u32[]{:S(2)}, u32[]{:S(2)}) collective-permute-start(f32[16,1024]{1,0:T(8,128)S(1)} %fusion.9), channel_id=1, source_target_pairs={{0,16},{8,24},{16,0},{24,8},{1,17},{9,25},{17,1},{25,9},{2,18},{10... | collective-permute-start | bytes 196616 | tf_op jit(solution)/shard_map/ppermute | solution.py:265
  71.9 3.5 %collective-permute-done.11 = f32[16,1024]{1,0:T(8,128)S(1)} collective-permute-done((f32[16,1024]{1,0:T(8,128)S(1)}, f32[16,1024]{1,0:T(8,128)S(1)}, u32[]{:S(2)}, u32[]{:S(2)}) %collective-permute-start.11) | collective-permute-done | bytes 65568 | tf_op jit(solution)/shard_map/ppermute | solution.py:265
  83.3 3.8 %collective-permute-done.13 = f32[16,1024]{1,0:T(8,128)S(1)} collective-permute-done((f32[16,1024]{1,0:T(8,128)S(1)}, f32[16,1024]{1,0:T(8,128)S(1)}, u32[]{:S(2)}, u32[]{:S(2)}) %collective-permute-start.13) | collective-permute-done | bytes 65568 | tf_op jit(solution)/shard_map/ppermute | solution.py:279
  88.2 4.0 %collective-permute-done.14 = f32[16,1024]{1,0:T(8,128)S(1)} collective-permute-done((f32[16,1024]{1,0:T(8,128)S(1)}, f32[16,1024]{1,0:T(8,128)S(1)}, u32[]{:S(2)}, u32[]{:S(2)}) %collective-permute-start.14) | collective-permute-done | bytes 65568 | tf_op jit(solution)/shard_map/ppermute | solution.py:279
  94.3 3.8 %shard_map.37 = (f32[128,1024]{1,0:T(8,128)S(1)}, f32[128,1024]{1,0:T(8,128)S(1)}) custom-call(f32[128,1024]{1,0:T(8,128)S(1)} %constant_dynamic-update-slice_fusion.refs_0_, f32[128,1024]{1,0:T(8,128)S(1)} %collective-permute-done.19.refs_1_, f32[256,512]{1,0:T(8,128)S(1)} %get-tuple-element.16.refs_0_.refs_2_, ...), custom_call_target="tpu_custom_call" | custom-call | tf_op jit(solution)/shard_map/pallas_call | solution.py:252
  103.7 3.8 %collective-permute-done.21 = f32[32,1024]{1,0:T(8,128)S(1)} collective-permute-done((f32[32,1024]{1,0:T(8,128)S(1)}, f32[32,1024]{1,0:T(8,128)S(1)}, u32[]{:S(2)}, u32[]{:S(2)}) %collective-permute-start.21) | collective-permute-done | bytes 131104 | tf_op jit(solution)/shard_map/ppermute | solution.py:279
  110.0 5.0 %collective-permute-done.24 = f32[32,1024]{1,0:T(8,128)S(1)} collective-permute-done((f32[32,1024]{1,0:T(8,128)S(1)}, f32[32,1024]{1,0:T(8,128)S(1)}, u32[]{:S(2)}, u32[]{:S(2)}) %collective-permute-start.24) | collective-permute-done | bytes 131104 | tf_op jit(solution)/shard_map/ppermute | solution.py:265
  116.6 6.7 %collective-permute-done.25 = f32[32,1024]{1,0:T(8,128)S(1)} collective-permute-done((f32[32,1024]{1,0:T(8,128)S(1)}, f32[32,1024]{1,0:T(8,128)S(1)}, u32[]{:S(2)}, u32[]{:S(2)}) %collective-permute-start.25) | collective-permute-done | bytes 131104 | tf_op jit(solution)/shard_map/ppermute | solution.py:265
  126.8 3.8 %collective-permute-done.28 = f32[32,1024]{1,0:T(8,128)S(1)} collective-permute-done((f32[32,1024]{1,0:T(8,128)S(1)}, f32[32,1024]{1,0:T(8,128)S(1)}, u32[]{:S(2)}, u32[]{:S(2)}) %collective-permute-start.28) | collective-permute-done | bytes 131104 | tf_op jit(solution)/shard_map/ppermute | solution.py:279
  133.6 2.4 %shard_map.33.work_ref = f32[256,512]{1,0:T(8,128)S(1)} custom-call(f32[256,512]{1,0:T(8,128)S(1)} %shard_map.32.work_ref), custom_call_target="tpu_custom_call" | custom-call | tf_op jit(solution)/shard_map/pallas_call | solution.py:252
  136.1 2.4 %shard_map.34.work_ref = f32[256,512]{1,0:T(8,128)S(1)} custom-call(f32[256,512]{1,0:T(8,128)S(1)} %shard_map.33.work_ref), custom_call_target="tpu_custom_call" | custom-call | tf_op jit(solution)/shard_map/pallas_call | solution.py:252
  138.4 2.2 %shard_map.35.work_ref = f32[256,512]{1,0:T(8,128)S(1)} custom-call(f32[256,512]{1,0:T(8,128)S(1)} %shard_map.34.work_ref), custom_call_target="tpu_custom_call" | custom-call | tf_op jit(solution)/shard_map/pallas_call | solution.py:252
  140.7 2.0 %shard_map.36.work_ref = f32[256,512]{1,0:T(8,128)S(1)} custom-call(f32[256,512]{1,0:T(8,128)S(1)} %shard_map.35.work_ref), custom_call_target="tpu_custom_call" | custom-call | tf_op jit(solution)/shard_map/pallas_call | solution.py:252
  142.7 13.2 %shard_map.38 = (f32[64,512]{1,0:T(8,128)S(1)}, f32[64,512]{1,0:T(8,128)S(1)}, f32[64,512]{1,0:T(8,128)S(1)}, f32[64,512]{1,0:T(8,128)S(1)}) custom-call(f32[256,512]{1,0:T(8,128)S(1)} %shard_map.36.work_ref, f32[128,1024]{1,0:T(8,128)S(1)} %pad_maximum_fusion.refs_0_, f32[128,1024]{1,0:T(8,128)S(1)} %collective-permute-done.29.refs_1_, ...), custom_call_target="tpu_custom_call" | custom-call | tf_op jit(solution)/shard_map/pallas_call | solution.py:252
  155.9 3.3 %collective-permute-start.31 = (f32[64,512]{1,0:T(8,128)S(1)}, f32[64,512]{1,0:T(8,128)S(1)}, u32[]{:S(2)}, u32[]{:S(2)}) collective-permute-start(f32[64,512]{1,0:T(8,128)S(1)} %get-tuple-element.25), channel_id=1, source_target_pairs={{0,16},{8,24},{16,0},{24,8},{1,17},{9,25},{17,1},{25,9},{2,18},{10... | collective-permute-start | bytes 393224 | tf_op jit(solution)/shard_map/ppermute | solution.py:265
  160.3 4.0 %collective-permute-done.30.refs_1_ = f32[64,512]{1,0:T(8,128)S(1)} collective-permute-done((f32[64,512]{1,0:T(8,128)S(1)}, f32[64,512]{1,0:T(8,128)S(1)}, u32[]{:S(2)}, u32[]{:S(2)}) %collective-permute-start.30) | collective-permute-done | bytes 131104 | tf_op jit(solution)/shard_map/ppermute | solution.py:265
  164.3 5.0 %collective-permute-done.31.refs_2_ = f32[64,512]{1,0:T(8,128)S(1)} collective-permute-done((f32[64,512]{1,0:T(8,128)S(1)}, f32[64,512]{1,0:T(8,128)S(1)}, u32[]{:S(2)}, u32[]{:S(2)}) %collective-permute-start.31) | collective-permute-done | bytes 131104 | tf_op jit(solution)/shard_map/ppermute | solution.py:265
  (71 shorter events, 44.3 us)
Async XLA Ops:
  1.7 29.1 %collective-permute-start.1 = (f32[256,512]{1,0:T(8,128)S(1)}, f32[256,512]{1,0:T(8,128)S(1)}, u32[]{:S(2)}, u32[]{:S(2)}) collective-permute-start(f32[256,512]{1,0:T(8,128)S(1)} %shard_map.29), channel_id=1, source_target_pairs={{0,16},{8,24},{16,0},{24,8},{1,17},{9,25},{17,1},{25,9},{2,18},{10... | collective-permute-start | bytes 1572872 | tf_op jit(solution)/shard_map/ppermute | solution.py:265
  7.5 34.8 %collective-permute-start = (f32[256,512]{1,0:T(8,128)S(1)}, f32[256,512]{1,0:T(8,128)S(1)}, u32[]{:S(2)}, u32[]{:S(2)}) collective-permute-start(f32[256,512]{1,0:T(8,128)S(1)} %get-tuple-element.17), channel_id=1, source_target_pairs={{0,8},{8,0},{16,24},{24,16},{1,9},{9,1},{17,25},{25,17},{2,10},{10... | collective-permute-start | bytes 1572872 | tf_op jit(solution)/shard_map/ppermute | solution.py:265
  9.1 34.6 %collective-permute-start.2 = (f32[256,512]{1,0:T(8,128)S(1)}, f32[256,512]{1,0:T(8,128)S(1)}, u32[]{:S(2)}, u32[]{:S(2)}) collective-permute-start(f32[256,512]{1,0:T(8,128)S(1)} %get-tuple-element.18), channel_id=1, source_target_pairs={{0,24},{8,16},{16,8},{24,0},{1,25},{9,17},{17,9},{25,1},{2,26},{10... | collective-permute-start | bytes 1572872 | tf_op jit(solution)/shard_map/ppermute | solution.py:265
  48.3 13.9 %collective-permute-start.4 = (f32[16,1024]{1,0:T(8,128)S(1)}, f32[16,1024]{1,0:T(8,128)S(1)}, u32[]{:S(2)}, u32[]{:S(2)}) collective-permute-start(f32[16,1024]{1,0:T(8,128)S(1)} %get-tuple-element.32), channel_id=1, source_target_pairs={{0,14},{1,15},{2,12},{3,13},{4,10},{5,11},{6,8},{7,9},{8,6},{9,7},... | collective-permute-start | bytes 196616 | tf_op jit(solution)/shard_map/ppermute | solution.py:279
  58.7 5.5 %collective-permute-start.10 = (f32[16,1024]{1,0:T(8,128)S(1)}, f32[16,1024]{1,0:T(8,128)S(1)}, u32[]{:S(2)}, u32[]{:S(2)}) collective-permute-start(f32[16,1024]{1,0:T(8,128)S(1)} %get-tuple-element.33), channel_id=1, source_target_pairs={{0,2},{1,3},{2,0},{3,1},{4,6},{5,7},{6,4},{7,5},{8,10},{9,11},{10,... | collective-permute-start | bytes 196616 | tf_op jit(solution)/shard_map/ppermute | solution.py:279
  59.8 5.9 %collective-permute-start.8 = (f32[16,1024]{1,0:T(8,128)S(1)}, f32[16,1024]{1,0:T(8,128)S(1)}, u32[]{:S(2)}, u32[]{:S(2)}) collective-permute-start(f32[16,1024]{1,0:T(8,128)S(1)} %get-tuple-element.35), channel_id=1, source_target_pairs={{0,6},{1,7},{2,4},{3,5},{4,2},{5,3},{6,0},{7,1},{8,14},{9,15},{10,... | collective-permute-start | bytes 196616 | tf_op jit(solution)/shard_map/ppermute | solution.py:279
  62.2 5.6 %collective-permute-start.6 = (f32[16,1024]{1,0:T(8,128)S(1)}, f32[16,1024]{1,0:T(8,128)S(1)}, u32[]{:S(2)}, u32[]{:S(2)}) collective-permute-start(f32[16,1024]{1,0:T(8,128)S(1)} %get-tuple-element.37), channel_id=1, source_target_pairs={{0,10},{1,11},{2,8},{3,9},{4,14},{5,15},{6,12},{7,13},{8,2},{9,3},... | collective-permute-start | bytes 196616 | tf_op jit(solution)/shard_map/ppermute | solution.py:279
  69.4 5.9 %collective-permute-start.11 = (f32[16,1024]{1,0:T(8,128)S(1)}, f32[16,1024]{1,0:T(8,128)S(1)}, u32[]{:S(2)}, u32[]{:S(2)}) collective-permute-start(f32[16,1024]{1,0:T(8,128)S(1)} %fusion.9), channel_id=1, source_target_pairs={{0,16},{8,24},{16,0},{24,8},{1,17},{9,25},{17,1},{25,9},{2,18},{10... | collective-permute-start | bytes 196616 | tf_op jit(solution)/shard_map/ppermute | solution.py:265
  75.4 7.4 %collective-permute-start.12 = (f32[16,1024]{1,0:T(8,128)S(1)}, f32[16,1024]{1,0:T(8,128)S(1)}, u32[]{:S(2)}, u32[]{:S(2)}) collective-permute-start(f32[16,1024]{1,0:T(8,128)S(1)} %get-tuple-element.28), channel_id=1, source_target_pairs={{0,2},{1,3},{2,0},{3,1},{4,6},{5,7},{6,4},{7,5},{8,10},{9,11},{10,... | collective-permute-start | bytes 196616 | tf_op jit(solution)/shard_map/ppermute | solution.py:279
  76.9 15.4 %collective-permute-start.18 = (f32[16,1024]{1,0:T(8,128)S(1)}, f32[16,1024]{1,0:T(8,128)S(1)}, u32[]{:S(2)}, u32[]{:S(2)}) collective-permute-start(f32[16,1024]{1,0:T(8,128)S(1)} %get-tuple-element.28), channel_id=1, source_target_pairs={{0,14},{1,15},{2,12},{3,13},{4,10},{5,11},{6,8},{7,9},{8,6},{9,7},... | collective-permute-start | bytes 196616 | tf_op jit(solution)/shard_map/ppermute | solution.py:279
  78.0 14.3 %collective-permute-start.17 = (f32[16,1024]{1,0:T(8,128)S(1)}, f32[16,1024]{1,0:T(8,128)S(1)}, u32[]{:S(2)}, u32[]{:S(2)}) collective-permute-start(f32[16,1024]{1,0:T(8,128)S(1)} %get-tuple-element.28), channel_id=1, source_target_pairs={{0,12},{1,13},{2,14},{3,15},{4,8},{5,9},{6,10},{7,11},{8,4},{9,5},... | collective-permute-start | bytes 196616 | tf_op jit(solution)/shard_map/ppermute | solution.py:279
  79.8 12.4 %collective-permute-start.16 = (f32[16,1024]{1,0:T(8,128)S(1)}, f32[16,1024]{1,0:T(8,128)S(1)}, u32[]{:S(2)}, u32[]{:S(2)}) collective-permute-start(f32[16,1024]{1,0:T(8,128)S(1)} %get-tuple-element.28), channel_id=1, source_target_pairs={{0,10},{1,11},{2,8},{3,9},{4,14},{5,15},{6,12},{7,13},{8,2},{9,3},... | collective-permute-start | bytes 196616 | tf_op jit(solution)/shard_map/ppermute | solution.py:279
  81.2 11.0 %collective-permute-start.15 = (f32[16,1024]{1,0:T(8,128)S(1)}, f32[16,1024]{1,0:T(8,128)S(1)}, u32[]{:S(2)}, u32[]{:S(2)}) collective-permute-start(f32[16,1024]{1,0:T(8,128)S(1)} %get-tuple-element.28), channel_id=1, source_target_pairs={{0,8},{1,9},{2,10},{3,11},{4,12},{5,13},{6,14},{7,15},{8,0},{9,1},... | collective-permute-start | bytes 196616 | tf_op jit(solution)/shard_map/ppermute | solution.py:279
  100.2 7.3 %collective-permute-start.21 = (f32[32,1024]{1,0:T(8,128)S(1)}, f32[32,1024]{1,0:T(8,128)S(1)}, u32[]{:S(2)}, u32[]{:S(2)}) collective-permute-start(f32[32,1024]{1,0:T(8,128)S(1)} %get-tuple-element.29), channel_id=1, source_target_pairs={{0,6},{1,7},{2,4},{3,5},{4,2},{5,3},{6,0},{7,1},{8,14},{9,15},{10,... | collective-permute-start | bytes 393224 | tf_op jit(solution)/shard_map/ppermute | solution.py:279
  101.4 7.1 %collective-permute-start.23 = (f32[32,1024]{1,0:T(8,128)S(1)}, f32[32,1024]{1,0:T(8,128)S(1)}, u32[]{:S(2)}, u32[]{:S(2)}) collective-permute-start(f32[32,1024]{1,0:T(8,128)S(1)} %get-tuple-element.30), channel_id=1, source_target_pairs={{0,2},{1,3},{2,0},{3,1},{4,6},{5,7},{6,4},{7,5},{8,10},{9,11},{10,... | collective-permute-start | bytes 393224 | tf_op jit(solution)/shard_map/ppermute | solution.py:279
  102.2 7.3 %collective-permute-start.22 = (f32[32,1024]{1,0:T(8,128)S(1)}, f32[32,1024]{1,0:T(8,128)S(1)}, u32[]{:S(2)}, u32[]{:S(2)}) collective-permute-start(f32[32,1024]{1,0:T(8,128)S(1)} %get-tuple-element.31), channel_id=1, source_target_pairs={{0,4},{1,5},{2,6},{3,7},{4,0},{5,1},{6,2},{7,3},{8,12},{9,13},{10,... | collective-permute-start | bytes 393224 | tf_op jit(solution)/shard_map/ppermute | solution.py:279
  115.0 8.2 %collective-permute-start.25 = (f32[32,1024]{1,0:T(8,128)S(1)}, f32[32,1024]{1,0:T(8,128)S(1)}, u32[]{:S(2)}, u32[]{:S(2)}) collective-permute-start(f32[32,1024]{1,0:T(8,128)S(1)} %add.98), channel_id=1, source_target_pairs={{0,16},{8,24},{16,0},{24,8},{1,17},{9,25},{17,1},{25,9},{2,18},{10... | collective-permute-start | bytes 393224 | tf_op jit(solution)/shard_map/ppermute | solution.py:265
  123.3 7.3 %collective-permute-start.28 = (f32[32,1024]{1,0:T(8,128)S(1)}, f32[32,1024]{1,0:T(8,128)S(1)}, u32[]{:S(2)}, u32[]{:S(2)}) collective-permute-start(f32[32,1024]{1,0:T(8,128)S(1)} %add.99), channel_id=1, source_target_pairs={{0,6},{1,7},{2,4},{3,5},{4,2},{5,3},{6,0},{7,1},{8,14},{9,15},{10,... | collective-permute-start | bytes 393224 | tf_op jit(solution)/shard_map/ppermute | solution.py:279
  124.6 7.6 %collective-permute-start.27 = (f32[32,1024]{1,0:T(8,128)S(1)}, f32[32,1024]{1,0:T(8,128)S(1)}, u32[]{:S(2)}, u32[]{:S(2)}) collective-permute-start(f32[32,1024]{1,0:T(8,128)S(1)} %add.99), channel_id=1, source_target_pairs={{0,4},{1,5},{2,6},{3,7},{4,0},{5,1},{6,2},{7,3},{8,12},{9,13},{10,... | collective-permute-start | bytes 393224 | tf_op jit(solution)/shard_map/ppermute | solution.py:279
  125.0 7.2 %collective-permute-start.26 = (f32[32,1024]{1,0:T(8,128)S(1)}, f32[32,1024]{1,0:T(8,128)S(1)}, u32[]{:S(2)}, u32[]{:S(2)}) collective-permute-start(f32[32,1024]{1,0:T(8,128)S(1)} %add.99), channel_id=1, source_target_pairs={{0,2},{1,3},{2,0},{3,1},{4,6},{5,7},{6,4},{7,5},{8,10},{9,11},{10,... | collective-permute-start | bytes 393224 | tf_op jit(solution)/shard_map/ppermute | solution.py:279
  132.2 10.4 %collective-permute-start.29 = (f32[128,1024]{1,0:T(8,128)S(1)}, f32[128,1024]{1,0:T(8,128)S(1)}, u32[]{:S(2)}, u32[]{:S(2)}) collective-permute-start(f32[128,1024]{1,0:T(8,128)S(1)} %pad_maximum_fusion.refs_0_), channel_id=1, source_target_pairs={{0,1},{1,0},{2,3},{3,2},{4,5},{5,4},{6,7},{7,6},{8,9},{9,8},{10,11... | collective-permute-start | bytes 1572872 | tf_op jit(solution)/shard_map/ppermute | solution.py:265
  155.9 8.4 %collective-permute-start.30 = (f32[64,512]{1,0:T(8,128)S(1)}, f32[64,512]{1,0:T(8,128)S(1)}, u32[]{:S(2)}, u32[]{:S(2)}) collective-permute-start(f32[64,512]{1,0:T(8,128)S(1)} %get-tuple-element.24), channel_id=1, source_target_pairs={{0,8},{8,0},{16,24},{24,16},{1,9},{9,1},{17,25},{25,17},{2,10},{10... | collective-permute-start | bytes 393224 | tf_op jit(solution)/shard_map/ppermute | solution.py:265
  155.9 13.3 %collective-permute-start.31 = (f32[64,512]{1,0:T(8,128)S(1)}, f32[64,512]{1,0:T(8,128)S(1)}, u32[]{:S(2)}, u32[]{:S(2)}) collective-permute-start(f32[64,512]{1,0:T(8,128)S(1)} %get-tuple-element.25), channel_id=1, source_target_pairs={{0,16},{8,24},{16,0},{24,8},{1,17},{9,25},{17,1},{25,9},{2,18},{10... | collective-permute-start | bytes 393224 | tf_op jit(solution)/shard_map/ppermute | solution.py:265
  159.2 10.0 %collective-permute-start.32 = (f32[64,512]{1,0:T(8,128)S(1)}, f32[64,512]{1,0:T(8,128)S(1)}, u32[]{:S(2)}, u32[]{:S(2)}) collective-permute-start(f32[64,512]{1,0:T(8,128)S(1)} %get-tuple-element.26), channel_id=1, source_target_pairs={{0,24},{8,16},{16,8},{24,0},{1,25},{9,17},{17,9},{25,1},{2,26},{10... | collective-permute-start | bytes 393224 | tf_op jit(solution)/shard_map/ppermute | solution.py:265
  (10 other events, 77.8 us)

commit v3 on v2

--- a/solution.py
+++ b/solution.py
@@ -93,43 +93,53 @@
     work[top:low, :] = wide
 
 
-def lanes(d, rows):
-    if rows % LANES:
-        return pl.ds(d * rows, rows)
-    return pl.ds(pl.multiple_of((lax.axis_index("mode") ^ d) * rows, rows), rows)
-
-
 def stage_side(stage):
     axis, bit = stage
     return lax.rem(lax.axis_index(axis) // bit, 2)
 
 
+def lanes(e, half, rows):
+    if rows % LANES:
+        return pl.ds(e * rows, rows)
+    here = lax.rem(lax.axis_index("mode"), half)
+    return pl.ds(pl.multiple_of((here ^ e) * rows, rows), rows)
+
+
+def half_of(blocks, first, kept):
+    half = len(blocks) // 2
+    top = (lax.axis_index("mode") // half) ^ stage_side(first)
+    lower, upper = (0, half) if kept else (half, 0)
+    return [jnp.where(top == 0, blocks[lower + e][...], blocks[upper + e][...]) for e in range(half)]
+
+
 def row_places(stages, height):
     members = 1 << (len(stages) - 1)
-    share = height // (2 * members)
+    share = height // members
     mine = sum((stage_side(stage) << index) for index, stage in enumerate(stages[1:]))
-    side = stage_side(stages[0])
-    return [
-        [pl.ds(pl.multiple_of((top * members + (mine ^ d)) * share, share), share) for d in range(members)]
-        for top in (side, 1 - side)
-    ]
-
-
-def gather_rows(parts, stages, matrix):
-    for part, places in zip(parts, row_places(stages, matrix.shape[0])):
-        share = part.shape[0] // len(places)
-        for d, place in enumerate(places):
-            matrix[place, :] = part[d * share : (d + 1) * share, :]
-
-
-def spread_out(inner, blocks, outs, stages, matrix):
-    rows = blocks[0].shape[0]
-    for d, block in enumerate(blocks):
-        matrix[:, lanes(d, rows)] = mm(inner, block[...], 1, 1)
-    for out, places in zip(outs, row_places(stages, matrix.shape[0])):
-        share = out.shape[0] // len(places)
-        for d, place in enumerate(places):
-            out[d * share : (d + 1) * share, :] = matrix[place, :]
+    return [pl.ds(pl.multiple_of((mine ^ d) * share, share), share) for d in range(members)]
+
+
+def absolute(part, stages, matrix):
+    places = row_places(stages, matrix.shape[0])
+    share = matrix.shape[0] // len(places)
+    for d, place in enumerate(places):
+        matrix[place, :] = part[d * share : (d + 1) * share, :]
+    return matrix[...]
+
+
+def spread(inner, blocks, first, kept, out):
+    chosen = half_of(blocks, first, kept)
+    for e, block in enumerate(chosen):
+        out[:, lanes(e, len(chosen), block.shape[0])] = mm(inner, block, 1, 1)
+
+
+def collect(part, blocks, first, kept):
+    chosen = half_of(blocks, first, kept)
+    inner = None
+    for e, block in enumerate(chosen):
+        term = mm(part[:, lanes(e, len(chosen), block.shape[0])], block, 1, 0)
+        inner = term if inner is None else inner + term
+    return inner
 
 
 def basis_term(basis_ref, block, d):
@@ -146,29 +156,38 @@
     out_ref[...] = inner
 
 
-def first_kernel(count, stages, basis_ref, early_ref, *refs):
-    blocks, outs, matrix = refs[:count], refs[count:-1], refs[-1]
-    inner = early_ref[...] + basis_term(basis_ref, blocks[-1], count - 1)
-    spread_out(inner, blocks, outs, stages, matrix)
-
-
-def second_kernel(count, inputs, arrived, stages, *refs):
-    parts, blocks = refs[:inputs], refs[inputs : inputs + count]
-    outs, matrix = refs[inputs + count : -1], refs[-1]
-    rows = blocks[0].shape[0]
-    gather_rows(parts, arrived, matrix)
+def first_kernel(stages, basis_ref, early_ref, *refs):
+    *blocks, inner_ref, sent_ref, held = refs
+    held[...] = early_ref[...] + basis_term(basis_ref, blocks[-1], len(blocks) - 1)
+    share = held.shape[0] >> (len(stages) - 1)
+    for d, place in enumerate(row_places(stages, held.shape[0])):
+        inner_ref[d * share : (d + 1) * share, :] = held[place, :]
+    spread(inner_ref[...], blocks, stages[0], False, sent_ref)
+
+
+def keep_kernel(first, inner_ref, *refs):
+    *blocks, kept_ref = refs
+    spread(inner_ref[...], blocks, first, True, kept_ref)
+
+
+def collect_kernel(first, part_ref, *refs):
+    *blocks, out_ref = refs
+    out_ref[...] = collect(part_ref, blocks, first, True)
+
+
+def second_kernel(first, early_ref, part_ref, *refs):
+    *blocks, inner_ref, sent_ref = refs
+    inner_ref[...] = (early_ref[...] + collect(part_ref, blocks, first, False)) * LIFT
+    spread(inner_ref[...], blocks, first, False, sent_ref)
+
+
+def inner_kernel(stages, kept_ref, got_ref, work, matrix):
     inner = None
-    for d, block in enumerate(blocks):
-        term = mm(matrix[:, lanes(d, rows)], block[...], 1, 0)
+    for part in (kept_ref, got_ref):
+        whole = absolute(part, stages, matrix)
+        term = mm(whole, whole, 1, 1)
         inner = term if inner is None else inner + term
-    spread_out(inner * LIFT, blocks, outs, stages, matrix)
-
-
-def inner_kernel(stages, *refs):
-    *parts, work, matrix = refs
-    gather_rows(parts, stages, matrix)
-    whole = matrix[...]
-    begin(mm(whole, whole, 1, 1), work)
+    begin(inner, work)
 
 
 def step_kernel(top, work_ref, work, ones):
@@ -177,22 +196,25 @@
     step(work, top, ones[...])
 
 
-def last_kernel(count, inputs, stages, work_ref, *refs):
-    parts, blocks = refs[:inputs], refs[inputs : inputs + count]
-    outs, (work, matrix, held, ones) = refs[inputs + count : -4], refs[-4:]
-    rank, rows = matrix.shape[0], blocks[0].shape[0]
-    gather_rows(parts, stages, matrix)
+def basis_half(work_ref, part, blocks, stages, kept, matrix):
+    rank = matrix.shape[0]
     factor = work_ref[:, rank:] * (1.0 / LIFT)
-    inner = None
-    projected = None
-    for d, block in enumerate(blocks):
-        basis = mm(factor, matrix[:, lanes(d, rows)], 1, 0)
-        term = mm(basis, basis, 1, 1)
-        inner = term if inner is None else inner + term
-        term = mm(basis, block[...], 1, 0)
-        projected = term if projected is None else projected + term
-    held[...] = projected
-    begin(inner, work)
+    matrix[...] = mm(factor, absolute(part, stages, matrix), 1, 0)
+    return mm(matrix[...], matrix[...], 1, 1), collect(matrix, blocks, stages[0], kept)
+
+
+def half_kernel(stages, work_ref, part_ref, *refs):
+    *blocks, inner_ref, projected_ref, matrix = refs
+    inner_ref[...], projected_ref[...] = basis_half(work_ref, part_ref, blocks, stages, True, matrix)
+
+
+def last_kernel(count, stages, work_ref, part_ref, inner_ref, projected_ref, *refs):
+    blocks = refs[:count]
+    outs, (work, matrix, held, ones) = refs[count:-4], refs[-4:]
+    rank = matrix.shape[0]
+    inner, projected = basis_half(work_ref, part_ref, blocks, stages, False, matrix)
+    held[...] = projected_ref[...] + projected
+    begin(inner_ref[...] + inner, work)
     ones[...] = jnp.ones_like(ones)
     for top in range(0, rank, HALF):
         step(work, top, ones[...])
@@ -200,8 +222,7 @@
     here = lax.axis_index("mode")
     part = rank // count
     for d, out in enumerate(outs):
-        place = pl.ds(pl.multiple_of((here ^ d) * part, part), part)
-        out[...] = held[place, :]
+        out[...] = held[pl.ds(pl.multiple_of((here ^ d) * part, part), part), :]
 
 
 def pick_kernel(distances, fibres, slab_ref, *refs):
@@ -279,11 +300,12 @@
     return lax.ppermute(block, axes, [(k, k ^ flip) for k in range(sizes[0] * sizes[1] * sizes[2])])
 
 
-def all_reduce(kept, sent, stages):
+def all_reduce(sent, keep, stages):
     members = 1 << (len(stages) - 1)
-    share = kept.shape[0] // members
+    share = sent.shape[0] // members
     far_first = range(members - 1, 0, -1)
     got = exchange(sent, *stages[0])
+    kept = keep()
 
     def summed(d):
         place = slice(d * share, (d + 1) * share)
@@ -320,11 +342,8 @@
     count = lax.axis_size("mode")
     here = lax.axis_index("mode")
     rows, nj, nk = density_slab.shape
-    width, rank = start_basis.shape
+    _, rank = start_basis.shape
     stages = [(axis, bit) for axis in ("rb", "ra") for bit in bits_of(axis)]
-    wider = stages + [("mode", 1)]
-    if rank >> len(wider) < SUB:
-        wider = stages
 
     share = nj // count
     slab = pltpu.with_memory_space_constraint(density_slab.reshape(rows * nj, nk), pltpu.HBM)
@@ -336,52 +355,58 @@
     for d, piece in zip(far_first + [0], picked):
         blocks[d] = exchange(piece, "mode", d) if d else piece
 
+    half = count // 2
+    first = stages[0]
+
     def turn(matrix):
         if rows % LANES == 0:
             return matrix
-        split = matrix.reshape(-1, count, rows).transpose(1, 0, 2)
-        return turned(split, count, here).transpose(1, 0, 2).reshape(-1, width)
-
-    def total(partials, stages):
-        kept, sent = partials
-        return all_reduce(turn(kept), turn(sent), stages)
-
-    half = [(rank // 2, width)] * 2
+        split = matrix.reshape(rank, half, rows).transpose(1, 0, 2)
+        return turned(split, half, here % half).transpose(1, 0, 2).reshape(rank, half * rows)
+
+    def total(inner, sent):
+        def keep():
+            (kept,) = call(functools.partial(keep_kernel, first), [column_half], [], inner, *blocks)
+            return turn(kept)
+
+        return all_reduce(turn(sent), keep, stages)
+
     inner_shape = (rank, share * nk)
-    tall = (rank, width)
+    column_half = (rank, half * rows)
     work = (rank, 2 * rank)
     (early,) = call(early_kernel, [inner_shape], [], start_basis, *blocks[:-1])
-    applied = total(
-        call(
-            functools.partial(first_kernel, count, wider),
-            half,
-            [tall],
-            start_basis,
-            early,
-            *blocks,
-        ),
-        wider,
-    )
-    turned_in = [turn(part) for part in applied]
-    again = total(
-        call(
-            functools.partial(second_kernel, count, len(applied), wider, stages),
-            half,
-            [tall],
-            *turned_in,
-            *blocks,
-        ),
-        stages,
-    )
-    (factor,) = call(functools.partial(inner_kernel, wider), [work], [tall], *applied)
+    inner, sent = call(
+        functools.partial(first_kernel, stages),
+        [inner_shape, column_half],
+        [inner_shape],
+        start_basis,
+        early,
+        *blocks,
+    )
+    kept, got = total(inner, sent)
+    (early,) = call(functools.partial(collect_kernel, first), [inner_shape], [], turn(kept), *blocks)
+    inner, sent = call(
+        functools.partial(second_kernel, first), [inner_shape, column_half], [], early, turn(got), *blocks
+    )
+    again, other = total(inner, sent)
+    (factor,) = call(functools.partial(inner_kernel, stages), [work], [column_half], kept, got)
     for top in range(0, rank, HALF):
         (factor,) = call(functools.partial(step_kernel, top), [work], [(SUB, LANES)], factor)
+    early = call(
+        functools.partial(half_kernel, stages),
+        [(rank, rank), inner_shape],
+        [column_half],
+        factor,
+        turn(again),
+        *blocks,
+    )
     outward = call(
-        functools.partial(last_kernel, count, len(again), stages),
+        functools.partial(last_kernel, count, stages),
         [(rank // count, share * nk)] * count,
-        [work, tall, inner_shape, (SUB, LANES)],
+        [work, column_half, inner_shape, (SUB, LANES)],
         factor,
-        *[turn(part) for part in again],
+        turn(other),
+        *early,
         *blocks,
     )
     back = list(outward)

time: 170 us -> 165 us (0.971)
  starting transfers between devices: 47.4 us -> 38.5 us
  waiting for transfers between devices: 86.7 us -> 88.4 us
    ppermute x20 -> x12, starting transfers between devices: 32.2 us -> 14.8 us  [plane_exchange(): lax.ppermute(block, axes, [(k, k ^ flip) for k in range(sizes[0] * sizes[...]
    ppermute x13 -> x14, starting transfers between devices: 15.2 us -> 23.7 us  [exchange(): return lax.ppermute(block, axis, [(k, k ^ bit) for k in range(size)])]
    ppermute x13 -> x14, waiting for transfers between devices: 62.8 us -> 64.7 us  [exchange(): return lax.ppermute(block, axis, [(k, k ^ bit) for k in range(size)])]
    pallas_call x10 -> x14, Pallas kernels: 32.4 us -> 34 us  [call(): pl.pallas_call(kernel, out_shape=[jax.ShapeDtypeStruct(shape, jnp.float32...]
    ppermute x20 -> x12, waiting for transfers between devices: 23.9 us -> 23.7 us  [plane_exchange(): lax.ppermute(block, axes, [(k, k ^ flip) for k in range(sizes[0] * sizes[...]
  transfers between devices with their start and end apart: 33 -> 26, of which waited for: 21 -> 21; matrix products, arithmetic and copies ran while one was open for 0% -> 0% of each run, Pallas kernels for 8% -> 12%
where the time goes in v3:
time: 165 us
  waiting for transfers between devices  88.4 us (54%)
  starting transfers between devices  38.5 us (23%)
  Pallas kernels  37.3 us (23%)
    ppermute x14, waiting for transfers between devices, exchange(): return lax.ppermute(block, axis, [(k, k ^ bit) for k in range(size)])  64.7 us
    pallas_call x14, Pallas kernels, call(): pl.pallas_call(kernel, out_shape=[jax.ShapeDtypeStruct(shape, jnp.float32...  34 us
    ppermute x12, waiting for transfers between devices, plane_exchange(): lax.ppermute(block, axes, [(k, k ^ flip) for k in range(sizes[0] * sizes[...  23.7 us
    ppermute x14, starting transfers between devices, exchange(): return lax.ppermute(block, axis, [(k, k ^ bit) for k in range(size)])  23.7 us
    ppermute x12, starting transfers between devices, plane_exchange(): lax.ppermute(block, axes, [(k, k ^ flip) for k in range(sizes[0] * sizes[...  14.8 us
    pallas_call x2, Pallas kernels, pick(): pl.pallas_call(functools.partial(pick_kernel, distances, fibres), out_sha...  3.31 us
  transfers between devices with their start and end apart: 26, of which 21 were waited for; matrix products, arithmetic and copies ran while one was open for 0% of the time, Pallas kernels for 12%

profile of v3, /device:TPU:0, one launch (start us, length us, event | category | flops | bytes accessed | tf_op | source)
XLA Modules:
  0.0 164.8 jit_solution(17912580282861849436)
XLA Ops:
  1.7 4.1 %collective-permute-start.1 = (f32[256,512]{1,0:T(8,128)S(1)}, f32[256,512]{1,0:T(8,128)S(1)}, u32[]{:S(2)}, u32[]{:S(2)}) collective-permute-start(f32[256,512]{1,0:T(8,128)S(1)} %shard_map.29), channel_id=1, source_target_pairs={{0,16},{8,24},{16,0},{24,8},{1,17},{9,25},{17,1},{25,9},{2,18},{10... | collective-permute-start | bytes 1572872 | tf_op jit(solution)/shard_map/ppermute | solution.py:286
  9.1 21.6 %collective-permute-done.1.refs_2_ = f32[256,512]{1,0:T(8,128)S(1)} collective-permute-done((f32[256,512]{1,0:T(8,128)S(1)}, f32[256,512]{1,0:T(8,128)S(1)}, u32[]{:S(2)}, u32[]{:S(2)}) %collective-permute-start.1) | collective-permute-done | bytes 524320 | tf_op jit(solution)/shard_map/ppermute | solution.py:286
  30.7 11.5 %collective-permute-done.refs_1_ = f32[256,512]{1,0:T(8,128)S(1)} collective-permute-done((f32[256,512]{1,0:T(8,128)S(1)}, f32[256,512]{1,0:T(8,128)S(1)}, u32[]{:S(2)}, u32[]{:S(2)}) %collective-permute-start) | collective-permute-done | bytes 524320 | tf_op jit(solution)/shard_map/ppermute | solution.py:286
  47.5 2.6 %collective-permute-start.4 = (f32[64,512]{1,0:T(8,128)S(1)}, f32[64,512]{1,0:T(8,128)S(1)}, u32[]{:S(2)}, u32[]{:S(2)}) collective-permute-start(f32[64,512]{1,0:T(8,128)S(1)} %get-tuple-element.34), channel_id=1, source_target_pairs={{0,6},{1,7},{2,4},{3,5},{4,2},{5,3},{6,0},{7,1},{8,14},{9,15},{10,... | collective-permute-start | bytes 393224 | tf_op jit(solution)/shard_map/ppermute | solution.py:300
  51.0 3.8 %collective-permute-done.4 = f32[64,512]{1,0:T(8,128)S(1)} collective-permute-done((f32[64,512]{1,0:T(8,128)S(1)}, f32[64,512]{1,0:T(8,128)S(1)}, u32[]{:S(2)}, u32[]{:S(2)}) %collective-permute-start.4) | collective-permute-done | bytes 131104 | tf_op jit(solution)/shard_map/ppermute | solution.py:300
  56.9 8.5 %collective-permute-start.7 = (f32[64,512]{1,0:T(8,128)S(1)}, f32[64,512]{1,0:T(8,128)S(1)}, u32[]{:S(2)}, u32[]{:S(2)}) collective-permute-start(f32[64,512]{1,0:T(8,128)S(1)} %fusion.5), channel_id=1, source_target_pairs={{0,8},{8,0},{16,24},{24,16},{1,9},{9,1},{17,25},{25,17},{2,10},{10... | collective-permute-start | bytes 393224 | tf_op jit(solution)/shard_map/ppermute | solution.py:286
  65.4 3.2 %collective-permute-done.7 = f32[64,512]{1,0:T(8,128)S(1)} collective-permute-done((f32[64,512]{1,0:T(8,128)S(1)}, f32[64,512]{1,0:T(8,128)S(1)}, u32[]{:S(2)}, u32[]{:S(2)}) %collective-permute-start.7) | collective-permute-done | bytes 131104 | tf_op jit(solution)/shard_map/ppermute | solution.py:286
  68.7 3.7 %collective-permute-start.8 = (f32[64,512]{1,0:T(8,128)S(1)}, f32[64,512]{1,0:T(8,128)S(1)}, u32[]{:S(2)}, u32[]{:S(2)}) collective-permute-start(f32[64,512]{1,0:T(8,128)S(1)} %add.61), channel_id=1, source_target_pairs={{0,16},{8,24},{16,0},{24,8},{1,17},{9,25},{17,1},{25,9},{2,18},{10... | collective-permute-start | bytes 393224 | tf_op jit(solution)/shard_map/ppermute | solution.py:286
  72.4 5.2 %collective-permute-done.8 = f32[64,512]{1,0:T(8,128)S(1)} collective-permute-done((f32[64,512]{1,0:T(8,128)S(1)}, f32[64,512]{1,0:T(8,128)S(1)}, u32[]{:S(2)}, u32[]{:S(2)}) %collective-permute-start.8) | collective-permute-done | bytes 131104 | tf_op jit(solution)/shard_map/ppermute | solution.py:286
  77.6 3.3 %collective-permute-start.11 = (f32[64,512]{1,0:T(8,128)S(1)}, f32[64,512]{1,0:T(8,128)S(1)}, u32[]{:S(2)}, u32[]{:S(2)}) collective-permute-start(f32[64,512]{1,0:T(8,128)S(1)} %add.62), channel_id=1, source_target_pairs={{0,6},{1,7},{2,4},{3,5},{4,2},{5,3},{6,0},{7,1},{8,14},{9,15},{10,... | collective-permute-start | bytes 393224 | tf_op jit(solution)/shard_map/ppermute | solution.py:300
  81.6 3.2 %collective-permute-done.11 = f32[64,512]{1,0:T(8,128)S(1)} collective-permute-done((f32[64,512]{1,0:T(8,128)S(1)}, f32[64,512]{1,0:T(8,128)S(1)}, u32[]{:S(2)}, u32[]{:S(2)}) %collective-permute-start.11) | collective-permute-done | bytes 131104 | tf_op jit(solution)/shard_map/ppermute | solution.py:300
  84.8 2.4 %collective-permute-done.10 = f32[64,512]{1,0:T(8,128)S(1)} collective-permute-done((f32[64,512]{1,0:T(8,128)S(1)}, f32[64,512]{1,0:T(8,128)S(1)}, u32[]{:S(2)}, u32[]{:S(2)}) %collective-permute-start.10) | collective-permute-done | bytes 131104 | tf_op jit(solution)/shard_map/ppermute | solution.py:300
  97.3 3.8 %collective-permute-done.14 = f32[64,512]{1,0:T(8,128)S(1)} collective-permute-done((f32[64,512]{1,0:T(8,128)S(1)}, f32[64,512]{1,0:T(8,128)S(1)}, u32[]{:S(2)}, u32[]{:S(2)}) %collective-permute-start.14) | collective-permute-done | bytes 131104 | tf_op jit(solution)/shard_map/ppermute | solution.py:300
  103.1 5.1 %collective-permute-done.17 = f32[64,512]{1,0:T(8,128)S(1)} collective-permute-done((f32[64,512]{1,0:T(8,128)S(1)}, f32[64,512]{1,0:T(8,128)S(1)}, u32[]{:S(2)}, u32[]{:S(2)}) %collective-permute-start.17) | collective-permute-done | bytes 131104 | tf_op jit(solution)/shard_map/ppermute | solution.py:286
  109.0 7.2 %collective-permute-done.18 = f32[64,512]{1,0:T(8,128)S(1)} collective-permute-done((f32[64,512]{1,0:T(8,128)S(1)}, f32[64,512]{1,0:T(8,128)S(1)}, u32[]{:S(2)}, u32[]{:S(2)}) %collective-permute-start.18) | collective-permute-done | bytes 131104 | tf_op jit(solution)/shard_map/ppermute | solution.py:286
  120.0 2.9 %collective-permute-done.21 = f32[64,512]{1,0:T(8,128)S(1)} collective-permute-done((f32[64,512]{1,0:T(8,128)S(1)}, f32[64,512]{1,0:T(8,128)S(1)}, u32[]{:S(2)}, u32[]{:S(2)}) %collective-permute-start.21) | collective-permute-done | bytes 131104 | tf_op jit(solution)/shard_map/ppermute | solution.py:300
  122.8 2.2 %collective-permute-done.20 = f32[64,512]{1,0:T(8,128)S(1)} collective-permute-done((f32[64,512]{1,0:T(8,128)S(1)}, f32[64,512]{1,0:T(8,128)S(1)}, u32[]{:S(2)}, u32[]{:S(2)}) %collective-permute-start.20) | collective-permute-done | bytes 131104 | tf_op jit(solution)/shard_map/ppermute | solution.py:300
  127.5 2.4 %shard_map.34.work_ref = f32[256,512]{1,0:T(8,128)S(1)} custom-call(f32[256,512]{1,0:T(8,128)S(1)} %shard_map.33.work_ref), custom_call_target="tpu_custom_call" | custom-call | tf_op jit(solution)/shard_map/pallas_call | solution.py:273
  130.0 2.4 %shard_map.35.work_ref = f32[256,512]{1,0:T(8,128)S(1)} custom-call(f32[256,512]{1,0:T(8,128)S(1)} %shard_map.34.work_ref), custom_call_target="tpu_custom_call" | custom-call | tf_op jit(solution)/shard_map/pallas_call | solution.py:273
  136.6 2.8 %shard_map.41 = (f32[256,256]{1,0:T(8,128)S(1)}, f32[256,512]{1,0:T(8,128)S(1)}) custom-call(f32[256,512]{1,0:T(8,128)S(1)} %shard_map.37.work_ref, f32[256,512]{1,0:T(8,128)S(1)} %pad_maximum_fusion.1.part_ref, f32[256,512]{1,0:T(8,128)S(1)} %get-tuple-element.18.refs_0_, f32[256,512]{1,0:T(8,128)S(1)} %collective-permute-done.refs_1_, ...), custom_call_target="tpu_custom_call" | custom-call | tf_op jit(solution)/shard_map/pallas_call | solution.py:273
  139.4 11.3 %shard_map.42 = (f32[64,512]{1,0:T(8,128)S(1)}, f32[64,512]{1,0:T(8,128)S(1)}, f32[64,512]{1,0:T(8,128)S(1)}, f32[64,512]{1,0:T(8,128)S(1)}) custom-call(f32[256,512]{1,0:T(8,128)S(1)} %shard_map.37.work_ref, f32[256,512]{1,0:T(8,128)S(1)} %collective-permute-done.22.part_ref, f32[256,256]{1,0:T(8,128)S(1)} %get-tuple-element.25.inner_ref, ...), custom_call_target="tpu_custom_call" | custom-call | tf_op jit(solution)/shard_map/pallas_call | solution.py:273
  150.7 2.5 %collective-permute-start.24 = (f32[64,512]{1,0:T(8,128)S(1)}, f32[64,512]{1,0:T(8,128)S(1)}, u32[]{:S(2)}, u32[]{:S(2)}) collective-permute-start(f32[64,512]{1,0:T(8,128)S(1)} %get-tuple-element.29), channel_id=1, source_target_pairs={{0,16},{8,24},{16,0},{24,8},{1,17},{9,25},{17,1},{25,9},{2,18},{10... | collective-permute-start | bytes 393224 | tf_op jit(solution)/shard_map/ppermute | solution.py:286
  155.1 3.6 %collective-permute-done.23.refs_1_ = f32[64,512]{1,0:T(8,128)S(1)} collective-permute-done((f32[64,512]{1,0:T(8,128)S(1)}, f32[64,512]{1,0:T(8,128)S(1)}, u32[]{:S(2)}, u32[]{:S(2)}) %collective-permute-start.23) | collective-permute-done | bytes 131104 | tf_op jit(solution)/shard_map/ppermute | solution.py:286
  158.7 5.1 %collective-permute-done.24.refs_2_ = f32[64,512]{1,0:T(8,128)S(1)} collective-permute-done((f32[64,512]{1,0:T(8,128)S(1)}, f32[64,512]{1,0:T(8,128)S(1)}, u32[]{:S(2)}, u32[]{:S(2)}) %collective-permute-start.24) | collective-permute-done | bytes 131104 | tf_op jit(solution)/shard_map/ppermute | solution.py:286
  (56 shorter events, 40.2 us)
Async XLA Ops:
  1.7 29.1 %collective-permute-start.1 = (f32[256,512]{1,0:T(8,128)S(1)}, f32[256,512]{1,0:T(8,128)S(1)}, u32[]{:S(2)}, u32[]{:S(2)}) collective-permute-start(f32[256,512]{1,0:T(8,128)S(1)} %shard_map.29), channel_id=1, source_target_pairs={{0,16},{8,24},{16,0},{24,8},{1,17},{9,25},{17,1},{25,9},{2,18},{10... | collective-permute-start | bytes 1572872 | tf_op jit(solution)/shard_map/ppermute | solution.py:286
  7.5 34.8 %collective-permute-start = (f32[256,512]{1,0:T(8,128)S(1)}, f32[256,512]{1,0:T(8,128)S(1)}, u32[]{:S(2)}, u32[]{:S(2)}) collective-permute-start(f32[256,512]{1,0:T(8,128)S(1)} %get-tuple-element.19), channel_id=1, source_target_pairs={{0,8},{8,0},{16,24},{24,16},{1,9},{9,1},{17,25},{25,17},{2,10},{10... | collective-permute-start | bytes 1572872 | tf_op jit(solution)/shard_map/ppermute | solution.py:286
  9.1 34.6 %collective-permute-start.2 = (f32[256,512]{1,0:T(8,128)S(1)}, f32[256,512]{1,0:T(8,128)S(1)}, u32[]{:S(2)}, u32[]{:S(2)}) collective-permute-start(f32[256,512]{1,0:T(8,128)S(1)} %get-tuple-element.20), channel_id=1, source_target_pairs={{0,24},{8,16},{16,8},{24,0},{1,25},{9,17},{17,9},{25,1},{2,26},{10... | collective-permute-start | bytes 1572872 | tf_op jit(solution)/shard_map/ppermute | solution.py:286
  47.5 7.3 %collective-permute-start.4 = (f32[64,512]{1,0:T(8,128)S(1)}, f32[64,512]{1,0:T(8,128)S(1)}, u32[]{:S(2)}, u32[]{:S(2)}) collective-permute-start(f32[64,512]{1,0:T(8,128)S(1)} %get-tuple-element.34), channel_id=1, source_target_pairs={{0,6},{1,7},{2,4},{3,5},{4,2},{5,3},{6,0},{7,1},{8,14},{9,15},{10,... | collective-permute-start | bytes 393224 | tf_op jit(solution)/shard_map/ppermute | solution.py:300
  50.0 6.9 %collective-permute-start.6 = (f32[64,512]{1,0:T(8,128)S(1)}, f32[64,512]{1,0:T(8,128)S(1)}, u32[]{:S(2)}, u32[]{:S(2)}) collective-permute-start(f32[64,512]{1,0:T(8,128)S(1)} %get-tuple-element.35), channel_id=1, source_target_pairs={{0,2},{1,3},{2,0},{3,1},{4,6},{5,7},{6,4},{7,5},{8,10},{9,11},{10,... | collective-permute-start | bytes 393224 | tf_op jit(solution)/shard_map/ppermute | solution.py:300
  50.6 6.3 %collective-permute-start.5 = (f32[64,512]{1,0:T(8,128)S(1)}, f32[64,512]{1,0:T(8,128)S(1)}, u32[]{:S(2)}, u32[]{:S(2)}) collective-permute-start(f32[64,512]{1,0:T(8,128)S(1)} %get-tuple-element.36), channel_id=1, source_target_pairs={{0,4},{1,5},{2,6},{3,7},{4,0},{5,1},{6,2},{7,3},{8,12},{9,13},{10,... | collective-permute-start | bytes 393224 | tf_op jit(solution)/shard_map/ppermute | solution.py:300
  56.9 11.7 %collective-permute-start.7 = (f32[64,512]{1,0:T(8,128)S(1)}, f32[64,512]{1,0:T(8,128)S(1)}, u32[]{:S(2)}, u32[]{:S(2)}) collective-permute-start(f32[64,512]{1,0:T(8,128)S(1)} %fusion.5), channel_id=1, source_target_pairs={{0,8},{8,0},{16,24},{24,16},{1,9},{9,1},{17,25},{25,17},{2,10},{10... | collective-permute-start | bytes 393224 | tf_op jit(solution)/shard_map/ppermute | solution.py:286
  68.7 8.9 %collective-permute-start.8 = (f32[64,512]{1,0:T(8,128)S(1)}, f32[64,512]{1,0:T(8,128)S(1)}, u32[]{:S(2)}, u32[]{:S(2)}) collective-permute-start(f32[64,512]{1,0:T(8,128)S(1)} %add.61), channel_id=1, source_target_pairs={{0,16},{8,24},{16,0},{24,8},{1,17},{9,25},{17,1},{25,9},{2,18},{10... | collective-permute-start | bytes 393224 | tf_op jit(solution)/shard_map/ppermute | solution.py:286
  77.6 7.2 %collective-permute-start.11 = (f32[64,512]{1,0:T(8,128)S(1)}, f32[64,512]{1,0:T(8,128)S(1)}, u32[]{:S(2)}, u32[]{:S(2)}) collective-permute-start(f32[64,512]{1,0:T(8,128)S(1)} %add.62), channel_id=1, source_target_pairs={{0,6},{1,7},{2,4},{3,5},{4,2},{5,3},{6,0},{7,1},{8,14},{9,15},{10,... | collective-permute-start | bytes 393224 | tf_op jit(solution)/shard_map/ppermute | solution.py:300
  81.0 6.3 %collective-permute-start.10 = (f32[64,512]{1,0:T(8,128)S(1)}, f32[64,512]{1,0:T(8,128)S(1)}, u32[]{:S(2)}, u32[]{:S(2)}) collective-permute-start(f32[64,512]{1,0:T(8,128)S(1)} %add.62), channel_id=1, source_target_pairs={{0,4},{1,5},{2,6},{3,7},{4,0},{5,1},{6,2},{7,3},{8,12},{9,13},{10,... | collective-permute-start | bytes 393224 | tf_op jit(solution)/shard_map/ppermute | solution.py:300
  81.0 6.6 %collective-permute-start.9 = (f32[64,512]{1,0:T(8,128)S(1)}, f32[64,512]{1,0:T(8,128)S(1)}, u32[]{:S(2)}, u32[]{:S(2)}) collective-permute-start(f32[64,512]{1,0:T(8,128)S(1)} %add.62), channel_id=1, source_target_pairs={{0,2},{1,3},{2,0},{3,1},{4,6},{5,7},{6,4},{7,5},{8,10},{9,11},{10,... | collective-permute-start | bytes 393224 | tf_op jit(solution)/shard_map/ppermute | solution.py:300
  87.6 2.0 %collective-permute-start.12 = (f32[256,512]{1,0:T(8,128)S(1)}, f32[256,512]{1,0:T(8,128)S(1)}, u32[]{:S(2)}, u32[]{:S(2)}) collective-permute-start(f32[256,512]{1,0:T(8,128)S(1)} %pad_maximum_fusion.kept_ref.part_ref), channel_id=1, source_target_pairs={{0,1},{1,0},{2,3},{3,2},{4,5},{5,4},{6,7},{7,6},{8,9},{9,8},{10,11... | collective-permute-start | bytes 1572872 | tf_op jit(solution)/shard_map/ppermute | solution.py:286
  93.7 7.3 %collective-permute-start.14 = (f32[64,512]{1,0:T(8,128)S(1)}, f32[64,512]{1,0:T(8,128)S(1)}, u32[]{:S(2)}, u32[]{:S(2)}) collective-permute-start(f32[64,512]{1,0:T(8,128)S(1)} %get-tuple-element.31), channel_id=1, source_target_pairs={{0,6},{1,7},{2,4},{3,5},{4,2},{5,3},{6,0},{7,1},{8,14},{9,15},{10,... | collective-permute-start | bytes 393224 | tf_op jit(solution)/shard_map/ppermute | solution.py:300
  95.3 7.7 %collective-permute-start.16 = (f32[64,512]{1,0:T(8,128)S(1)}, f32[64,512]{1,0:T(8,128)S(1)}, u32[]{:S(2)}, u32[]{:S(2)}) collective-permute-start(f32[64,512]{1,0:T(8,128)S(1)} %get-tuple-element.32), channel_id=1, source_target_pairs={{0,2},{1,3},{2,0},{3,1},{4,6},{5,7},{6,4},{7,5},{8,10},{9,11},{10,... | collective-permute-start | bytes 393224 | tf_op jit(solution)/shard_map/ppermute | solution.py:300
  96.7 6.3 %collective-permute-start.15 = (f32[64,512]{1,0:T(8,128)S(1)}, f32[64,512]{1,0:T(8,128)S(1)}, u32[]{:S(2)}, u32[]{:S(2)}) collective-permute-start(f32[64,512]{1,0:T(8,128)S(1)} %get-tuple-element.33), channel_id=1, source_target_pairs={{0,4},{1,5},{2,6},{3,7},{4,0},{5,1},{6,2},{7,3},{8,12},{9,13},{10,... | collective-permute-start | bytes 393224 | tf_op jit(solution)/shard_map/ppermute | solution.py:300
  103.1 5.1 %collective-permute-start.17 = (f32[64,512]{1,0:T(8,128)S(1)}, f32[64,512]{1,0:T(8,128)S(1)}, u32[]{:S(2)}, u32[]{:S(2)}) collective-permute-start(f32[64,512]{1,0:T(8,128)S(1)} %fusion.2), channel_id=1, source_target_pairs={{0,8},{8,0},{16,24},{24,16},{1,9},{9,1},{17,25},{25,17},{2,10},{10... | collective-permute-start | bytes 393224 | tf_op jit(solution)/shard_map/ppermute | solution.py:286
  108.2 8.0 %collective-permute-start.18 = (f32[64,512]{1,0:T(8,128)S(1)}, f32[64,512]{1,0:T(8,128)S(1)}, u32[]{:S(2)}, u32[]{:S(2)}) collective-permute-start(f32[64,512]{1,0:T(8,128)S(1)} %add.70), channel_id=1, source_target_pairs={{0,16},{8,24},{16,0},{24,8},{1,17},{9,25},{17,1},{25,9},{2,18},{10... | collective-permute-start | bytes 393224 | tf_op jit(solution)/shard_map/ppermute | solution.py:286
  116.3 6.6 %collective-permute-start.21 = (f32[64,512]{1,0:T(8,128)S(1)}, f32[64,512]{1,0:T(8,128)S(1)}, u32[]{:S(2)}, u32[]{:S(2)}) collective-permute-start(f32[64,512]{1,0:T(8,128)S(1)} %add.71), channel_id=1, source_target_pairs={{0,6},{1,7},{2,4},{3,5},{4,2},{5,3},{6,0},{7,1},{8,14},{9,15},{10,... | collective-permute-start | bytes 393224 | tf_op jit(solution)/shard_map/ppermute | solution.py:300
  117.9 7.2 %collective-permute-start.20 = (f32[64,512]{1,0:T(8,128)S(1)}, f32[64,512]{1,0:T(8,128)S(1)}, u32[]{:S(2)}, u32[]{:S(2)}) collective-permute-start(f32[64,512]{1,0:T(8,128)S(1)} %add.71), channel_id=1, source_target_pairs={{0,4},{1,5},{2,6},{3,7},{4,0},{5,1},{6,2},{7,3},{8,12},{9,13},{10,... | collective-permute-start | bytes 393224 | tf_op jit(solution)/shard_map/ppermute | solution.py:300
  120.0 6.1 %collective-permute-start.19 = (f32[64,512]{1,0:T(8,128)S(1)}, f32[64,512]{1,0:T(8,128)S(1)}, u32[]{:S(2)}, u32[]{:S(2)}) collective-permute-start(f32[64,512]{1,0:T(8,128)S(1)} %add.71), channel_id=1, source_target_pairs={{0,2},{1,3},{2,0},{3,1},{4,6},{5,7},{6,4},{7,5},{8,10},{9,11},{10,... | collective-permute-start | bytes 393224 | tf_op jit(solution)/shard_map/ppermute | solution.py:300
  126.1 13.3 %collective-permute-start.22 = (f32[256,512]{1,0:T(8,128)S(1)}, f32[256,512]{1,0:T(8,128)S(1)}, u32[]{:S(2)}, u32[]{:S(2)}) collective-permute-start(f32[256,512]{1,0:T(8,128)S(1)} %pad_maximum_fusion.1.part_ref), channel_id=1, source_target_pairs={{0,1},{1,0},{2,3},{3,2},{4,5},{5,4},{6,7},{7,6},{8,9},{9,8},{10,11... | collective-permute-start | bytes 1572872 | tf_op jit(solution)/shard_map/ppermute | solution.py:286
  150.6 8.0 %collective-permute-start.23 = (f32[64,512]{1,0:T(8,128)S(1)}, f32[64,512]{1,0:T(8,128)S(1)}, u32[]{:S(2)}, u32[]{:S(2)}) collective-permute-start(f32[64,512]{1,0:T(8,128)S(1)} %get-tuple-element.28), channel_id=1, source_target_pairs={{0,8},{8,0},{16,24},{24,16},{1,9},{9,1},{17,25},{25,17},{2,10},{10... | collective-permute-start | bytes 393224 | tf_op jit(solution)/shard_map/ppermute | solution.py:286
  150.7 13.0 %collective-permute-start.24 = (f32[64,512]{1,0:T(8,128)S(1)}, f32[64,512]{1,0:T(8,128)S(1)}, u32[]{:S(2)}, u32[]{:S(2)}) collective-permute-start(f32[64,512]{1,0:T(8,128)S(1)} %get-tuple-element.29), channel_id=1, source_target_pairs={{0,16},{8,24},{16,0},{24,8},{1,17},{9,25},{17,1},{25,9},{2,18},{10... | collective-permute-start | bytes 393224 | tf_op jit(solution)/shard_map/ppermute | solution.py:286
  153.2 10.5 %collective-permute-start.25 = (f32[64,512]{1,0:T(8,128)S(1)}, f32[64,512]{1,0:T(8,128)S(1)}, u32[]{:S(2)}, u32[]{:S(2)}) collective-permute-start(f32[64,512]{1,0:T(8,128)S(1)} %get-tuple-element.30), channel_id=1, source_target_pairs={{0,24},{8,16},{16,8},{24,0},{1,25},{9,17},{17,9},{25,1},{2,26},{10... | collective-permute-start | bytes 393224 | tf_op jit(solution)/shard_map/ppermute | solution.py:286
  (3 other events, 46.2 us)

commit v4 on v3

--- a/solution.py
+++ b/solution.py
@@ -87,10 +87,12 @@
         unit = (lane == sub + (g * SUB + HALF)).astype(jnp.float32)
         groups.append(jnp.concatenate([tile, unit[:, HALF:]], axis=1))
     small = jnp.concatenate([tile[:, HALF:] for tile in eliminate(groups, ones)], axis=0)
-    wide = mm(small, work[top:low, :], 1, 0)
+    left, right = low // LANES * LANES, -(-(order + low) // LANES) * LANES
+    wide = mm(small, work[top:low, left:right], 1, 0)
     if low < order:
-        work[low:, :] = work[low:, :] - mm(wide[:, low:order], wide, 0, 0)
-    work[top:low, :] = wide
+        update = mm(wide[:, low - left : order - left], wide, 0, 0)
+        work[low:, left:right] = work[low:, left:right] - update
+    work[top:low, left:right] = wide
 
 
 def stage_side(stage):

time: 165 us -> 165 us (level)
  no operation moved by 1% of the time
where the time goes in v4:
time: 165 us; the launch traced here: 164 us
  waiting for transfers between devices  88.4 us (54%)
  starting transfers between devices  38.5 us (23%)
  Pallas kernels  37 us (22%)
    ppermute x14, waiting for transfers between devices, exchange(): return lax.ppermute(block, axis, [(k, k ^ bit) for k in range(size)])  64.7 us
    pallas_call x14, Pallas kernels, call(): pl.pallas_call(kernel, out_shape=[jax.ShapeDtypeStruct(shape, jnp.float32...  33.7 us
    ppermute x12, waiting for transfers between devices, plane_exchange(): lax.ppermute(block, axes, [(k, k ^ flip) for k in range(sizes[0] * sizes[...  23.7 us
    ppermute x14, starting transfers between devices, exchange(): return lax.ppermute(block, axis, [(k, k ^ bit) for k in range(size)])  23.7 us
    ppermute x12, starting transfers between devices, plane_exchange(): lax.ppermute(block, axes, [(k, k ^ flip) for k in range(sizes[0] * sizes[...  14.8 us
    pallas_call x2, Pallas kernels, pick(): pl.pallas_call(functools.partial(pick_kernel, distances, fibres), out_sha...  3.31 us
  transfers between devices with their start and end apart: 26, of which 21 were waited for; matrix products, arithmetic and copies ran while one was open for 0% of the time, Pallas kernels for 12%

profile of v4, /device:TPU:0, one launch (start us, length us, event | category | flops | bytes accessed | tf_op | source)
XLA Modules:
  0.0 164.5 jit_solution(10105502549919432627)
XLA Ops:
  1.7 4.1 %collective-permute-start.1 = (f32[256,512]{1,0:T(8,128)S(1)}, f32[256,512]{1,0:T(8,128)S(1)}, u32[]{:S(2)}, u32[]{:S(2)}) collective-permute-start(f32[256,512]{1,0:T(8,128)S(1)} %shard_map.29), channel_id=1, source_target_pairs={{0,16},{8,24},{16,0},{24,8},{1,17},{9,25},{17,1},{25,9},{2,18},{10... | collective-permute-start | bytes 1572872 | tf_op jit(solution)/shard_map/ppermute | solution.py:288
  9.1 21.6 %collective-permute-done.1.refs_2_ = f32[256,512]{1,0:T(8,128)S(1)} collective-permute-done((f32[256,512]{1,0:T(8,128)S(1)}, f32[256,512]{1,0:T(8,128)S(1)}, u32[]{:S(2)}, u32[]{:S(2)}) %collective-permute-start.1) | collective-permute-done | bytes 524320 | tf_op jit(solution)/shard_map/ppermute | solution.py:288
  30.7 11.5 %collective-permute-done.refs_1_ = f32[256,512]{1,0:T(8,128)S(1)} collective-permute-done((f32[256,512]{1,0:T(8,128)S(1)}, f32[256,512]{1,0:T(8,128)S(1)}, u32[]{:S(2)}, u32[]{:S(2)}) %collective-permute-start) | collective-permute-done | bytes 524320 | tf_op jit(solution)/shard_map/ppermute | solution.py:288
  47.5 2.6 %collective-permute-start.4 = (f32[64,512]{1,0:T(8,128)S(1)}, f32[64,512]{1,0:T(8,128)S(1)}, u32[]{:S(2)}, u32[]{:S(2)}) collective-permute-start(f32[64,512]{1,0:T(8,128)S(1)} %get-tuple-element.34), channel_id=1, source_target_pairs={{0,6},{1,7},{2,4},{3,5},{4,2},{5,3},{6,0},{7,1},{8,14},{9,15},{10,... | collective-permute-start | bytes 393224 | tf_op jit(solution)/shard_map/ppermute | solution.py:302
  51.0 3.8 %collective-permute-done.4 = f32[64,512]{1,0:T(8,128)S(1)} collective-permute-done((f32[64,512]{1,0:T(8,128)S(1)}, f32[64,512]{1,0:T(8,128)S(1)}, u32[]{:S(2)}, u32[]{:S(2)}) %collective-permute-start.4) | collective-permute-done | bytes 131104 | tf_op jit(solution)/shard_map/ppermute | solution.py:302
  56.9 8.5 %collective-permute-start.7 = (f32[64,512]{1,0:T(8,128)S(1)}, f32[64,512]{1,0:T(8,128)S(1)}, u32[]{:S(2)}, u32[]{:S(2)}) collective-permute-start(f32[64,512]{1,0:T(8,128)S(1)} %fusion.5), channel_id=1, source_target_pairs={{0,8},{8,0},{16,24},{24,16},{1,9},{9,1},{17,25},{25,17},{2,10},{10... | collective-permute-start | bytes 393224 | tf_op jit(solution)/shard_map/ppermute | solution.py:288
  65.4 3.2 %collective-permute-done.7 = f32[64,512]{1,0:T(8,128)S(1)} collective-permute-done((f32[64,512]{1,0:T(8,128)S(1)}, f32[64,512]{1,0:T(8,128)S(1)}, u32[]{:S(2)}, u32[]{:S(2)}) %collective-permute-start.7) | collective-permute-done | bytes 131104 | tf_op jit(solution)/shard_map/ppermute | solution.py:288
  68.7 3.7 %collective-permute-start.8 = (f32[64,512]{1,0:T(8,128)S(1)}, f32[64,512]{1,0:T(8,128)S(1)}, u32[]{:S(2)}, u32[]{:S(2)}) collective-permute-start(f32[64,512]{1,0:T(8,128)S(1)} %add.61), channel_id=1, source_target_pairs={{0,16},{8,24},{16,0},{24,8},{1,17},{9,25},{17,1},{25,9},{2,18},{10... | collective-permute-start | bytes 393224 | tf_op jit(solution)/shard_map/ppermute | solution.py:288
  72.4 5.2 %collective-permute-done.8 = f32[64,512]{1,0:T(8,128)S(1)} collective-permute-done((f32[64,512]{1,0:T(8,128)S(1)}, f32[64,512]{1,0:T(8,128)S(1)}, u32[]{:S(2)}, u32[]{:S(2)}) %collective-permute-start.8) | collective-permute-done | bytes 131104 | tf_op jit(solution)/shard_map/ppermute | solution.py:288
  77.6 3.3 %collective-permute-start.11 = (f32[64,512]{1,0:T(8,128)S(1)}, f32[64,512]{1,0:T(8,128)S(1)}, u32[]{:S(2)}, u32[]{:S(2)}) collective-permute-start(f32[64,512]{1,0:T(8,128)S(1)} %add.62), channel_id=1, source_target_pairs={{0,6},{1,7},{2,4},{3,5},{4,2},{5,3},{6,0},{7,1},{8,14},{9,15},{10,... | collective-permute-start | bytes 393224 | tf_op jit(solution)/shard_map/ppermute | solution.py:302
  81.6 3.2 %collective-permute-done.11 = f32[64,512]{1,0:T(8,128)S(1)} collective-permute-done((f32[64,512]{1,0:T(8,128)S(1)}, f32[64,512]{1,0:T(8,128)S(1)}, u32[]{:S(2)}, u32[]{:S(2)}) %collective-permute-start.11) | collective-permute-done | bytes 131104 | tf_op jit(solution)/shard_map/ppermute | solution.py:302
  84.8 2.4 %collective-permute-done.10 = f32[64,512]{1,0:T(8,128)S(1)} collective-permute-done((f32[64,512]{1,0:T(8,128)S(1)}, f32[64,512]{1,0:T(8,128)S(1)}, u32[]{:S(2)}, u32[]{:S(2)}) %collective-permute-start.10) | collective-permute-done | bytes 131104 | tf_op jit(solution)/shard_map/ppermute | solution.py:302
  97.3 3.8 %collective-permute-done.14 = f32[64,512]{1,0:T(8,128)S(1)} collective-permute-done((f32[64,512]{1,0:T(8,128)S(1)}, f32[64,512]{1,0:T(8,128)S(1)}, u32[]{:S(2)}, u32[]{:S(2)}) %collective-permute-start.14) | collective-permute-done | bytes 131104 | tf_op jit(solution)/shard_map/ppermute | solution.py:302
  103.1 5.1 %collective-permute-done.17 = f32[64,512]{1,0:T(8,128)S(1)} collective-permute-done((f32[64,512]{1,0:T(8,128)S(1)}, f32[64,512]{1,0:T(8,128)S(1)}, u32[]{:S(2)}, u32[]{:S(2)}) %collective-permute-start.17) | collective-permute-done | bytes 131104 | tf_op jit(solution)/shard_map/ppermute | solution.py:288
  109.0 7.2 %collective-permute-done.18 = f32[64,512]{1,0:T(8,128)S(1)} collective-permute-done((f32[64,512]{1,0:T(8,128)S(1)}, f32[64,512]{1,0:T(8,128)S(1)}, u32[]{:S(2)}, u32[]{:S(2)}) %collective-permute-start.18) | collective-permute-done | bytes 131104 | tf_op jit(solution)/shard_map/ppermute | solution.py:288
  120.0 2.9 %collective-permute-done.21 = f32[64,512]{1,0:T(8,128)S(1)} collective-permute-done((f32[64,512]{1,0:T(8,128)S(1)}, f32[64,512]{1,0:T(8,128)S(1)}, u32[]{:S(2)}, u32[]{:S(2)}) %collective-permute-start.21) | collective-permute-done | bytes 131104 | tf_op jit(solution)/shard_map/ppermute | solution.py:302
  122.8 2.2 %collective-permute-done.20 = f32[64,512]{1,0:T(8,128)S(1)} collective-permute-done((f32[64,512]{1,0:T(8,128)S(1)}, f32[64,512]{1,0:T(8,128)S(1)}, u32[]{:S(2)}, u32[]{:S(2)}) %collective-permute-start.20) | collective-permute-done | bytes 131104 | tf_op jit(solution)/shard_map/ppermute | solution.py:302
  127.5 2.4 %shard_map.34.work_ref = f32[256,512]{1,0:T(8,128)S(1)} custom-call(f32[256,512]{1,0:T(8,128)S(1)} %shard_map.33.work_ref), custom_call_target="tpu_custom_call" | custom-call | tf_op jit(solution)/shard_map/pallas_call | solution.py:275
  129.9 2.3 %shard_map.35.work_ref = f32[256,512]{1,0:T(8,128)S(1)} custom-call(f32[256,512]{1,0:T(8,128)S(1)} %shard_map.34.work_ref), custom_call_target="tpu_custom_call" | custom-call | tf_op jit(solution)/shard_map/pallas_call | solution.py:275
  136.3 2.8 %shard_map.41 = (f32[256,256]{1,0:T(8,128)S(1)}, f32[256,512]{1,0:T(8,128)S(1)}) custom-call(f32[256,512]{1,0:T(8,128)S(1)} %shard_map.37.work_ref, f32[256,512]{1,0:T(8,128)S(1)} %pad_maximum_fusion.1.part_ref, f32[256,512]{1,0:T(8,128)S(1)} %get-tuple-element.18.refs_0_, f32[256,512]{1,0:T(8,128)S(1)} %collective-permute-done.refs_1_, ...), custom_call_target="tpu_custom_call" | custom-call | tf_op jit(solution)/shard_map/pallas_call | solution.py:275
  139.2 11.2 %shard_map.42 = (f32[64,512]{1,0:T(8,128)S(1)}, f32[64,512]{1,0:T(8,128)S(1)}, f32[64,512]{1,0:T(8,128)S(1)}, f32[64,512]{1,0:T(8,128)S(1)}) custom-call(f32[256,512]{1,0:T(8,128)S(1)} %shard_map.37.work_ref, f32[256,512]{1,0:T(8,128)S(1)} %collective-permute-done.22.part_ref, f32[256,256]{1,0:T(8,128)S(1)} %get-tuple-element.25.inner_ref, ...), custom_call_target="tpu_custom_call" | custom-call | tf_op jit(solution)/shard_map/pallas_call | solution.py:275
  150.4 2.5 %collective-permute-start.24 = (f32[64,512]{1,0:T(8,128)S(1)}, f32[64,512]{1,0:T(8,128)S(1)}, u32[]{:S(2)}, u32[]{:S(2)}) collective-permute-start(f32[64,512]{1,0:T(8,128)S(1)} %get-tuple-element.29), channel_id=1, source_target_pairs={{0,16},{8,24},{16,0},{24,8},{1,17},{9,25},{17,1},{25,9},{2,18},{10... | collective-permute-start | bytes 393224 | tf_op jit(solution)/shard_map/ppermute | solution.py:288
  154.8 3.6 %collective-permute-done.23.refs_1_ = f32[64,512]{1,0:T(8,128)S(1)} collective-permute-done((f32[64,512]{1,0:T(8,128)S(1)}, f32[64,512]{1,0:T(8,128)S(1)}, u32[]{:S(2)}, u32[]{:S(2)}) %collective-permute-start.23) | collective-permute-done | bytes 131104 | tf_op jit(solution)/shard_map/ppermute | solution.py:288
  158.4 5.1 %collective-permute-done.24.refs_2_ = f32[64,512]{1,0:T(8,128)S(1)} collective-permute-done((f32[64,512]{1,0:T(8,128)S(1)}, f32[64,512]{1,0:T(8,128)S(1)}, u32[]{:S(2)}, u32[]{:S(2)}) %collective-permute-start.24) | collective-permute-done | bytes 131104 | tf_op jit(solution)/shard_map/ppermute | solution.py:288
  (56 shorter events, 40.1 us)
Async XLA Ops:
  1.7 29.1 %collective-permute-start.1 = (f32[256,512]{1,0:T(8,128)S(1)}, f32[256,512]{1,0:T(8,128)S(1)}, u32[]{:S(2)}, u32[]{:S(2)}) collective-permute-start(f32[256,512]{1,0:T(8,128)S(1)} %shard_map.29), channel_id=1, source_target_pairs={{0,16},{8,24},{16,0},{24,8},{1,17},{9,25},{17,1},{25,9},{2,18},{10... | collective-permute-start | bytes 1572872 | tf_op jit(solution)/shard_map/ppermute | solution.py:288
  7.5 34.8 %collective-permute-start = (f32[256,512]{1,0:T(8,128)S(1)}, f32[256,512]{1,0:T(8,128)S(1)}, u32[]{:S(2)}, u32[]{:S(2)}) collective-permute-start(f32[256,512]{1,0:T(8,128)S(1)} %get-tuple-element.19), channel_id=1, source_target_pairs={{0,8},{8,0},{16,24},{24,16},{1,9},{9,1},{17,25},{25,17},{2,10},{10... | collective-permute-start | bytes 1572872 | tf_op jit(solution)/shard_map/ppermute | solution.py:288
  9.1 34.6 %collective-permute-start.2 = (f32[256,512]{1,0:T(8,128)S(1)}, f32[256,512]{1,0:T(8,128)S(1)}, u32[]{:S(2)}, u32[]{:S(2)}) collective-permute-start(f32[256,512]{1,0:T(8,128)S(1)} %get-tuple-element.20), channel_id=1, source_target_pairs={{0,24},{8,16},{16,8},{24,0},{1,25},{9,17},{17,9},{25,1},{2,26},{10... | collective-permute-start | bytes 1572872 | tf_op jit(solution)/shard_map/ppermute | solution.py:288
  47.5 7.3 %collective-permute-start.4 = (f32[64,512]{1,0:T(8,128)S(1)}, f32[64,512]{1,0:T(8,128)S(1)}, u32[]{:S(2)}, u32[]{:S(2)}) collective-permute-start(f32[64,512]{1,0:T(8,128)S(1)} %get-tuple-element.34), channel_id=1, source_target_pairs={{0,6},{1,7},{2,4},{3,5},{4,2},{5,3},{6,0},{7,1},{8,14},{9,15},{10,... | collective-permute-start | bytes 393224 | tf_op jit(solution)/shard_map/ppermute | solution.py:302
  50.0 6.9 %collective-permute-start.6 = (f32[64,512]{1,0:T(8,128)S(1)}, f32[64,512]{1,0:T(8,128)S(1)}, u32[]{:S(2)}, u32[]{:S(2)}) collective-permute-start(f32[64,512]{1,0:T(8,128)S(1)} %get-tuple-element.35), channel_id=1, source_target_pairs={{0,2},{1,3},{2,0},{3,1},{4,6},{5,7},{6,4},{7,5},{8,10},{9,11},{10,... | collective-permute-start | bytes 393224 | tf_op jit(solution)/shard_map/ppermute | solution.py:302
  50.6 6.3 %collective-permute-start.5 = (f32[64,512]{1,0:T(8,128)S(1)}, f32[64,512]{1,0:T(8,128)S(1)}, u32[]{:S(2)}, u32[]{:S(2)}) collective-permute-start(f32[64,512]{1,0:T(8,128)S(1)} %get-tuple-element.36), channel_id=1, source_target_pairs={{0,4},{1,5},{2,6},{3,7},{4,0},{5,1},{6,2},{7,3},{8,12},{9,13},{10,... | collective-permute-start | bytes 393224 | tf_op jit(solution)/shard_map/ppermute | solution.py:302
  56.9 11.7 %collective-permute-start.7 = (f32[64,512]{1,0:T(8,128)S(1)}, f32[64,512]{1,0:T(8,128)S(1)}, u32[]{:S(2)}, u32[]{:S(2)}) collective-permute-start(f32[64,512]{1,0:T(8,128)S(1)} %fusion.5), channel_id=1, source_target_pairs={{0,8},{8,0},{16,24},{24,16},{1,9},{9,1},{17,25},{25,17},{2,10},{10... | collective-permute-start | bytes 393224 | tf_op jit(solution)/shard_map/ppermute | solution.py:288
  68.7 8.9 %collective-permute-start.8 = (f32[64,512]{1,0:T(8,128)S(1)}, f32[64,512]{1,0:T(8,128)S(1)}, u32[]{:S(2)}, u32[]{:S(2)}) collective-permute-start(f32[64,512]{1,0:T(8,128)S(1)} %add.61), channel_id=1, source_target_pairs={{0,16},{8,24},{16,0},{24,8},{1,17},{9,25},{17,1},{25,9},{2,18},{10... | collective-permute-start | bytes 393224 | tf_op jit(solution)/shard_map/ppermute | solution.py:288
  77.6 7.2 %collective-permute-start.11 = (f32[64,512]{1,0:T(8,128)S(1)}, f32[64,512]{1,0:T(8,128)S(1)}, u32[]{:S(2)}, u32[]{:S(2)}) collective-permute-start(f32[64,512]{1,0:T(8,128)S(1)} %add.62), channel_id=1, source_target_pairs={{0,6},{1,7},{2,4},{3,5},{4,2},{5,3},{6,0},{7,1},{8,14},{9,15},{10,... | collective-permute-start | bytes 393224 | tf_op jit(solution)/shard_map/ppermute | solution.py:302
  81.0 6.3 %collective-permute-start.10 = (f32[64,512]{1,0:T(8,128)S(1)}, f32[64,512]{1,0:T(8,128)S(1)}, u32[]{:S(2)}, u32[]{:S(2)}) collective-permute-start(f32[64,512]{1,0:T(8,128)S(1)} %add.62), channel_id=1, source_target_pairs={{0,4},{1,5},{2,6},{3,7},{4,0},{5,1},{6,2},{7,3},{8,12},{9,13},{10,... | collective-permute-start | bytes 393224 | tf_op jit(solution)/shard_map/ppermute | solution.py:302
  81.0 6.6 %collective-permute-start.9 = (f32[64,512]{1,0:T(8,128)S(1)}, f32[64,512]{1,0:T(8,128)S(1)}, u32[]{:S(2)}, u32[]{:S(2)}) collective-permute-start(f32[64,512]{1,0:T(8,128)S(1)} %add.62), channel_id=1, source_target_pairs={{0,2},{1,3},{2,0},{3,1},{4,6},{5,7},{6,4},{7,5},{8,10},{9,11},{10,... | collective-permute-start | bytes 393224 | tf_op jit(solution)/shard_map/ppermute | solution.py:302
  87.6 2.0 %collective-permute-start.12 = (f32[256,512]{1,0:T(8,128)S(1)}, f32[256,512]{1,0:T(8,128)S(1)}, u32[]{:S(2)}, u32[]{:S(2)}) collective-permute-start(f32[256,512]{1,0:T(8,128)S(1)} %pad_maximum_fusion.kept_ref.part_ref), channel_id=1, source_target_pairs={{0,1},{1,0},{2,3},{3,2},{4,5},{5,4},{6,7},{7,6},{8,9},{9,8},{10,11... | collective-permute-start | bytes 1572872 | tf_op jit(solution)/shard_map/ppermute | solution.py:288
  93.7 7.3 %collective-permute-start.14 = (f32[64,512]{1,0:T(8,128)S(1)}, f32[64,512]{1,0:T(8,128)S(1)}, u32[]{:S(2)}, u32[]{:S(2)}) collective-permute-start(f32[64,512]{1,0:T(8,128)S(1)} %get-tuple-element.31), channel_id=1, source_target_pairs={{0,6},{1,7},{2,4},{3,5},{4,2},{5,3},{6,0},{7,1},{8,14},{9,15},{10,... | collective-permute-start | bytes 393224 | tf_op jit(solution)/shard_map/ppermute | solution.py:302
  95.3 7.7 %collective-permute-start.16 = (f32[64,512]{1,0:T(8,128)S(1)}, f32[64,512]{1,0:T(8,128)S(1)}, u32[]{:S(2)}, u32[]{:S(2)}) collective-permute-start(f32[64,512]{1,0:T(8,128)S(1)} %get-tuple-element.32), channel_id=1, source_target_pairs={{0,2},{1,3},{2,0},{3,1},{4,6},{5,7},{6,4},{7,5},{8,10},{9,11},{10,... | collective-permute-start | bytes 393224 | tf_op jit(solution)/shard_map/ppermute | solution.py:302
  96.7 6.3 %collective-permute-start.15 = (f32[64,512]{1,0:T(8,128)S(1)}, f32[64,512]{1,0:T(8,128)S(1)}, u32[]{:S(2)}, u32[]{:S(2)}) collective-permute-start(f32[64,512]{1,0:T(8,128)S(1)} %get-tuple-element.33), channel_id=1, source_target_pairs={{0,4},{1,5},{2,6},{3,7},{4,0},{5,1},{6,2},{7,3},{8,12},{9,13},{10,... | collective-permute-start | bytes 393224 | tf_op jit(solution)/shard_map/ppermute | solution.py:302
  103.1 5.1 %collective-permute-start.17 = (f32[64,512]{1,0:T(8,128)S(1)}, f32[64,512]{1,0:T(8,128)S(1)}, u32[]{:S(2)}, u32[]{:S(2)}) collective-permute-start(f32[64,512]{1,0:T(8,128)S(1)} %fusion.2), channel_id=1, source_target_pairs={{0,8},{8,0},{16,24},{24,16},{1,9},{9,1},{17,25},{25,17},{2,10},{10... | collective-permute-start | bytes 393224 | tf_op jit(solution)/shard_map/ppermute | solution.py:288
  108.2 8.0 %collective-permute-start.18 = (f32[64,512]{1,0:T(8,128)S(1)}, f32[64,512]{1,0:T(8,128)S(1)}, u32[]{:S(2)}, u32[]{:S(2)}) collective-permute-start(f32[64,512]{1,0:T(8,128)S(1)} %add.70), channel_id=1, source_target_pairs={{0,16},{8,24},{16,0},{24,8},{1,17},{9,25},{17,1},{25,9},{2,18},{10... | collective-permute-start | bytes 393224 | tf_op jit(solution)/shard_map/ppermute | solution.py:288
  116.3 6.6 %collective-permute-start.21 = (f32[64,512]{1,0:T(8,128)S(1)}, f32[64,512]{1,0:T(8,128)S(1)}, u32[]{:S(2)}, u32[]{:S(2)}) collective-permute-start(f32[64,512]{1,0:T(8,128)S(1)} %add.71), channel_id=1, source_target_pairs={{0,6},{1,7},{2,4},{3,5},{4,2},{5,3},{6,0},{7,1},{8,14},{9,15},{10,... | collective-permute-start | bytes 393224 | tf_op jit(solution)/shard_map/ppermute | solution.py:302
  117.9 7.2 %collective-permute-start.20 = (f32[64,512]{1,0:T(8,128)S(1)}, f32[64,512]{1,0:T(8,128)S(1)}, u32[]{:S(2)}, u32[]{:S(2)}) collective-permute-start(f32[64,512]{1,0:T(8,128)S(1)} %add.71), channel_id=1, source_target_pairs={{0,4},{1,5},{2,6},{3,7},{4,0},{5,1},{6,2},{7,3},{8,12},{9,13},{10,... | collective-permute-start | bytes 393224 | tf_op jit(solution)/shard_map/ppermute | solution.py:302
  120.0 6.1 %collective-permute-start.19 = (f32[64,512]{1,0:T(8,128)S(1)}, f32[64,512]{1,0:T(8,128)S(1)}, u32[]{:S(2)}, u32[]{:S(2)}) collective-permute-start(f32[64,512]{1,0:T(8,128)S(1)} %add.71), channel_id=1, source_target_pairs={{0,2},{1,3},{2,0},{3,1},{4,6},{5,7},{6,4},{7,5},{8,10},{9,11},{10,... | collective-permute-start | bytes 393224 | tf_op jit(solution)/shard_map/ppermute | solution.py:302
  126.1 13.0 %collective-permute-start.22 = (f32[256,512]{1,0:T(8,128)S(1)}, f32[256,512]{1,0:T(8,128)S(1)}, u32[]{:S(2)}, u32[]{:S(2)}) collective-permute-start(f32[256,512]{1,0:T(8,128)S(1)} %pad_maximum_fusion.1.part_ref), channel_id=1, source_target_pairs={{0,1},{1,0},{2,3},{3,2},{4,5},{5,4},{6,7},{7,6},{8,9},{9,8},{10,11... | collective-permute-start | bytes 1572872 | tf_op jit(solution)/shard_map/ppermute | solution.py:288
  150.3 8.0 %collective-permute-start.23 = (f32[64,512]{1,0:T(8,128)S(1)}, f32[64,512]{1,0:T(8,128)S(1)}, u32[]{:S(2)}, u32[]{:S(2)}) collective-permute-start(f32[64,512]{1,0:T(8,128)S(1)} %get-tuple-element.28), channel_id=1, source_target_pairs={{0,8},{8,0},{16,24},{24,16},{1,9},{9,1},{17,25},{25,17},{2,10},{10... | collective-permute-start | bytes 393224 | tf_op jit(solution)/shard_map/ppermute | solution.py:288
  150.4 13.0 %collective-permute-start.24 = (f32[64,512]{1,0:T(8,128)S(1)}, f32[64,512]{1,0:T(8,128)S(1)}, u32[]{:S(2)}, u32[]{:S(2)}) collective-permute-start(f32[64,512]{1,0:T(8,128)S(1)} %get-tuple-element.29), channel_id=1, source_target_pairs={{0,16},{8,24},{16,0},{24,8},{1,17},{9,25},{17,1},{25,9},{2,18},{10... | collective-permute-start | bytes 393224 | tf_op jit(solution)/shard_map/ppermute | solution.py:288
  152.9 10.5 %collective-permute-start.25 = (f32[64,512]{1,0:T(8,128)S(1)}, f32[64,512]{1,0:T(8,128)S(1)}, u32[]{:S(2)}, u32[]{:S(2)}) collective-permute-start(f32[64,512]{1,0:T(8,128)S(1)} %get-tuple-element.30), channel_id=1, source_target_pairs={{0,24},{8,16},{16,8},{24,0},{1,25},{9,17},{17,9},{25,1},{2,26},{10... | collective-permute-start | bytes 393224 | tf_op jit(solution)/shard_map/ppermute | solution.py:288
  (3 other events, 46.2 us)

commit v5 on v4

--- a/solution.py
+++ b/solution.py
@@ -27,16 +27,21 @@
 
 def eliminate(groups, ones):
     sub = lax.broadcasted_iota(jnp.int32, (SUB, LANES), 0)
+
+    def columns_of(tile, first):
+        return [jnp.broadcast_to(tile[:, first + j : first + j + 1], (SUB, LANES)) * ones for j in range(SUB)]
+
+    def row_of(tile, j):
+        return jnp.broadcast_to(tile[j : j + 1, :], (SUB, LANES))
+
     done = []
+    across = columns_of(groups[0], 0)
     for p in range(len(groups)):
         first = p * SUB
-        rows = [jnp.broadcast_to(groups[p][j : j + 1, :], (SUB, LANES)) for j in range(SUB)]
-        across = [
-            jnp.broadcast_to(groups[p][:, first + j : first + j + 1], (SUB, LANES)) * ones for j in range(SUB)
-        ]
+        rows = [row_of(groups[p], j) for j in range(SUB)]
+        upcoming = columns_of(groups[p + 1], first + SUB) if p + 1 < len(groups) else None
         block = [
-            [jnp.broadcast_to(across[j][i : i + 1, :], (SUB, LANES)) if j >= i else None for j in range(SUB)]
-            for i in range(SUB)
+            [row_of(across[j], i) if j >= i else None for j in range(SUB)] for i in range(SUB)
         ]
         lower = [[None] * SUB for _ in range(SUB)]
         inverse = []
@@ -52,15 +57,19 @@
         scaled = [rows[i] * inverse[i] for i in range(SUB)]
         for g in range(p + 1, len(groups)):
             tile = groups[g]
-            columns = [
-                jnp.broadcast_to(tile[:, first + j : first + j + 1], (SUB, LANES)) for j in range(SUB)
-            ]
+            columns = columns_of(tile, first)
             for i in range(SUB):
                 for j in range(i + 1, SUB):
                     columns[j] = columns[j] - columns[i] * lower[j][i]
+            if g == p + 1:
+                for i in range(SUB):
+                    weighted = columns[i] * inverse[i]
+                    for j in range(SUB):
+                        upcoming[j] = upcoming[j] - weighted * row_of(columns[i], j)
             for i in range(SUB):
                 tile = tile - columns[i] * scaled[i]
             groups[g] = tile
+        across = upcoming
         out = rows[0] * lax.rsqrt(block[0][0])
         for i in range(1, SUB):
             out = jnp.where(sub == i, rows[i] * lax.rsqrt(block[i][i]), out)

time: 165 us -> 160 us (0.970)
  Pallas kernels: 37 us -> 32.8 us
    pallas_call x14, Pallas kernels: 33.7 us -> 29.4 us  [call(): pl.pallas_call(kernel, out_shape=[jax.ShapeDtypeStruct(shape, jnp.float32...]
  transfers between devices with their start and end apart: 26 -> 26, of which waited for: 21 -> 21; matrix products, arithmetic and copies ran while one was open for 0% -> 0% of each run, Pallas kernels for 12% -> 11%
where the time goes in v5:
time: 160 us
  waiting for transfers between devices  88.4 us (55%)
  starting transfers between devices  38.5 us (24%)
  Pallas kernels  32.8 us (20%)
    ppermute x14, waiting for transfers between devices, exchange(): return lax.ppermute(block, axis, [(k, k ^ bit) for k in range(size)])  64.7 us
    pallas_call x14, Pallas kernels, call(): pl.pallas_call(kernel, out_shape=[jax.ShapeDtypeStruct(shape, jnp.float32...  29.4 us
    ppermute x12, waiting for transfers between devices, plane_exchange(): lax.ppermute(block, axes, [(k, k ^ flip) for k in range(sizes[0] * sizes[...  23.7 us
    ppermute x14, starting transfers between devices, exchange(): return lax.ppermute(block, axis, [(k, k ^ bit) for k in range(size)])  23.7 us
    ppermute x12, starting transfers between devices, plane_exchange(): lax.ppermute(block, axes, [(k, k ^ flip) for k in range(sizes[0] * sizes[...  14.8 us
    pallas_call x2, Pallas kernels, pick(): pl.pallas_call(functools.partial(pick_kernel, distances, fibres), out_sha...  3.31 us
  transfers between devices with their start and end apart: 26, of which 21 were waited for; matrix products, arithmetic and copies ran while one was open for 0% of the time, Pallas kernels for 11%

profile of v5, /device:TPU:0, one launch (start us, length us, event | category | flops | bytes accessed | tf_op | source)
XLA Modules:
  0.0 160.2 jit_solution(9891976577648637910)
XLA Ops:
  1.7 4.1 %collective-permute-start.1 = (f32[256,512]{1,0:T(8,128)S(1)}, f32[256,512]{1,0:T(8,128)S(1)}, u32[]{:S(2)}, u32[]{:S(2)}) collective-permute-start(f32[256,512]{1,0:T(8,128)S(1)} %shard_map.29), channel_id=1, source_target_pairs={{0,16},{8,24},{16,0},{24,8},{1,17},{9,25},{17,1},{25,9},{2,18},{10... | collective-permute-start | bytes 1572872 | tf_op jit(solution)/shard_map/ppermute | solution.py:297
  9.1 21.6 %collective-permute-done.1.refs_2_ = f32[256,512]{1,0:T(8,128)S(1)} collective-permute-done((f32[256,512]{1,0:T(8,128)S(1)}, f32[256,512]{1,0:T(8,128)S(1)}, u32[]{:S(2)}, u32[]{:S(2)}) %collective-permute-start.1) | collective-permute-done | bytes 524320 | tf_op jit(solution)/shard_map/ppermute | solution.py:297
  30.7 11.5 %collective-permute-done.refs_1_ = f32[256,512]{1,0:T(8,128)S(1)} collective-permute-done((f32[256,512]{1,0:T(8,128)S(1)}, f32[256,512]{1,0:T(8,128)S(1)}, u32[]{:S(2)}, u32[]{:S(2)}) %collective-permute-start) | collective-permute-done | bytes 524320 | tf_op jit(solution)/shard_map/ppermute | solution.py:297
  47.5 2.6 %collective-permute-start.4 = (f32[64,512]{1,0:T(8,128)S(1)}, f32[64,512]{1,0:T(8,128)S(1)}, u32[]{:S(2)}, u32[]{:S(2)}) collective-permute-start(f32[64,512]{1,0:T(8,128)S(1)} %get-tuple-element.34), channel_id=1, source_target_pairs={{0,6},{1,7},{2,4},{3,5},{4,2},{5,3},{6,0},{7,1},{8,14},{9,15},{10,... | collective-permute-start | bytes 393224 | tf_op jit(solution)/shard_map/ppermute | solution.py:311
  51.0 3.8 %collective-permute-done.4 = f32[64,512]{1,0:T(8,128)S(1)} collective-permute-done((f32[64,512]{1,0:T(8,128)S(1)}, f32[64,512]{1,0:T(8,128)S(1)}, u32[]{:S(2)}, u32[]{:S(2)}) %collective-permute-start.4) | collective-permute-done | bytes 131104 | tf_op jit(solution)/shard_map/ppermute | solution.py:311
  54.8 2.1 %collective-permute-done.6 = f32[64,512]{1,0:T(8,128)S(1)} collective-permute-done((f32[64,512]{1,0:T(8,128)S(1)}, f32[64,512]{1,0:T(8,128)S(1)}, u32[]{:S(2)}, u32[]{:S(2)}) %collective-permute-start.6) | collective-permute-done | bytes 131104 | tf_op jit(solution)/shard_map/ppermute | solution.py:311
  56.9 8.5 %collective-permute-start.7 = (f32[64,512]{1,0:T(8,128)S(1)}, f32[64,512]{1,0:T(8,128)S(1)}, u32[]{:S(2)}, u32[]{:S(2)}) collective-permute-start(f32[64,512]{1,0:T(8,128)S(1)} %fusion.5), channel_id=1, source_target_pairs={{0,8},{8,0},{16,24},{24,16},{1,9},{9,1},{17,25},{25,17},{2,10},{10... | collective-permute-start | bytes 393224 | tf_op jit(solution)/shard_map/ppermute | solution.py:297
  65.4 3.2 %collective-permute-done.7 = f32[64,512]{1,0:T(8,128)S(1)} collective-permute-done((f32[64,512]{1,0:T(8,128)S(1)}, f32[64,512]{1,0:T(8,128)S(1)}, u32[]{:S(2)}, u32[]{:S(2)}) %collective-permute-start.7) | collective-permute-done | bytes 131104 | tf_op jit(solution)/shard_map/ppermute | solution.py:297
  68.7 3.7 %collective-permute-start.8 = (f32[64,512]{1,0:T(8,128)S(1)}, f32[64,512]{1,0:T(8,128)S(1)}, u32[]{:S(2)}, u32[]{:S(2)}) collective-permute-start(f32[64,512]{1,0:T(8,128)S(1)} %add.61), channel_id=1, source_target_pairs={{0,16},{8,24},{16,0},{24,8},{1,17},{9,25},{17,1},{25,9},{2,18},{10... | collective-permute-start | bytes 393224 | tf_op jit(solution)/shard_map/ppermute | solution.py:297
  72.4 5.2 %collective-permute-done.8 = f32[64,512]{1,0:T(8,128)S(1)} collective-permute-done((f32[64,512]{1,0:T(8,128)S(1)}, f32[64,512]{1,0:T(8,128)S(1)}, u32[]{:S(2)}, u32[]{:S(2)}) %collective-permute-start.8) | collective-permute-done | bytes 131104 | tf_op jit(solution)/shard_map/ppermute | solution.py:297
  77.6 3.3 %collective-permute-start.11 = (f32[64,512]{1,0:T(8,128)S(1)}, f32[64,512]{1,0:T(8,128)S(1)}, u32[]{:S(2)}, u32[]{:S(2)}) collective-permute-start(f32[64,512]{1,0:T(8,128)S(1)} %add.62), channel_id=1, source_target_pairs={{0,6},{1,7},{2,4},{3,5},{4,2},{5,3},{6,0},{7,1},{8,14},{9,15},{10,... | collective-permute-start | bytes 393224 | tf_op jit(solution)/shard_map/ppermute | solution.py:311
  81.6 3.2 %collective-permute-done.11 = f32[64,512]{1,0:T(8,128)S(1)} collective-permute-done((f32[64,512]{1,0:T(8,128)S(1)}, f32[64,512]{1,0:T(8,128)S(1)}, u32[]{:S(2)}, u32[]{:S(2)}) %collective-permute-start.11) | collective-permute-done | bytes 131104 | tf_op jit(solution)/shard_map/ppermute | solution.py:311
  84.8 2.4 %collective-permute-done.10 = f32[64,512]{1,0:T(8,128)S(1)} collective-permute-done((f32[64,512]{1,0:T(8,128)S(1)}, f32[64,512]{1,0:T(8,128)S(1)}, u32[]{:S(2)}, u32[]{:S(2)}) %collective-permute-start.10) | collective-permute-done | bytes 131104 | tf_op jit(solution)/shard_map/ppermute | solution.py:311
  89.6 2.1 %shard_map.39 = (f32[256,512]{1,0:T(8,128)S(1)}, f32[256,512]{1,0:T(8,128)S(1)}) custom-call(f32[256,512]{1,0:T(8,128)S(1)} %shard_map.38.early_ref, f32[256,512]{1,0:T(8,128)S(1)} %collective-permute-done.12.got_ref.part_ref, f32[256,512]{1,0:T(8,128)S(1)} %get-tuple-element.18.refs_0_, f32[256,512]{1,0:T(8,128)S(1)} %collective-permute-done.refs_1_, ...), custom_call_target="tpu_custom_call" | custom-call | tf_op jit(solution)/shard_map/pallas_call | solution.py:284
  97.3 3.8 %collective-permute-done.14 = f32[64,512]{1,0:T(8,128)S(1)} collective-permute-done((f32[64,512]{1,0:T(8,128)S(1)}, f32[64,512]{1,0:T(8,128)S(1)}, u32[]{:S(2)}, u32[]{:S(2)}) %collective-permute-start.14) | collective-permute-done | bytes 131104 | tf_op jit(solution)/shard_map/ppermute | solution.py:311
  103.1 5.1 %collective-permute-done.17 = f32[64,512]{1,0:T(8,128)S(1)} collective-permute-done((f32[64,512]{1,0:T(8,128)S(1)}, f32[64,512]{1,0:T(8,128)S(1)}, u32[]{:S(2)}, u32[]{:S(2)}) %collective-permute-start.17) | collective-permute-done | bytes 131104 | tf_op jit(solution)/shard_map/ppermute | solution.py:297
  109.0 7.2 %collective-permute-done.18 = f32[64,512]{1,0:T(8,128)S(1)} collective-permute-done((f32[64,512]{1,0:T(8,128)S(1)}, f32[64,512]{1,0:T(8,128)S(1)}, u32[]{:S(2)}, u32[]{:S(2)}) %collective-permute-start.18) | collective-permute-done | bytes 131104 | tf_op jit(solution)/shard_map/ppermute | solution.py:297
  120.0 2.9 %collective-permute-done.21 = f32[64,512]{1,0:T(8,128)S(1)} collective-permute-done((f32[64,512]{1,0:T(8,128)S(1)}, f32[64,512]{1,0:T(8,128)S(1)}, u32[]{:S(2)}, u32[]{:S(2)}) %collective-permute-start.21) | collective-permute-done | bytes 131104 | tf_op jit(solution)/shard_map/ppermute | solution.py:311
  122.8 2.2 %collective-permute-done.20 = f32[64,512]{1,0:T(8,128)S(1)} collective-permute-done((f32[64,512]{1,0:T(8,128)S(1)}, f32[64,512]{1,0:T(8,128)S(1)}, u32[]{:S(2)}, u32[]{:S(2)}) %collective-permute-start.20) | collective-permute-done | bytes 131104 | tf_op jit(solution)/shard_map/ppermute | solution.py:311
  134.2 2.8 %shard_map.41 = (f32[256,256]{1,0:T(8,128)S(1)}, f32[256,512]{1,0:T(8,128)S(1)}) custom-call(f32[256,512]{1,0:T(8,128)S(1)} %shard_map.37.work_ref, f32[256,512]{1,0:T(8,128)S(1)} %pad_maximum_fusion.1.part_ref, f32[256,512]{1,0:T(8,128)S(1)} %get-tuple-element.18.refs_0_, f32[256,512]{1,0:T(8,128)S(1)} %collective-permute-done.refs_1_, ...), custom_call_target="tpu_custom_call" | custom-call | tf_op jit(solution)/shard_map/pallas_call | solution.py:284
  137.0 9.1 %shard_map.42 = (f32[64,512]{1,0:T(8,128)S(1)}, f32[64,512]{1,0:T(8,128)S(1)}, f32[64,512]{1,0:T(8,128)S(1)}, f32[64,512]{1,0:T(8,128)S(1)}) custom-call(f32[256,512]{1,0:T(8,128)S(1)} %shard_map.37.work_ref, f32[256,512]{1,0:T(8,128)S(1)} %collective-permute-done.22.part_ref, f32[256,256]{1,0:T(8,128)S(1)} %get-tuple-element.25.inner_ref, ...), custom_call_target="tpu_custom_call" | custom-call | tf_op jit(solution)/shard_map/pallas_call | solution.py:284
  146.2 2.5 %collective-permute-start.24 = (f32[64,512]{1,0:T(8,128)S(1)}, f32[64,512]{1,0:T(8,128)S(1)}, u32[]{:S(2)}, u32[]{:S(2)}) collective-permute-start(f32[64,512]{1,0:T(8,128)S(1)} %get-tuple-element.29), channel_id=1, source_target_pairs={{0,16},{8,24},{16,0},{24,8},{1,17},{9,25},{17,1},{25,9},{2,18},{10... | collective-permute-start | bytes 393224 | tf_op jit(solution)/shard_map/ppermute | solution.py:297
  150.5 3.6 %collective-permute-done.23.refs_1_ = f32[64,512]{1,0:T(8,128)S(1)} collective-permute-done((f32[64,512]{1,0:T(8,128)S(1)}, f32[64,512]{1,0:T(8,128)S(1)}, u32[]{:S(2)}, u32[]{:S(2)}) %collective-permute-start.23) | collective-permute-done | bytes 131104 | tf_op jit(solution)/shard_map/ppermute | solution.py:297
  154.1 5.1 %collective-permute-done.24.refs_2_ = f32[64,512]{1,0:T(8,128)S(1)} collective-permute-done((f32[64,512]{1,0:T(8,128)S(1)}, f32[64,512]{1,0:T(8,128)S(1)}, u32[]{:S(2)}, u32[]{:S(2)}) %collective-permute-start.24) | collective-permute-done | bytes 131104 | tf_op jit(solution)/shard_map/ppermute | solution.py:297
  (56 shorter events, 38.4 us)
Async XLA Ops:
  1.7 29.1 %collective-permute-start.1 = (f32[256,512]{1,0:T(8,128)S(1)}, f32[256,512]{1,0:T(8,128)S(1)}, u32[]{:S(2)}, u32[]{:S(2)}) collective-permute-start(f32[256,512]{1,0:T(8,128)S(1)} %shard_map.29), channel_id=1, source_target_pairs={{0,16},{8,24},{16,0},{24,8},{1,17},{9,25},{17,1},{25,9},{2,18},{10... | collective-permute-start | bytes 1572872 | tf_op jit(solution)/shard_map/ppermute | solution.py:297
  7.5 34.8 %collective-permute-start = (f32[256,512]{1,0:T(8,128)S(1)}, f32[256,512]{1,0:T(8,128)S(1)}, u32[]{:S(2)}, u32[]{:S(2)}) collective-permute-start(f32[256,512]{1,0:T(8,128)S(1)} %get-tuple-element.19), channel_id=1, source_target_pairs={{0,8},{8,0},{16,24},{24,16},{1,9},{9,1},{17,25},{25,17},{2,10},{10... | collective-permute-start | bytes 1572872 | tf_op jit(solution)/shard_map/ppermute | solution.py:297
  9.1 34.6 %collective-permute-start.2 = (f32[256,512]{1,0:T(8,128)S(1)}, f32[256,512]{1,0:T(8,128)S(1)}, u32[]{:S(2)}, u32[]{:S(2)}) collective-permute-start(f32[256,512]{1,0:T(8,128)S(1)} %get-tuple-element.20), channel_id=1, source_target_pairs={{0,24},{8,16},{16,8},{24,0},{1,25},{9,17},{17,9},{25,1},{2,26},{10... | collective-permute-start | bytes 1572872 | tf_op jit(solution)/shard_map/ppermute | solution.py:297
  47.5 7.3 %collective-permute-start.4 = (f32[64,512]{1,0:T(8,128)S(1)}, f32[64,512]{1,0:T(8,128)S(1)}, u32[]{:S(2)}, u32[]{:S(2)}) collective-permute-start(f32[64,512]{1,0:T(8,128)S(1)} %get-tuple-element.34), channel_id=1, source_target_pairs={{0,6},{1,7},{2,4},{3,5},{4,2},{5,3},{6,0},{7,1},{8,14},{9,15},{10,... | collective-permute-start | bytes 393224 | tf_op jit(solution)/shard_map/ppermute | solution.py:311
  50.0 6.9 %collective-permute-start.6 = (f32[64,512]{1,0:T(8,128)S(1)}, f32[64,512]{1,0:T(8,128)S(1)}, u32[]{:S(2)}, u32[]{:S(2)}) collective-permute-start(f32[64,512]{1,0:T(8,128)S(1)} %get-tuple-element.35), channel_id=1, source_target_pairs={{0,2},{1,3},{2,0},{3,1},{4,6},{5,7},{6,4},{7,5},{8,10},{9,11},{10,... | collective-permute-start | bytes 393224 | tf_op jit(solution)/shard_map/ppermute | solution.py:311
  50.6 6.3 %collective-permute-start.5 = (f32[64,512]{1,0:T(8,128)S(1)}, f32[64,512]{1,0:T(8,128)S(1)}, u32[]{:S(2)}, u32[]{:S(2)}) collective-permute-start(f32[64,512]{1,0:T(8,128)S(1)} %get-tuple-element.36), channel_id=1, source_target_pairs={{0,4},{1,5},{2,6},{3,7},{4,0},{5,1},{6,2},{7,3},{8,12},{9,13},{10,... | collective-permute-start | bytes 393224 | tf_op jit(solution)/shard_map/ppermute | solution.py:311
  56.9 11.7 %collective-permute-start.7 = (f32[64,512]{1,0:T(8,128)S(1)}, f32[64,512]{1,0:T(8,128)S(1)}, u32[]{:S(2)}, u32[]{:S(2)}) collective-permute-start(f32[64,512]{1,0:T(8,128)S(1)} %fusion.5), channel_id=1, source_target_pairs={{0,8},{8,0},{16,24},{24,16},{1,9},{9,1},{17,25},{25,17},{2,10},{10... | collective-permute-start | bytes 393224 | tf_op jit(solution)/shard_map/ppermute | solution.py:297
  68.7 8.9 %collective-permute-start.8 = (f32[64,512]{1,0:T(8,128)S(1)}, f32[64,512]{1,0:T(8,128)S(1)}, u32[]{:S(2)}, u32[]{:S(2)}) collective-permute-start(f32[64,512]{1,0:T(8,128)S(1)} %add.61), channel_id=1, source_target_pairs={{0,16},{8,24},{16,0},{24,8},{1,17},{9,25},{17,1},{25,9},{2,18},{10... | collective-permute-start | bytes 393224 | tf_op jit(solution)/shard_map/ppermute | solution.py:297
  77.6 7.2 %collective-permute-start.11 = (f32[64,512]{1,0:T(8,128)S(1)}, f32[64,512]{1,0:T(8,128)S(1)}, u32[]{:S(2)}, u32[]{:S(2)}) collective-permute-start(f32[64,512]{1,0:T(8,128)S(1)} %add.62), channel_id=1, source_target_pairs={{0,6},{1,7},{2,4},{3,5},{4,2},{5,3},{6,0},{7,1},{8,14},{9,15},{10,... | collective-permute-start | bytes 393224 | tf_op jit(solution)/shard_map/ppermute | solution.py:311
  81.0 6.3 %collective-permute-start.10 = (f32[64,512]{1,0:T(8,128)S(1)}, f32[64,512]{1,0:T(8,128)S(1)}, u32[]{:S(2)}, u32[]{:S(2)}) collective-permute-start(f32[64,512]{1,0:T(8,128)S(1)} %add.62), channel_id=1, source_target_pairs={{0,4},{1,5},{2,6},{3,7},{4,0},{5,1},{6,2},{7,3},{8,12},{9,13},{10,... | collective-permute-start | bytes 393224 | tf_op jit(solution)/shard_map/ppermute | solution.py:311
  81.0 6.6 %collective-permute-start.9 = (f32[64,512]{1,0:T(8,128)S(1)}, f32[64,512]{1,0:T(8,128)S(1)}, u32[]{:S(2)}, u32[]{:S(2)}) collective-permute-start(f32[64,512]{1,0:T(8,128)S(1)} %add.62), channel_id=1, source_target_pairs={{0,2},{1,3},{2,0},{3,1},{4,6},{5,7},{6,4},{7,5},{8,10},{9,11},{10,... | collective-permute-start | bytes 393224 | tf_op jit(solution)/shard_map/ppermute | solution.py:311
  87.6 2.0 %collective-permute-start.12 = (f32[256,512]{1,0:T(8,128)S(1)}, f32[256,512]{1,0:T(8,128)S(1)}, u32[]{:S(2)}, u32[]{:S(2)}) collective-permute-start(f32[256,512]{1,0:T(8,128)S(1)} %pad_maximum_fusion.kept_ref.part_ref), channel_id=1, source_target_pairs={{0,1},{1,0},{2,3},{3,2},{4,5},{5,4},{6,7},{7,6},{8,9},{9,8},{10,11... | collective-permute-start | bytes 1572872 | tf_op jit(solution)/shard_map/ppermute | solution.py:297
  93.7 7.3 %collective-permute-start.14 = (f32[64,512]{1,0:T(8,128)S(1)}, f32[64,512]{1,0:T(8,128)S(1)}, u32[]{:S(2)}, u32[]{:S(2)}) collective-permute-start(f32[64,512]{1,0:T(8,128)S(1)} %get-tuple-element.31), channel_id=1, source_target_pairs={{0,6},{1,7},{2,4},{3,5},{4,2},{5,3},{6,0},{7,1},{8,14},{9,15},{10,... | collective-permute-start | bytes 393224 | tf_op jit(solution)/shard_map/ppermute | solution.py:311
  95.3 7.7 %collective-permute-start.16 = (f32[64,512]{1,0:T(8,128)S(1)}, f32[64,512]{1,0:T(8,128)S(1)}, u32[]{:S(2)}, u32[]{:S(2)}) collective-permute-start(f32[64,512]{1,0:T(8,128)S(1)} %get-tuple-element.32), channel_id=1, source_target_pairs={{0,2},{1,3},{2,0},{3,1},{4,6},{5,7},{6,4},{7,5},{8,10},{9,11},{10,... | collective-permute-start | bytes 393224 | tf_op jit(solution)/shard_map/ppermute | solution.py:311
  96.7 6.3 %collective-permute-start.15 = (f32[64,512]{1,0:T(8,128)S(1)}, f32[64,512]{1,0:T(8,128)S(1)}, u32[]{:S(2)}, u32[]{:S(2)}) collective-permute-start(f32[64,512]{1,0:T(8,128)S(1)} %get-tuple-element.33), channel_id=1, source_target_pairs={{0,4},{1,5},{2,6},{3,7},{4,0},{5,1},{6,2},{7,3},{8,12},{9,13},{10,... | collective-permute-start | bytes 393224 | tf_op jit(solution)/shard_map/ppermute | solution.py:311
  103.1 5.1 %collective-permute-start.17 = (f32[64,512]{1,0:T(8,128)S(1)}, f32[64,512]{1,0:T(8,128)S(1)}, u32[]{:S(2)}, u32[]{:S(2)}) collective-permute-start(f32[64,512]{1,0:T(8,128)S(1)} %fusion.2), channel_id=1, source_target_pairs={{0,8},{8,0},{16,24},{24,16},{1,9},{9,1},{17,25},{25,17},{2,10},{10... | collective-permute-start | bytes 393224 | tf_op jit(solution)/shard_map/ppermute | solution.py:297
  108.2 8.0 %collective-permute-start.18 = (f32[64,512]{1,0:T(8,128)S(1)}, f32[64,512]{1,0:T(8,128)S(1)}, u32[]{:S(2)}, u32[]{:S(2)}) collective-permute-start(f32[64,512]{1,0:T(8,128)S(1)} %add.70), channel_id=1, source_target_pairs={{0,16},{8,24},{16,0},{24,8},{1,17},{9,25},{17,1},{25,9},{2,18},{10... | collective-permute-start | bytes 393224 | tf_op jit(solution)/shard_map/ppermute | solution.py:297
  116.3 6.6 %collective-permute-start.21 = (f32[64,512]{1,0:T(8,128)S(1)}, f32[64,512]{1,0:T(8,128)S(1)}, u32[]{:S(2)}, u32[]{:S(2)}) collective-permute-start(f32[64,512]{1,0:T(8,128)S(1)} %add.71), channel_id=1, source_target_pairs={{0,6},{1,7},{2,4},{3,5},{4,2},{5,3},{6,0},{7,1},{8,14},{9,15},{10,... | collective-permute-start | bytes 393224 | tf_op jit(solution)/shard_map/ppermute | solution.py:311
  117.9 7.2 %collective-permute-start.20 = (f32[64,512]{1,0:T(8,128)S(1)}, f32[64,512]{1,0:T(8,128)S(1)}, u32[]{:S(2)}, u32[]{:S(2)}) collective-permute-start(f32[64,512]{1,0:T(8,128)S(1)} %add.71), channel_id=1, source_target_pairs={{0,4},{1,5},{2,6},{3,7},{4,0},{5,1},{6,2},{7,3},{8,12},{9,13},{10,... | collective-permute-start | bytes 393224 | tf_op jit(solution)/shard_map/ppermute | solution.py:311
  120.0 6.1 %collective-permute-start.19 = (f32[64,512]{1,0:T(8,128)S(1)}, f32[64,512]{1,0:T(8,128)S(1)}, u32[]{:S(2)}, u32[]{:S(2)}) collective-permute-start(f32[64,512]{1,0:T(8,128)S(1)} %add.71), channel_id=1, source_target_pairs={{0,2},{1,3},{2,0},{3,1},{4,6},{5,7},{6,4},{7,5},{8,10},{9,11},{10,... | collective-permute-start | bytes 393224 | tf_op jit(solution)/shard_map/ppermute | solution.py:311
  126.1 10.9 %collective-permute-start.22 = (f32[256,512]{1,0:T(8,128)S(1)}, f32[256,512]{1,0:T(8,128)S(1)}, u32[]{:S(2)}, u32[]{:S(2)}) collective-permute-start(f32[256,512]{1,0:T(8,128)S(1)} %pad_maximum_fusion.1.part_ref), channel_id=1, source_target_pairs={{0,1},{1,0},{2,3},{3,2},{4,5},{5,4},{6,7},{7,6},{8,9},{9,8},{10,11... | collective-permute-start | bytes 1572872 | tf_op jit(solution)/shard_map/ppermute | solution.py:297
  146.1 8.0 %collective-permute-start.23 = (f32[64,512]{1,0:T(8,128)S(1)}, f32[64,512]{1,0:T(8,128)S(1)}, u32[]{:S(2)}, u32[]{:S(2)}) collective-permute-start(f32[64,512]{1,0:T(8,128)S(1)} %get-tuple-element.28), channel_id=1, source_target_pairs={{0,8},{8,0},{16,24},{24,16},{1,9},{9,1},{17,25},{25,17},{2,10},{10... | collective-permute-start | bytes 393224 | tf_op jit(solution)/shard_map/ppermute | solution.py:297
  146.2 13.0 %collective-permute-start.24 = (f32[64,512]{1,0:T(8,128)S(1)}, f32[64,512]{1,0:T(8,128)S(1)}, u32[]{:S(2)}, u32[]{:S(2)}) collective-permute-start(f32[64,512]{1,0:T(8,128)S(1)} %get-tuple-element.29), channel_id=1, source_target_pairs={{0,16},{8,24},{16,0},{24,8},{1,17},{9,25},{17,1},{25,9},{2,18},{10... | collective-permute-start | bytes 393224 | tf_op jit(solution)/shard_map/ppermute | solution.py:297
  148.6 10.5 %collective-permute-start.25 = (f32[64,512]{1,0:T(8,128)S(1)}, f32[64,512]{1,0:T(8,128)S(1)}, u32[]{:S(2)}, u32[]{:S(2)}) collective-permute-start(f32[64,512]{1,0:T(8,128)S(1)} %get-tuple-element.30), channel_id=1, source_target_pairs={{0,24},{8,16},{16,8},{24,0},{1,25},{9,17},{17,9},{25,1},{2,26},{10... | collective-permute-start | bytes 393224 | tf_op jit(solution)/shard_map/ppermute | solution.py:297
  (3 other events, 46.2 us)

commit v6 on v5

--- a/solution.py
+++ b/solution.py
@@ -9,7 +9,7 @@
 
 
 SUB, LANES = 8, 128
-PARTS = 8
+PARTS = 4
 HALF = LANES // 2
 VMEM_BYTES = 20 * 2**20
 LIFT = 2.0**20
@@ -29,13 +29,13 @@
     sub = lax.broadcasted_iota(jnp.int32, (SUB, LANES), 0)
 
     def columns_of(tile, first):
-        return [jnp.broadcast_to(tile[:, first + j : first + j + 1], (SUB, LANES)) * ones for j in range(SUB)]
+        return [jnp.broadcast_to(tile[:, first + j : first + j + 1], (SUB, LANES)) for j in range(SUB)]
 
     def row_of(tile, j):
         return jnp.broadcast_to(tile[j : j + 1, :], (SUB, LANES))
 
     done = []
-    across = columns_of(groups[0], 0)
+    across = [column * ones for column in columns_of(groups[0], 0)]
     for p in range(len(groups)):
         first = p * SUB
         rows = [row_of(groups[p], j) for j in range(SUB)]
@@ -58,6 +58,8 @@
         for g in range(p + 1, len(groups)):
             tile = groups[g]
             columns = columns_of(tile, first)
+            if g == p + 1:
+                columns[0] = columns[0] * ones
             for i in range(SUB):
                 for j in range(i + 1, SUB):
                     columns[j] = columns[j] - columns[i] * lower[j][i]

time: 160 us -> 160 us (level)
  no operation moved by 1% of the time
where the time goes in v6:
time: 160 us
  waiting for transfers between devices  88.4 us (55%)
  starting transfers between devices  38.4 us (24%)
  Pallas kernels  32.8 us (20%)
    ppermute x14, waiting for transfers between devices, exchange(): return lax.ppermute(block, axis, [(k, k ^ bit) for k in range(size)])  64.7 us
    pallas_call x14, Pallas kernels, call(): pl.pallas_call(kernel, out_shape=[jax.ShapeDtypeStruct(shape, jnp.float32...  29.4 us
    ppermute x12, waiting for transfers between devices, plane_exchange(): lax.ppermute(block, axes, [(k, k ^ flip) for k in range(sizes[0] * sizes[...  23.7 us
    ppermute x14, starting transfers between devices, exchange(): return lax.ppermute(block, axis, [(k, k ^ bit) for k in range(size)])  23.6 us
    ppermute x12, starting transfers between devices, plane_exchange(): lax.ppermute(block, axes, [(k, k ^ flip) for k in range(sizes[0] * sizes[...  14.8 us
    pallas_call x2, Pallas kernels, pick(): pl.pallas_call(functools.partial(pick_kernel, distances, fibres), out_sha...  3.35 us
  transfers between devices with their start and end apart: 26, of which 21 were waited for; matrix products, arithmetic and copies ran while one was open for 0% of the time, Pallas kernels for 11%

profile of v6, /device:TPU:0, one launch (start us, length us, event | category | flops | bytes accessed | tf_op | source)
XLA Modules:
  0.0 160.2 jit_solution(17363313501945101743)
XLA Ops:
  1.7 4.1 %collective-permute-start.1 = (f32[256,512]{1,0:T(8,128)S(1)}, f32[256,512]{1,0:T(8,128)S(1)}, u32[]{:S(2)}, u32[]{:S(2)}) collective-permute-start(f32[256,512]{1,0:T(8,128)S(1)} %shard_map.29), channel_id=1, source_target_pairs={{0,16},{8,24},{16,0},{24,8},{1,17},{9,25},{17,1},{25,9},{2,18},{10... | collective-permute-start | bytes 1572872 | tf_op jit(solution)/shard_map/ppermute | solution.py:299
  9.1 21.6 %collective-permute-done.1.refs_2_ = f32[256,512]{1,0:T(8,128)S(1)} collective-permute-done((f32[256,512]{1,0:T(8,128)S(1)}, f32[256,512]{1,0:T(8,128)S(1)}, u32[]{:S(2)}, u32[]{:S(2)}) %collective-permute-start.1) | collective-permute-done | bytes 524320 | tf_op jit(solution)/shard_map/ppermute | solution.py:299
  30.7 11.5 %collective-permute-done.refs_1_ = f32[256,512]{1,0:T(8,128)S(1)} collective-permute-done((f32[256,512]{1,0:T(8,128)S(1)}, f32[256,512]{1,0:T(8,128)S(1)}, u32[]{:S(2)}, u32[]{:S(2)}) %collective-permute-start) | collective-permute-done | bytes 524320 | tf_op jit(solution)/shard_map/ppermute | solution.py:299
  47.5 2.6 %collective-permute-start.4 = (f32[64,512]{1,0:T(8,128)S(1)}, f32[64,512]{1,0:T(8,128)S(1)}, u32[]{:S(2)}, u32[]{:S(2)}) collective-permute-start(f32[64,512]{1,0:T(8,128)S(1)} %get-tuple-element.34), channel_id=1, source_target_pairs={{0,6},{1,7},{2,4},{3,5},{4,2},{5,3},{6,0},{7,1},{8,14},{9,15},{10,... | collective-permute-start | bytes 393224 | tf_op jit(solution)/shard_map/ppermute | solution.py:313
  51.1 3.8 %collective-permute-done.4 = f32[64,512]{1,0:T(8,128)S(1)} collective-permute-done((f32[64,512]{1,0:T(8,128)S(1)}, f32[64,512]{1,0:T(8,128)S(1)}, u32[]{:S(2)}, u32[]{:S(2)}) %collective-permute-start.4) | collective-permute-done | bytes 131104 | tf_op jit(solution)/shard_map/ppermute | solution.py:313
  54.8 2.1 %collective-permute-done.6 = f32[64,512]{1,0:T(8,128)S(1)} collective-permute-done((f32[64,512]{1,0:T(8,128)S(1)}, f32[64,512]{1,0:T(8,128)S(1)}, u32[]{:S(2)}, u32[]{:S(2)}) %collective-permute-start.6) | collective-permute-done | bytes 131104 | tf_op jit(solution)/shard_map/ppermute | solution.py:313
  57.0 8.5 %collective-permute-start.7 = (f32[64,512]{1,0:T(8,128)S(1)}, f32[64,512]{1,0:T(8,128)S(1)}, u32[]{:S(2)}, u32[]{:S(2)}) collective-permute-start(f32[64,512]{1,0:T(8,128)S(1)} %fusion.5), channel_id=1, source_target_pairs={{0,8},{8,0},{16,24},{24,16},{1,9},{9,1},{17,25},{25,17},{2,10},{10... | collective-permute-start | bytes 393224 | tf_op jit(solution)/shard_map/ppermute | solution.py:299
  65.4 3.2 %collective-permute-done.7 = f32[64,512]{1,0:T(8,128)S(1)} collective-permute-done((f32[64,512]{1,0:T(8,128)S(1)}, f32[64,512]{1,0:T(8,128)S(1)}, u32[]{:S(2)}, u32[]{:S(2)}) %collective-permute-start.7) | collective-permute-done | bytes 131104 | tf_op jit(solution)/shard_map/ppermute | solution.py:299
  68.7 3.7 %collective-permute-start.8 = (f32[64,512]{1,0:T(8,128)S(1)}, f32[64,512]{1,0:T(8,128)S(1)}, u32[]{:S(2)}, u32[]{:S(2)}) collective-permute-start(f32[64,512]{1,0:T(8,128)S(1)} %add.61), channel_id=1, source_target_pairs={{0,16},{8,24},{16,0},{24,8},{1,17},{9,25},{17,1},{25,9},{2,18},{10... | collective-permute-start | bytes 393224 | tf_op jit(solution)/shard_map/ppermute | solution.py:299
  72.4 5.2 %collective-permute-done.8 = f32[64,512]{1,0:T(8,128)S(1)} collective-permute-done((f32[64,512]{1,0:T(8,128)S(1)}, f32[64,512]{1,0:T(8,128)S(1)}, u32[]{:S(2)}, u32[]{:S(2)}) %collective-permute-start.8) | collective-permute-done | bytes 131104 | tf_op jit(solution)/shard_map/ppermute | solution.py:299
  77.6 3.3 %collective-permute-start.11 = (f32[64,512]{1,0:T(8,128)S(1)}, f32[64,512]{1,0:T(8,128)S(1)}, u32[]{:S(2)}, u32[]{:S(2)}) collective-permute-start(f32[64,512]{1,0:T(8,128)S(1)} %add.62), channel_id=1, source_target_pairs={{0,6},{1,7},{2,4},{3,5},{4,2},{5,3},{6,0},{7,1},{8,14},{9,15},{10,... | collective-permute-start | bytes 393224 | tf_op jit(solution)/shard_map/ppermute | solution.py:313
  81.6 3.2 %collective-permute-done.11 = f32[64,512]{1,0:T(8,128)S(1)} collective-permute-done((f32[64,512]{1,0:T(8,128)S(1)}, f32[64,512]{1,0:T(8,128)S(1)}, u32[]{:S(2)}, u32[]{:S(2)}) %collective-permute-start.11) | collective-permute-done | bytes 131104 | tf_op jit(solution)/shard_map/ppermute | solution.py:313
  84.8 2.4 %collective-permute-done.10 = f32[64,512]{1,0:T(8,128)S(1)} collective-permute-done((f32[64,512]{1,0:T(8,128)S(1)}, f32[64,512]{1,0:T(8,128)S(1)}, u32[]{:S(2)}, u32[]{:S(2)}) %collective-permute-start.10) | collective-permute-done | bytes 131104 | tf_op jit(solution)/shard_map/ppermute | solution.py:313
  89.6 2.1 %shard_map.39 = (f32[256,512]{1,0:T(8,128)S(1)}, f32[256,512]{1,0:T(8,128)S(1)}) custom-call(f32[256,512]{1,0:T(8,128)S(1)} %shard_map.38.early_ref, f32[256,512]{1,0:T(8,128)S(1)} %collective-permute-done.12.got_ref.part_ref, f32[256,512]{1,0:T(8,128)S(1)} %get-tuple-element.18.refs_0_, f32[256,512]{1,0:T(8,128)S(1)} %collective-permute-done.refs_1_, ...), custom_call_target="tpu_custom_call" | custom-call | tf_op jit(solution)/shard_map/pallas_call | solution.py:286
  97.3 3.8 %collective-permute-done.14 = f32[64,512]{1,0:T(8,128)S(1)} collective-permute-done((f32[64,512]{1,0:T(8,128)S(1)}, f32[64,512]{1,0:T(8,128)S(1)}, u32[]{:S(2)}, u32[]{:S(2)}) %collective-permute-start.14) | collective-permute-done | bytes 131104 | tf_op jit(solution)/shard_map/ppermute | solution.py:313
  103.1 5.1 %collective-permute-done.17 = f32[64,512]{1,0:T(8,128)S(1)} collective-permute-done((f32[64,512]{1,0:T(8,128)S(1)}, f32[64,512]{1,0:T(8,128)S(1)}, u32[]{:S(2)}, u32[]{:S(2)}) %collective-permute-start.17) | collective-permute-done | bytes 131104 | tf_op jit(solution)/shard_map/ppermute | solution.py:299
  109.0 7.2 %collective-permute-done.18 = f32[64,512]{1,0:T(8,128)S(1)} collective-permute-done((f32[64,512]{1,0:T(8,128)S(1)}, f32[64,512]{1,0:T(8,128)S(1)}, u32[]{:S(2)}, u32[]{:S(2)}) %collective-permute-start.18) | collective-permute-done | bytes 131104 | tf_op jit(solution)/shard_map/ppermute | solution.py:299
  120.0 2.9 %collective-permute-done.21 = f32[64,512]{1,0:T(8,128)S(1)} collective-permute-done((f32[64,512]{1,0:T(8,128)S(1)}, f32[64,512]{1,0:T(8,128)S(1)}, u32[]{:S(2)}, u32[]{:S(2)}) %collective-permute-start.21) | collective-permute-done | bytes 131104 | tf_op jit(solution)/shard_map/ppermute | solution.py:313
  122.8 2.2 %collective-permute-done.20 = f32[64,512]{1,0:T(8,128)S(1)} collective-permute-done((f32[64,512]{1,0:T(8,128)S(1)}, f32[64,512]{1,0:T(8,128)S(1)}, u32[]{:S(2)}, u32[]{:S(2)}) %collective-permute-start.20) | collective-permute-done | bytes 131104 | tf_op jit(solution)/shard_map/ppermute | solution.py:313
  134.2 2.8 %shard_map.41 = (f32[256,256]{1,0:T(8,128)S(1)}, f32[256,512]{1,0:T(8,128)S(1)}) custom-call(f32[256,512]{1,0:T(8,128)S(1)} %shard_map.37.work_ref, f32[256,512]{1,0:T(8,128)S(1)} %pad_maximum_fusion.1.part_ref, f32[256,512]{1,0:T(8,128)S(1)} %get-tuple-element.18.refs_0_, f32[256,512]{1,0:T(8,128)S(1)} %collective-permute-done.refs_1_, ...), custom_call_target="tpu_custom_call" | custom-call | tf_op jit(solution)/shard_map/pallas_call | solution.py:286
  137.0 9.1 %shard_map.42 = (f32[64,512]{1,0:T(8,128)S(1)}, f32[64,512]{1,0:T(8,128)S(1)}, f32[64,512]{1,0:T(8,128)S(1)}, f32[64,512]{1,0:T(8,128)S(1)}) custom-call(f32[256,512]{1,0:T(8,128)S(1)} %shard_map.37.work_ref, f32[256,512]{1,0:T(8,128)S(1)} %collective-permute-done.22.part_ref, f32[256,256]{1,0:T(8,128)S(1)} %get-tuple-element.25.inner_ref, ...), custom_call_target="tpu_custom_call" | custom-call | tf_op jit(solution)/shard_map/pallas_call | solution.py:286
  146.1 2.5 %collective-permute-start.24 = (f32[64,512]{1,0:T(8,128)S(1)}, f32[64,512]{1,0:T(8,128)S(1)}, u32[]{:S(2)}, u32[]{:S(2)}) collective-permute-start(f32[64,512]{1,0:T(8,128)S(1)} %get-tuple-element.29), channel_id=1, source_target_pairs={{0,16},{8,24},{16,0},{24,8},{1,17},{9,25},{17,1},{25,9},{2,18},{10... | collective-permute-start | bytes 393224 | tf_op jit(solution)/shard_map/ppermute | solution.py:299
  150.5 3.6 %collective-permute-done.23.refs_1_ = f32[64,512]{1,0:T(8,128)S(1)} collective-permute-done((f32[64,512]{1,0:T(8,128)S(1)}, f32[64,512]{1,0:T(8,128)S(1)}, u32[]{:S(2)}, u32[]{:S(2)}) %collective-permute-start.23) | collective-permute-done | bytes 131104 | tf_op jit(solution)/shard_map/ppermute | solution.py:299
  154.1 5.1 %collective-permute-done.24.refs_2_ = f32[64,512]{1,0:T(8,128)S(1)} collective-permute-done((f32[64,512]{1,0:T(8,128)S(1)}, f32[64,512]{1,0:T(8,128)S(1)}, u32[]{:S(2)}, u32[]{:S(2)}) %collective-permute-start.24) | collective-permute-done | bytes 131104 | tf_op jit(solution)/shard_map/ppermute | solution.py:299
  (56 shorter events, 38.4 us)
Async XLA Ops:
  1.7 29.1 %collective-permute-start.1 = (f32[256,512]{1,0:T(8,128)S(1)}, f32[256,512]{1,0:T(8,128)S(1)}, u32[]{:S(2)}, u32[]{:S(2)}) collective-permute-start(f32[256,512]{1,0:T(8,128)S(1)} %shard_map.29), channel_id=1, source_target_pairs={{0,16},{8,24},{16,0},{24,8},{1,17},{9,25},{17,1},{25,9},{2,18},{10... | collective-permute-start | bytes 1572872 | tf_op jit(solution)/shard_map/ppermute | solution.py:299
  7.5 34.8 %collective-permute-start = (f32[256,512]{1,0:T(8,128)S(1)}, f32[256,512]{1,0:T(8,128)S(1)}, u32[]{:S(2)}, u32[]{:S(2)}) collective-permute-start(f32[256,512]{1,0:T(8,128)S(1)} %get-tuple-element.19), channel_id=1, source_target_pairs={{0,8},{8,0},{16,24},{24,16},{1,9},{9,1},{17,25},{25,17},{2,10},{10... | collective-permute-start | bytes 1572872 | tf_op jit(solution)/shard_map/ppermute | solution.py:299
  9.1 34.6 %collective-permute-start.2 = (f32[256,512]{1,0:T(8,128)S(1)}, f32[256,512]{1,0:T(8,128)S(1)}, u32[]{:S(2)}, u32[]{:S(2)}) collective-permute-start(f32[256,512]{1,0:T(8,128)S(1)} %get-tuple-element.20), channel_id=1, source_target_pairs={{0,24},{8,16},{16,8},{24,0},{1,25},{9,17},{17,9},{25,1},{2,26},{10... | collective-permute-start | bytes 1572872 | tf_op jit(solution)/shard_map/ppermute | solution.py:299
  45.5 2.0 %collective-permute-start.3 = (f32[256,512]{1,0:T(8,128)S(1)}, f32[256,512]{1,0:T(8,128)S(1)}, u32[]{:S(2)}, u32[]{:S(2)}) collective-permute-start(f32[256,512]{1,0:T(8,128)S(1)} %get-tuple-element.22), channel_id=1, source_target_pairs={{0,1},{1,0},{2,3},{3,2},{4,5},{5,4},{6,7},{7,6},{8,9},{9,8},{10,11... | collective-permute-start | bytes 1572872 | tf_op jit(solution)/shard_map/ppermute | solution.py:299
  47.5 7.3 %collective-permute-start.4 = (f32[64,512]{1,0:T(8,128)S(1)}, f32[64,512]{1,0:T(8,128)S(1)}, u32[]{:S(2)}, u32[]{:S(2)}) collective-permute-start(f32[64,512]{1,0:T(8,128)S(1)} %get-tuple-element.34), channel_id=1, source_target_pairs={{0,6},{1,7},{2,4},{3,5},{4,2},{5,3},{6,0},{7,1},{8,14},{9,15},{10,... | collective-permute-start | bytes 393224 | tf_op jit(solution)/shard_map/ppermute | solution.py:313
  50.1 6.9 %collective-permute-start.6 = (f32[64,512]{1,0:T(8,128)S(1)}, f32[64,512]{1,0:T(8,128)S(1)}, u32[]{:S(2)}, u32[]{:S(2)}) collective-permute-start(f32[64,512]{1,0:T(8,128)S(1)} %get-tuple-element.35), channel_id=1, source_target_pairs={{0,2},{1,3},{2,0},{3,1},{4,6},{5,7},{6,4},{7,5},{8,10},{9,11},{10,... | collective-permute-start | bytes 393224 | tf_op jit(solution)/shard_map/ppermute | solution.py:313
  50.6 6.3 %collective-permute-start.5 = (f32[64,512]{1,0:T(8,128)S(1)}, f32[64,512]{1,0:T(8,128)S(1)}, u32[]{:S(2)}, u32[]{:S(2)}) collective-permute-start(f32[64,512]{1,0:T(8,128)S(1)} %get-tuple-element.36), channel_id=1, source_target_pairs={{0,4},{1,5},{2,6},{3,7},{4,0},{5,1},{6,2},{7,3},{8,12},{9,13},{10,... | collective-permute-start | bytes 393224 | tf_op jit(solution)/shard_map/ppermute | solution.py:313
  57.0 11.7 %collective-permute-start.7 = (f32[64,512]{1,0:T(8,128)S(1)}, f32[64,512]{1,0:T(8,128)S(1)}, u32[]{:S(2)}, u32[]{:S(2)}) collective-permute-start(f32[64,512]{1,0:T(8,128)S(1)} %fusion.5), channel_id=1, source_target_pairs={{0,8},{8,0},{16,24},{24,16},{1,9},{9,1},{17,25},{25,17},{2,10},{10... | collective-permute-start | bytes 393224 | tf_op jit(solution)/shard_map/ppermute | solution.py:299
  68.7 8.9 %collective-permute-start.8 = (f32[64,512]{1,0:T(8,128)S(1)}, f32[64,512]{1,0:T(8,128)S(1)}, u32[]{:S(2)}, u32[]{:S(2)}) collective-permute-start(f32[64,512]{1,0:T(8,128)S(1)} %add.61), channel_id=1, source_target_pairs={{0,16},{8,24},{16,0},{24,8},{1,17},{9,25},{17,1},{25,9},{2,18},{10... | collective-permute-start | bytes 393224 | tf_op jit(solution)/shard_map/ppermute | solution.py:299
  77.6 7.2 %collective-permute-start.11 = (f32[64,512]{1,0:T(8,128)S(1)}, f32[64,512]{1,0:T(8,128)S(1)}, u32[]{:S(2)}, u32[]{:S(2)}) collective-permute-start(f32[64,512]{1,0:T(8,128)S(1)} %add.62), channel_id=1, source_target_pairs={{0,6},{1,7},{2,4},{3,5},{4,2},{5,3},{6,0},{7,1},{8,14},{9,15},{10,... | collective-permute-start | bytes 393224 | tf_op jit(solution)/shard_map/ppermute | solution.py:313
  81.0 6.3 %collective-permute-start.10 = (f32[64,512]{1,0:T(8,128)S(1)}, f32[64,512]{1,0:T(8,128)S(1)}, u32[]{:S(2)}, u32[]{:S(2)}) collective-permute-start(f32[64,512]{1,0:T(8,128)S(1)} %add.62), channel_id=1, source_target_pairs={{0,4},{1,5},{2,6},{3,7},{4,0},{5,1},{6,2},{7,3},{8,12},{9,13},{10,... | collective-permute-start | bytes 393224 | tf_op jit(solution)/shard_map/ppermute | solution.py:313
  81.0 6.6 %collective-permute-start.9 = (f32[64,512]{1,0:T(8,128)S(1)}, f32[64,512]{1,0:T(8,128)S(1)}, u32[]{:S(2)}, u32[]{:S(2)}) collective-permute-start(f32[64,512]{1,0:T(8,128)S(1)} %add.62), channel_id=1, source_target_pairs={{0,2},{1,3},{2,0},{3,1},{4,6},{5,7},{6,4},{7,5},{8,10},{9,11},{10,... | collective-permute-start | bytes 393224 | tf_op jit(solution)/shard_map/ppermute | solution.py:313
  93.7 7.3 %collective-permute-start.14 = (f32[64,512]{1,0:T(8,128)S(1)}, f32[64,512]{1,0:T(8,128)S(1)}, u32[]{:S(2)}, u32[]{:S(2)}) collective-permute-start(f32[64,512]{1,0:T(8,128)S(1)} %get-tuple-element.31), channel_id=1, source_target_pairs={{0,6},{1,7},{2,4},{3,5},{4,2},{5,3},{6,0},{7,1},{8,14},{9,15},{10,... | collective-permute-start | bytes 393224 | tf_op jit(solution)/shard_map/ppermute | solution.py:313
  95.3 7.7 %collective-permute-start.16 = (f32[64,512]{1,0:T(8,128)S(1)}, f32[64,512]{1,0:T(8,128)S(1)}, u32[]{:S(2)}, u32[]{:S(2)}) collective-permute-start(f32[64,512]{1,0:T(8,128)S(1)} %get-tuple-element.32), channel_id=1, source_target_pairs={{0,2},{1,3},{2,0},{3,1},{4,6},{5,7},{6,4},{7,5},{8,10},{9,11},{10,... | collective-permute-start | bytes 393224 | tf_op jit(solution)/shard_map/ppermute | solution.py:313
  96.7 6.3 %collective-permute-start.15 = (f32[64,512]{1,0:T(8,128)S(1)}, f32[64,512]{1,0:T(8,128)S(1)}, u32[]{:S(2)}, u32[]{:S(2)}) collective-permute-start(f32[64,512]{1,0:T(8,128)S(1)} %get-tuple-element.33), channel_id=1, source_target_pairs={{0,4},{1,5},{2,6},{3,7},{4,0},{5,1},{6,2},{7,3},{8,12},{9,13},{10,... | collective-permute-start | bytes 393224 | tf_op jit(solution)/shard_map/ppermute | solution.py:313
  103.1 5.1 %collective-permute-start.17 = (f32[64,512]{1,0:T(8,128)S(1)}, f32[64,512]{1,0:T(8,128)S(1)}, u32[]{:S(2)}, u32[]{:S(2)}) collective-permute-start(f32[64,512]{1,0:T(8,128)S(1)} %fusion.2), channel_id=1, source_target_pairs={{0,8},{8,0},{16,24},{24,16},{1,9},{9,1},{17,25},{25,17},{2,10},{10... | collective-permute-start | bytes 393224 | tf_op jit(solution)/shard_map/ppermute | solution.py:299
  108.2 8.0 %collective-permute-start.18 = (f32[64,512]{1,0:T(8,128)S(1)}, f32[64,512]{1,0:T(8,128)S(1)}, u32[]{:S(2)}, u32[]{:S(2)}) collective-permute-start(f32[64,512]{1,0:T(8,128)S(1)} %add.70), channel_id=1, source_target_pairs={{0,16},{8,24},{16,0},{24,8},{1,17},{9,25},{17,1},{25,9},{2,18},{10... | collective-permute-start | bytes 393224 | tf_op jit(solution)/shard_map/ppermute | solution.py:299
  116.3 6.6 %collective-permute-start.21 = (f32[64,512]{1,0:T(8,128)S(1)}, f32[64,512]{1,0:T(8,128)S(1)}, u32[]{:S(2)}, u32[]{:S(2)}) collective-permute-start(f32[64,512]{1,0:T(8,128)S(1)} %add.71), channel_id=1, source_target_pairs={{0,6},{1,7},{2,4},{3,5},{4,2},{5,3},{6,0},{7,1},{8,14},{9,15},{10,... | collective-permute-start | bytes 393224 | tf_op jit(solution)/shard_map/ppermute | solution.py:313
  117.9 7.2 %collective-permute-start.20 = (f32[64,512]{1,0:T(8,128)S(1)}, f32[64,512]{1,0:T(8,128)S(1)}, u32[]{:S(2)}, u32[]{:S(2)}) collective-permute-start(f32[64,512]{1,0:T(8,128)S(1)} %add.71), channel_id=1, source_target_pairs={{0,4},{1,5},{2,6},{3,7},{4,0},{5,1},{6,2},{7,3},{8,12},{9,13},{10,... | collective-permute-start | bytes 393224 | tf_op jit(solution)/shard_map/ppermute | solution.py:313
  120.0 6.1 %collective-permute-start.19 = (f32[64,512]{1,0:T(8,128)S(1)}, f32[64,512]{1,0:T(8,128)S(1)}, u32[]{:S(2)}, u32[]{:S(2)}) collective-permute-start(f32[64,512]{1,0:T(8,128)S(1)} %add.71), channel_id=1, source_target_pairs={{0,2},{1,3},{2,0},{3,1},{4,6},{5,7},{6,4},{7,5},{8,10},{9,11},{10,... | collective-permute-start | bytes 393224 | tf_op jit(solution)/shard_map/ppermute | solution.py:313
  126.1 10.9 %collective-permute-start.22 = (f32[256,512]{1,0:T(8,128)S(1)}, f32[256,512]{1,0:T(8,128)S(1)}, u32[]{:S(2)}, u32[]{:S(2)}) collective-permute-start(f32[256,512]{1,0:T(8,128)S(1)} %pad_maximum_fusion.1.part_ref), channel_id=1, source_target_pairs={{0,1},{1,0},{2,3},{3,2},{4,5},{5,4},{6,7},{7,6},{8,9},{9,8},{10,11... | collective-permute-start | bytes 1572872 | tf_op jit(solution)/shard_map/ppermute | solution.py:299
  146.1 8.0 %collective-permute-start.23 = (f32[64,512]{1,0:T(8,128)S(1)}, f32[64,512]{1,0:T(8,128)S(1)}, u32[]{:S(2)}, u32[]{:S(2)}) collective-permute-start(f32[64,512]{1,0:T(8,128)S(1)} %get-tuple-element.28), channel_id=1, source_target_pairs={{0,8},{8,0},{16,24},{24,16},{1,9},{9,1},{17,25},{25,17},{2,10},{10... | collective-permute-start | bytes 393224 | tf_op jit(solution)/shard_map/ppermute | solution.py:299
  146.1 13.0 %collective-permute-start.24 = (f32[64,512]{1,0:T(8,128)S(1)}, f32[64,512]{1,0:T(8,128)S(1)}, u32[]{:S(2)}, u32[]{:S(2)}) collective-permute-start(f32[64,512]{1,0:T(8,128)S(1)} %get-tuple-element.29), channel_id=1, source_target_pairs={{0,16},{8,24},{16,0},{24,8},{1,17},{9,25},{17,1},{25,9},{2,18},{10... | collective-permute-start | bytes 393224 | tf_op jit(solution)/shard_map/ppermute | solution.py:299
  148.6 10.5 %collective-permute-start.25 = (f32[64,512]{1,0:T(8,128)S(1)}, f32[64,512]{1,0:T(8,128)S(1)}, u32[]{:S(2)}, u32[]{:S(2)}) collective-permute-start(f32[64,512]{1,0:T(8,128)S(1)} %get-tuple-element.30), channel_id=1, source_target_pairs={{0,24},{8,16},{16,8},{24,0},{1,25},{9,17},{17,9},{25,1},{2,26},{10... | collective-permute-start | bytes 393224 | tf_op jit(solution)/shard_map/ppermute | solution.py:299
  (3 other events, 46.2 us)
